TPU v7x, 128 devices: a whole 4x4x4 slice. The times are simulated.
128 devices in a mesh: leaf: 8 (over y, core), front: 16 (over z, x).
Axes of the slice: x: 4, y: 4, z: 4, core: 2. Of those that a mesh axis runs over, the one named last changes fastest.
Arguments:
- front_entries: float32 [16, 8, 128, 8, 16, 128], P(None, 'leaf', None, None, 'front'), as said below
- child_panels: bfloat16 [8, 2048, 512], P('leaf', 'front'), may hold values from -0.053955078 to 0.053955078
- child_blocks: bfloat16 [8, 2048, 2048], P('leaf', None, 'front'), as said below
- child_map: int32 [8, 16], replicated, may hold values from 0 to 127, as said below
Outputs:
- factored: float32 [16, 8, 128, 8, 16, 128], P(None, 'leaf', None, None, 'front')
Inputs may be any that keep to these rules, and one draw needn't show every extreme that they name: The blocks of one subtree go to distinct parent blocks, and child_map[c, j] modulo 16 equals j. front_entries is symmetric and positive definite, with its diagonal in 6 to 9. `child_blocks`: each subtree's block is symmetric with diagonal in 6 to 9 and small independent entries elsewhere.
All inputs are finite; a program needn't handle non-finite values.
Results may differ from a plain program's by a relative error of at most 0.0012.
Values may be sent and summed in bfloat16 or wider, within the bound.
No kernel may reach another device: no remote copies, remote signals or barrier semaphores. Data moves between devices by JAX's collectives and lax.ppermute only.
A program may use at most 128 MiB of HBM per device.

v0:
```python
import jax
import jax.numpy as jnp
from jax import lax
from jax.experimental import pallas as pl
from jax.experimental.pallas import tpu as pltpu
from jax.sharding import PartitionSpec as P


F32 = jnp.float32
BF16 = jnp.bfloat16
KS = 8
BLK = 128
ORDER = KS * BLK
N_LEAF = 8
N_FRONT = 16
STEP_ROWS = 4
MESH_AXES = ("leaf", "front")
WHOLE = pl.BlockSpec(memory_space=pltpu.VMEM)
TABLE = pl.BlockSpec(memory_space=pltpu.SMEM)


def dot(a, b, ca, cb, precision=None):
    return lax.dot_general(
        a, b, (((ca,), (cb,)), ((), ())), precision=precision, preferred_element_type=F32
    )


def place():
    return lax.axis_index("leaf"), lax.axis_index("front")


def rows_of(rows_ref, c):
    return jnp.concatenate([rows_ref[0, c], rows_ref[1, c]], axis=0)


def update_of(given, left, right):
    return (given.astype(F32) - dot(left, right, 1, 1)).astype(BF16)


def pivot_kernel(
    map_ref, front_ref, given_ref, rows_ref, cols_ref, flat_ref, turned_ref, first_ref, sum_ref
):
    leaf, front = place()
    for s in range(8):
        sum_ref[:, s * BLK : (s + 1) * BLK] = front_ref[pl.ds(s, BLK, stride=8), :]
    for c in range(N_LEAF):
        cycle = map_ref[c, front] // N_FRONT

        @pl.when(map_ref[c, leaf] // N_FRONT == 0)
        def _():
            cols = pl.ds(pl.multiple_of(cycle * BLK, BLK), BLK)
            update = update_of(given_ref[c, 0], rows_of(rows_ref, c), cols_ref[c])
            sum_ref[:, cols] += update.astype(F32)

    flat_ref[...] = sum_ref[...].astype(BF16)
    for s in range(8):
        turned_ref[s] = jnp.transpose(sum_ref[:, s * BLK : (s + 1) * BLK]).astype(BF16)
    half = BLK // 2
    bottom = sum_ref[half:, :BLK]
    top = jnp.where(leaf > front, jnp.transpose(sum_ref[:, :BLK])[:half], sum_ref[:half, :BLK])
    first_ref[0] = jnp.where(leaf < front, bottom, top).astype(BF16)
    first_ref[1] = bottom.astype(BF16)


def pivot_rows(child_map, front, given, rows, cols):
    return pl.pallas_call(
        pivot_kernel,
        name="pivot_rows",
        grid=(1,),
        out_shape=(
            jax.ShapeDtypeStruct((BLK, 8 * BLK), BF16),
            jax.ShapeDtypeStruct((8, BLK, BLK), BF16),
            jax.ShapeDtypeStruct((2, BLK // 2, BLK), BF16),
        ),
        in_specs=[
            TABLE,
            pl.BlockSpec((8 * BLK, BLK), lambda i: (0, 0)),
            pl.BlockSpec((N_LEAF, 1, BLK, BLK), lambda i: (0, 0, 0, 0)),
            pl.BlockSpec(rows.shape, lambda i: (0, 0, 0, 0)),
            pl.BlockSpec(cols.shape, lambda i: (0, 0, 0)),
        ],
        out_specs=(
            pl.BlockSpec((BLK, 8 * BLK), lambda i: (0, 0)),
            pl.BlockSpec((8, BLK, BLK), lambda i: (0, 0, 0)),
            pl.BlockSpec((2, BLK // 2, BLK), lambda i: (0, 0, 0)),
        ),
        scratch_shapes=[pltpu.VMEM((BLK, 8 * BLK), F32)],
    )(child_map, front, given, rows, cols)


def lanes(x, j):
    return jnp.broadcast_to(x[:, j : j + 1], (8, BLK))


def subs(x, i):
    return jnp.broadcast_to(x[i : i + 1, :], (8, BLK))


def sum_products(v, r):
    t = [v[i] * r[i] for i in range(8)]
    while len(t) > 1:
        t = [t[i] + t[i + 1] for i in range(0, len(t), 2)]
    return t[0]


def factor(g_ref, e_ref):
    for p in range(16):
        rows = pl.ds(8 * p, 8)
        below = pl.ds(8 * p + 8, 8)
        top = g_ref[rows, :]
        side = e_ref[rows, :]
        cols = [lanes(top, 8 * p + j) for j in range(8)]
        a = [[subs(cols[j], i) if j <= i else None for j in range(8)] for i in range(8)]
        r = [subs(top, i) for i in range(8)]
        e = [subs(side, i) for i in range(8)]
        more = p < 15
        if more:
            after = g_ref[below, :]
            v = [lanes(after, 8 * p + j) for j in range(8)]
        for j in range(8):
            inv = lax.rsqrt(a[j][j])
            r[j] = r[j] * inv
            e[j] = e[j] * inv
            if more:
                v[j] = v[j] * inv
            col = [None] * 8
            for i in range(j + 1, 8):
                col[i] = a[i][j] * inv
            for i in range(j + 1, 8):
                for k in range(j + 1, i + 1):
                    a[i][k] = a[i][k] - col[i] * col[k]
            for i in range(j + 1, 8):
                r[i] = r[i] - col[i] * r[j]
                e[i] = e[i] - col[i] * e[j]
                if more:
                    v[i] = v[i] - col[i] * v[j]
        if more:
            g_ref[below, :] = after - sum_products(v, r)
            e_ref[below, :] = e_ref[below, :] - sum_products(v, e)
        sub = lax.broadcasted_iota(jnp.int32, (8, BLK), 0)
        u, w = r[0], e[0]
        for i in range(1, 8):
            u = jnp.where(sub == i, r[i], u)
            w = jnp.where(sub == i, e[i], w)
        g_ref[rows, :] = u
        e_ref[rows, :] = w
        if p < 14:
            turned = jnp.transpose(u)
            for g in range(p + 2, 16):
                vg = [lanes(turned[8 * g : 8 * g + 8, :], i) for i in range(8)]
                there = pl.ds(8 * g, 8)
                g_ref[there, :] = g_ref[there, :] - sum_products(vg, r)
                e_ref[there, :] = e_ref[there, :] - sum_products(vg, e)


def halves(x):
    high = x.astype(BF16)
    return high, (x - high.astype(F32)).astype(BF16)


def dot3(a, b, ca, cb):
    return dot(a[0], b[0], ca, cb) + (dot(a[0], b[1], ca, cb) + dot(a[1], b[0], ca, cb))


def cholesky_kernel(
    a_ref, m_hbm, l_ref, s_ref, d_ref, g_ref, e_ref, nh_ref, nl_ref, m_ref, sem
):
    half = BLK // 2
    for r in range(KS):
        for c in range(r, KS):
            cols = slice(c * BLK, (c + 1) * BLK)
            lower = a_ref[r, KS] if c == r else a_ref[r, c]
            s_ref[r * BLK : r * BLK + half, cols] = a_ref[c, r].astype(F32)
            s_ref[r * BLK + half : (r + 1) * BLK, cols] = lower.astype(F32)
    row_id = lax.broadcasted_iota(jnp.int32, (BLK, BLK), 0)
    col_id = lax.broadcasted_iota(jnp.int32, (BLK, BLK), 1)
    ident = (row_id == col_id).astype(F32)

    @pl.loop(0, KS)
    def _(k):
        here = pl.ds(pl.multiple_of(k * BLK, BLK), BLK)
        g_ref[...] = s_ref[here, here]
        e_ref[...] = ident
        factor(g_ref, e_ref)
        d_ref[here, :] = g_ref[...]
        s_ref[here, here] = ident
        row = dot3(halves(e_ref[...]), halves(s_ref[here, :]), 1, 0)
        s_ref[here, :] = row
        nh_ref[...], nl_ref[...] = halves(row)
        keep = lax.broadcasted_iota(jnp.int32, (BLK, ORDER), 1) < (k + 1) * BLK
        m_ref[here, :] = jnp.where(keep, row, 0.0).astype(BF16)

        @pl.loop(k + 1, KS)
        def _(i):
            there = pl.ds(pl.multiple_of(i * BLK, BLK), BLK)
            s_ref[there, here] = jnp.zeros((BLK, BLK), F32)
            part = nh_ref[:, there], nl_ref[:, there]
            s_ref[there, :] = s_ref[there, :] - dot3(part, (nh_ref[...], nl_ref[...]), 0, 0)

    out = pltpu.make_async_copy(m_ref, m_hbm, sem)
    out.start()
    leaf, front = place()
    front = jnp.minimum(front, KS - 1)
    mine = pl.ds(pl.multiple_of(leaf * BLK, BLK), BLK)
    other = pl.ds(pl.multiple_of(front * BLK, BLK), BLK)
    upper = jnp.where(row_id <= col_id, d_ref[mine, :], 0.0)
    beyond = jnp.where(front < leaf, s_ref[other, mine], 0.0)
    l_ref[...] = jnp.transpose(jnp.where(front == leaf, upper, beyond))
    out.wait()


def cholesky(a):
    return pl.pallas_call(
        cholesky_kernel,
        name="cholesky",
        out_shape=(
            jax.ShapeDtypeStruct((ORDER, ORDER), BF16),
            jax.ShapeDtypeStruct((BLK, BLK), F32),
        ),
        in_specs=[WHOLE],
        out_specs=(pl.BlockSpec(memory_space=pltpu.HBM), WHOLE),
        scratch_shapes=[
            pltpu.VMEM((ORDER, ORDER), F32),
            pltpu.VMEM((ORDER, BLK), F32),
            pltpu.VMEM((BLK, BLK), F32),
            pltpu.VMEM((BLK, BLK), F32),
            pltpu.VMEM((BLK, ORDER), BF16),
            pltpu.VMEM((BLK, ORDER), BF16),
            pltpu.VMEM((ORDER, ORDER), BF16),
            pltpu.SemaphoreType.DMA,
        ],
        compiler_params=pltpu.CompilerParams(vmem_limit_bytes=24 << 20),
        cost_estimate=pl.CostEstimate(
            flops=60_000_000_000, bytes_accessed=6 << 20, transcendentals=1024
        ),
    )(a)


def schur_kernel(
    map_ref, l_ref, given_ref, upper_ref, panel_ref, m_hbm, cols_hbm, rows_hbm, front_ref,
    out_ref, m_ref, cols_ref, rows_ref, lower_ref, w_ref, low_ref, update_ref, sem
):
    step = pl.program_id(0)
    leaf, front = place()
    owner = jnp.minimum(front, KS - 1)
    rows_here = STEP_ROWS * BLK

    def copies():
        yield pltpu.make_async_copy(m_hbm, m_ref, sem.at[2, 0])
        yield pltpu.make_async_copy(cols_hbm, cols_ref, sem.at[2, 1])
        for b in range(2):
            for a in range(KS):
                columns = pl.ds(a * BLK, BLK)
                source = rows_hbm.at[b, a]
                yield pltpu.make_async_copy(
                    source.at[pl.ds(0, ORDER)], rows_ref.at[b, :, columns], sem.at[b, a]
                )
                yield pltpu.make_async_copy(
                    source.at[pl.ds(ORDER, 2 * BLK)], lower_ref.at[b, a], sem.at[3 + b, a]
                )

    @pl.when(step == 0)
    def _():
        for copy in copies():
            copy.start()
        for c in range(N_LEAF):
            update_ref[c, 0] = update_of(given_ref[c, 0], rows_of(upper_ref, c), panel_ref[c])
        waits = list(copies())
        waits[0].wait()
        waits[1].wait()
        for n in range(4):
            take = slice(n * 256, (n + 1) * 256)
            upto = slice(0, (n + 1) * 256)
            w_ref[take, :] = dot(m_ref[take, upto], cols_ref[upto, :], 1, 0).astype(BF16)
        for copy in waits[2:]:
            copy.wait()
        for c in range(N_LEAF):
            product = jnp.zeros((BLK, BLK), F32)
            for n in range(4):
                part = slice(n * BLK // 2, (n + 1) * BLK // 2)
                rows = jnp.concatenate([lower_ref[0, c, part], lower_ref[1, c, part]], axis=0)
                product += dot(rows, panel_ref[c, :, n * BLK : (n + 1) * BLK], 1, 1)
            update_ref[c, 1] = (given_ref[c, 1].astype(F32) - product).astype(BF16)

    for q in range(STEP_ROWS):
        source = pl.ds(pl.multiple_of((step * (STEP_ROWS // 2) + q // 2) * BLK, BLK), BLK)
        mine = slice(q * BLK, (q + 1) * BLK)
        for n in range(4):
            take = slice(n * 256, (n + 1) * 256)
            upto = slice(0, (n + 1) * 256)
            low_ref[mine, take] = dot(rows_ref[q % 2, source, upto], m_ref[take, upto], 1, 1)
    low = low_ref[...].astype(BF16)
    for n in range(4):
        part = dot(low, w_ref[:, n * 256 : (n + 1) * 256], 1, 0)
        for s in range(2):
            there = pl.ds(2 * n + s, rows_here, stride=8)
            out_ref[there, :] = front_ref[there, :] - part[:, s * BLK : (s + 1) * BLK]
    for c in range(N_LEAF):
        s = map_ref[c, front] // N_FRONT
        for b in range(2):
            q = map_ref[c, leaf + b * N_LEAF] // N_FRONT * 2 + b - step * STEP_ROWS

            @pl.when((q >= 0) & (q < STEP_ROWS))
            def _():
                there = pl.ds(q * (8 * BLK) + s, BLK, stride=8)
                out_ref[there, :] = out_ref[there, :] + update_ref[c, b].astype(F32)

    @pl.when(front < KS)
    def _():
        column = pl.ds(pl.multiple_of(owner * BLK, BLK), BLK)
        out_ref[pl.ds(0, rows_here, stride=8), :] = low_ref[:, column]

    @pl.when(step == 0)
    def _():
        out_ref[: 8 * BLK, :] = jnp.zeros((8 * BLK, BLK), F32)

        @pl.when(front < KS)
        def _():
            out_ref[pl.ds(0, BLK, stride=8), :] = l_ref[...]


def schur(child_map, low, given, upper, panels, m, cols, rows, front):
    steps = 16 // STEP_ROWS
    block = pl.BlockSpec((STEP_ROWS * BLK * 8, BLK), lambda i: (i, 0))
    return pl.pallas_call(
        schur_kernel,
        name="schur",
        grid=(steps,),
        out_shape=jax.ShapeDtypeStruct((16 * BLK * 8, BLK), F32),
        in_specs=[TABLE] + [WHOLE] * 4 + [pl.BlockSpec(memory_space=pltpu.HBM)] * 3 + [block],
        out_specs=block,
        scratch_shapes=[
            pltpu.VMEM((ORDER, ORDER), BF16),
            pltpu.VMEM((ORDER, ORDER), BF16),
            pltpu.VMEM((2, ORDER, ORDER), BF16),
            pltpu.VMEM((2, KS, 2 * BLK, BLK), BF16),
            pltpu.VMEM((ORDER, ORDER), BF16),
            pltpu.VMEM((STEP_ROWS * BLK, ORDER), F32),
            pltpu.VMEM((N_LEAF, 2, BLK, BLK), BF16),
            pltpu.SemaphoreType.DMA((5, KS)),
        ],
        compiler_params=pltpu.CompilerParams(vmem_limit_bytes=48 << 20),
    )(child_map, low, given, upper, panels, m, cols, rows, front)


def gather(x, axis, count):
    spread = jnp.broadcast_to(x[None], (count, *x.shape))
    return lax.all_to_all(spread, axis, 0, 0)


def exchange(flip):
    return [
        (a * N_FRONT + b * N_LEAF + c, c * N_FRONT + (b ^ flip) * N_LEAF + a)
        for a in range(N_LEAF)
        for b in range(2)
        for c in range(N_LEAF)
    ]


def one_pass(front_entries, child_panels, child_blocks, child_map):
    front = front_entries.reshape(16 * BLK * 8, BLK)
    front_id = lax.axis_index("front")
    leaf_id = lax.axis_index("leaf")
    own = child_panels[0]
    panels = lax.all_gather(own, "leaf", axis=0)
    halves_of = own.reshape(2, BLK // 2, own.shape[1])
    early = front_id < N_LEAF
    same = lax.ppermute(jnp.where(early, halves_of[0], halves_of[1]), MESH_AXES, exchange(0))
    other = lax.ppermute(jnp.where(early, halves_of[1], halves_of[0]), MESH_AXES, exchange(1))
    upper = gather(jnp.where(early, same, other), "front", N_FRONT)
    upper = upper.reshape(2, N_LEAF, BLK // 2, own.shape[1])
    lower = jnp.where(early, other, same).reshape(BLK // 2, 4, BLK).transpose(1, 0, 2)
    blocks = child_blocks[0].reshape(2, N_LEAF, BLK, BLK).transpose(1, 0, 2, 3)
    blocks, upper = lax.optimization_barrier((blocks, upper))
    given = lax.all_to_all(blocks, "leaf", 0, 0)
    flat, turned, first = pivot_rows(child_map, front, given, upper, panels)
    turned = lax.ppermute(turned, MESH_AXES, exchange(0))
    packed = jnp.concatenate([turned.reshape(ORDER, BLK), lower.reshape(2 * BLK, BLK)], axis=0)
    pieces = gather(first, "front", N_FRONT)[:KS]
    packed, pieces = lax.optimization_barrier((packed, pieces))
    rows = lax.all_gather(packed, "front", axis=0)
    extra = lax.dynamic_index_in_dim(pieces[:, 1], leaf_id, 0, keepdims=True)
    whole = jnp.concatenate([pieces[:, 0], extra], axis=0)
    separator = gather(whole, "leaf", N_LEAF)
    flat, separator = lax.optimization_barrier((flat, separator))
    cols = lax.all_gather(flat, "leaf", axis=0, tiled=True)
    m, low = cholesky(separator)
    rows = rows.reshape(2, KS, ORDER + 2 * BLK, BLK)
    out = schur(child_map, low, given, upper, panels, m, cols, rows, front)
    return out.reshape(16, 1, BLK, 8, 1, BLK)


def solution(mesh):
    placed = (
        P(None, "leaf", None, None, "front", None),
        P("leaf", "front", None),
        P("leaf", None, "front"),
        P(),
    )
    return jax.shard_map(
        one_pass,
        mesh=mesh,
        in_specs=placed,
        out_specs=P(None, "leaf", None, None, "front", None),
        check_vma=False,
    )
```

profile of v0, /device:TPU:0, one launch (start us, length us, event | category | flops | bytes accessed | tf_op | source)
XLA Modules:
  0.0 217.0 jit_solution(9756442323738548794)
XLA Ops:
  6.5 0.0 copy-start.8
  6.5 0.0 all-gather.5.cloned.1.call-start
  6.5 0.7 all-gather.5.cloned.1.call-update
  7.3 0.9 select_bitcast_fusion
  8.2 4.1 %collective-permute-start.1 = (bf16[64,512]{1,0:T(8,128)(2,1)S(1)}, bf16[64,512]{1,0:T(8,128)(2,1)S(1)}, u32[]{:S(2)}, u32[]{:S(2)}) collective-permute-start(bf16[64,512]{1,0:T(8,128)(2,1)S(1)} %get-tuple-element.31), channel_id=1, source_target_pairs={{0,8},{1,24},{2,40},{3,56},{4,72},{5,88},{6,104},{7,120},{8,0},{9,... | collective-permute-start | bytes 196616 | tf_op jit(solution)/shard_map/ppermute | solution.py:369
  12.2 0.7 collective-permute-start
  12.9 1.9 collective-permute-done.1
  14.7 0.0 collective-permute-done
  14.8 1.1 broadcast_in_dim.6
  15.8 14.3 %all-to-all-start = ((bf16[16,64,512]{2,1,0:T(8,128)(2,1)}), bf16[16,64,512]{2,1,0:T(8,128)(2,1)S(1)}, u32[]{:S(2)}, u32[]{:S(2)}) async-start(bf16[16,64,512]{2,1,0:T(8,128)(2,1)} %broadcast_in_dim.6), calls=%async_computation | async-start | bytes 2097152 | tf_op jit(solution)/shard_map/all_to_all | solution.py:348
  30.2 0.0 copy-done.8
  30.2 16.6 %all-to-all-done = bf16[16,64,512]{2,1,0:T(8,128)(2,1)S(1)} async-done(((bf16[16,64,512]{2,1,0:T(8,128)(2,1)}), bf16[16,64,512]{2,1,0:T(8,128)(2,1)S(1)}, u32[]{:S(2)}, u32[]{:S(2)}) %all-to-all-start) | async-done | bytes 1048608 | tf_op jit(solution)/shard_map/all_to_all | solution.py:348
  46.8 0.0 copy-start
  46.8 14.7 %all_to_all.20.given_ref = bf16[8,2,128,128]{3,2,1,0:T(8,128)(2,1)} all-to-all(bf16[8,2,128,128]{3,2,1,0:T(8,128)(2,1)S(1)} %bitcast.26), channel_id=1, replica_groups=mesh['leaf'=8,'front'=16] {'leaf'}, dimensions={0} | all-to-all | bytes 1048576 | tf_op jit(solution)/shard_map/all_to_all | solution.py:375
  61.5 0.0 all-gather.5.cloned.1.call-done.cols_ref.panel_ref
  61.5 0.0 copy-done
  61.5 3.1 %pivot_rows.1 = (bf16[128,1024]{1,0:T(8,128)(2,1)}, bf16[8,128,128]{2,1,0:T(8,128)(2,1)}, bf16[2,64,128]{2,1,0:T(8,128)(2,1)}) custom-call(s32[8,16]{1,0:T(8,128)} %map_ref.3, f32[16384,128]{1,0:T(8,128)} %bitcast.23, bf16[8,2,128,128]{3,2,1,0:T(8,128)(2,1)} %all_to_all.20.given_ref, bf16[2,8,64,512]{3,2,1,0:T(8,128)(2,1)} %bitcast.21, ...), custom_call_target="tpu_custom_call" | custom-call | tf_op jit(solution)/shard_map/pivot_rows/pallas_call | solution.py:66
  64.6 1.6 collective-permute-start.2
  66.2 1.7 broadcast_in_dim.7
  67.9 6.7 %all-to-all-start.2 = ((bf16[16,2,64,128]{3,2,1,0:T(8,128)(2,1)}), bf16[16,2,64,128]{3,2,1,0:T(8,128)(2,1)S(1)}, u32[]{:S(2)}, u32[]{:S(2)}) async-start(bf16[16,2,64,128]{3,2,1,0:T(8,128)(2,1)} %broadcast_in_dim.7), calls=%async_computation.2 | async-start | bytes 1048576 | tf_op jit(solution)/shard_map/all_to_all | solution.py:348
  74.6 0.0 all-gather.7.cloned.1.call-start
  74.7 0.0 collective-permute-done.2
  74.7 0.8 pad_maximum_fusion
  75.5 9.7 %all-to-all-done.2 = bf16[16,2,64,128]{3,2,1,0:T(8,128)(2,1)S(1)} async-done(((bf16[16,2,64,128]{3,2,1,0:T(8,128)(2,1)}), bf16[16,2,64,128]{3,2,1,0:T(8,128)(2,1)S(1)}, u32[]{:S(2)}, u32[]{:S(2)}) %all-to-all-start.2) | async-done | bytes 524320 | tf_op jit(solution)/shard_map/all_to_all | solution.py:348
  85.3 0.3 broadcast_in_dim.8
  85.6 20.5 %all_to_all.21.a_ref = bf16[8,9,64,128]{3,2,1,0:T(8,128)(2,1)} all-to-all(bf16[8,9,64,128]{3,2,1,0:T(8,128)(2,1)S(1)} %broadcast_in_dim.8), channel_id=1, replica_groups=mesh['leaf'=8,'front'=16] {'leaf'}, dimensions={0} | all-to-all | bytes 2359296 | tf_op jit(solution)/shard_map/all_to_all | solution.py:348
  106.1 0.0 all-gather.7.cloned.1.call-update
  106.1 0.2 all-gather.9.cloned.1.call-start
  106.3 0.5 all-gather.9.cloned.1.call-update
  106.8 0.0 copy-start.6
  106.9 1.3 copy-done.6
  108.1 0.0 copy-start.1
  108.1 0.0 copy-start.2
  108.1 0.0 copy-start.3
  108.1 0.0 copy-start.7
  108.1 54.5 %cholesky.1 = (bf16[1024,1024]{1,0:T(8,128)(2,1)S(1)}, f32[128,128]{1,0:T(8,128)S(1)}) custom-call(bf16[8,9,64,128]{3,2,1,0:T(8,128)(2,1)S(1)} %copy-done.6), custom_call_target="tpu_custom_call" | custom-call | flops 60000002048 | bytes 6291456 | tf_op jit(solution)/shard_map/cholesky/pallas_call | solution.py:213
  162.7 0.0 copy-start.4
  162.7 1.3 copy-done.4
  164.0 0.0 all-gather.7.cloned.1.call-done.cols_hbm
  164.0 22.1 %all-gather.9.cloned.1.call-done = bf16[20480,128]{1,0:T(8,128)(2,1)} async-done(((bf16[1280,128]{1,0:T(8,128)(2,1)}), bf16[20480,128]{1,0:T(8,128)(2,1)}) %all-gather.9.cloned.1.call-update) | async-done | bytes 5242896 | tf_op jit(solution)/shard_map/all_gather | solution.py:381
  186.1 0.0 copy-done.1
  186.1 0.0 copy-done.2
  186.1 0.0 copy-done.3
  186.1 0.0 copy-done.7
  186.1 0.0 copy-start.5
  186.1 1.6 copy-done.5
  187.7 22.7 %schur.1 = f32[16384,128]{1,0:T(8,128)} custom-call(s32[8,16]{1,0:T(8,128)S(1)} %copy-done.7, f32[128,128]{1,0:T(8,128)S(1)} %get-tuple-element.23.l_ref, bf16[8,2,128,128]{3,2,1,0:T(8,128)(2,1)S(1)} %copy-done.2, bf16[2,8,64,512]{3,2,1,0:T(8,128)(2,1)S(1)} %bitcast.22, bf16[8,128,512]{2,1,0:T(8,128)(2,1)S(1)} %copy-done.3, ...), custom_call_target="tpu_custom_call" | custom-call | tf_op jit(solution)/shard_map/schur/pallas_call | solution.py:325
  (8 shorter events, 0.2 us)
Async XLA Ops:
  6.5 23.6 %copy-start.8 = (bf16[1,2048,128]{2,1,0:T(8,128)(2,1)S(1)}, bf16[1,2048,128]{2,1,0:T(8,128)(2,1)}, u32[]{:S(2)}) copy-start(bf16[1,2048,128]{2,1,0:T(8,128)(2,1)} %param.6) | copy-start | bytes 1572868
  6.5 55.0 %all-gather.5.cloned.1.call-start = ((), (), s32[]{:S(2)}) async-start(), calls=%async_computation.4 | async-start | bytes 1179648 | tf_op jit(solution)/shard_map/all_gather | solution.py:365
  8.2 6.6 %collective-permute-start.1 = (bf16[64,512]{1,0:T(8,128)(2,1)S(1)}, bf16[64,512]{1,0:T(8,128)(2,1)S(1)}, u32[]{:S(2)}, u32[]{:S(2)}) collective-permute-start(bf16[64,512]{1,0:T(8,128)(2,1)S(1)} %get-tuple-element.31), channel_id=1, source_target_pairs={{0,8},{1,24},{2,40},{3,56},{4,72},{5,88},{6,104},{7,120},{8,0},{9,... | collective-permute-start | bytes 196616 | tf_op jit(solution)/shard_map/ppermute | solution.py:369
  12.2 2.5 %collective-permute-start = (bf16[64,512]{1,0:T(8,128)(2,1)S(1)}, bf16[64,512]{1,0:T(8,128)(2,1)S(1)}, u32[]{:S(2)}, u32[]{:S(2)}) collective-permute-start(bf16[64,512]{1,0:T(8,128)(2,1)S(1)} %get-tuple-element.32), channel_id=1, source_target_pairs={{0,0},{1,16},{2,32},{3,48},{4,64},{5,80},{6,96},{7,112},{8,8},{9,2... | collective-permute-start | bytes 196616 | tf_op jit(solution)/shard_map/ppermute | solution.py:368
  15.8 31.0 %all-to-all-start = ((bf16[16,64,512]{2,1,0:T(8,128)(2,1)}), bf16[16,64,512]{2,1,0:T(8,128)(2,1)S(1)}, u32[]{:S(2)}, u32[]{:S(2)}) async-start(bf16[16,64,512]{2,1,0:T(8,128)(2,1)} %broadcast_in_dim.6), calls=%async_computation | async-start | bytes 2097152 | tf_op jit(solution)/shard_map/all_to_all | solution.py:348
  46.8 14.7 %copy-start = (bf16[16,64,512]{2,1,0:T(8,128)(2,1)}, bf16[16,64,512]{2,1,0:T(8,128)(2,1)S(1)}, u32[]{:S(2)}) copy-start(bf16[16,64,512]{2,1,0:T(8,128)(2,1)S(1)} %all-to-all-done) | copy-start | bytes 3145732
  64.6 10.1 %collective-permute-start.2 = (bf16[8,128,128]{2,1,0:T(8,128)(2,1)}, bf16[8,128,128]{2,1,0:T(8,128)(2,1)S(1)}, u32[]{:S(2)}, u32[]{:S(2)}) collective-permute-start(bf16[8,128,128]{2,1,0:T(8,128)(2,1)} %get-tuple-element.19), channel_id=1, source_target_pairs={{0,0},{1,16},{2,32},{3,48},{4,64},{5,80},{6,96},{7,112},{8,8},{9,2... | collective-permute-start | bytes 786440 | tf_op jit(solution)/shard_map/ppermute | solution.py:377
  67.9 17.3 %all-to-all-start.2 = ((bf16[16,2,64,128]{3,2,1,0:T(8,128)(2,1)}), bf16[16,2,64,128]{3,2,1,0:T(8,128)(2,1)S(1)}, u32[]{:S(2)}, u32[]{:S(2)}) async-start(bf16[16,2,64,128]{3,2,1,0:T(8,128)(2,1)} %broadcast_in_dim.7), calls=%async_computation.2 | async-start | bytes 1048576 | tf_op jit(solution)/shard_map/all_to_all | solution.py:348
  74.6 89.4 %all-gather.7.cloned.1.call-start = ((), (), s32[]{:S(2)}) async-start(), calls=%async_computation.5 | async-start | bytes 2359296 | tf_op jit(solution)/shard_map/all_gather | solution.py:386
  106.1 80.0 %all-gather.9.cloned.1.call-start = ((), (), s32[]{:S(2)}) async-start(), calls=%async_computation.6 | async-start | bytes 5570560 | tf_op jit(solution)/shard_map/all_gather | solution.py:381
  106.8 1.3 copy-start.6
  108.1 78.0 %copy-start.1 = (bf16[16,64,512]{2,1,0:T(8,128)(2,1)S(1)}, bf16[16,64,512]{2,1,0:T(8,128)(2,1)}, u32[]{:S(2)}) copy-start(bf16[16,64,512]{2,1,0:T(8,128)(2,1)} %copy-done) | copy-start | bytes 3145732
  108.1 78.0 %copy-start.2 = (bf16[8,2,128,128]{3,2,1,0:T(8,128)(2,1)S(1)}, bf16[8,2,128,128]{3,2,1,0:T(8,128)(2,1)}, u32[]{:S(2)}) copy-start(bf16[8,2,128,128]{3,2,1,0:T(8,128)(2,1)} %all_to_all.20.given_ref) | copy-start | bytes 1572868
  108.1 78.0 %copy-start.3 = (bf16[8,128,512]{2,1,0:T(8,128)(2,1)S(1)}, bf16[8,128,512]{2,1,0:T(8,128)(2,1)}, u32[]{:S(2)}) copy-start(bf16[8,128,512]{2,1,0:T(8,128)(2,1)} %all-gather.5.cloned.1.call-done.cols_ref.panel_ref) | copy-start | bytes 3145732
  108.1 78.0 %copy-start.7 = (s32[8,16]{1,0:T(8,128)S(1)}, s32[8,16]{1,0:T(8,128)}, u32[]{:S(2)}) copy-start(s32[8,16]{1,0:T(8,128)} %map_ref.3) | copy-start | bytes 1540
  162.7 1.3 copy-start.4
  186.1 1.6 copy-start.5
Sparse Core Ops, SparseCore 0:
  9.0 25.7 all-gather.4
  106.2 20.9 all-gather.6
  129.3 56.7 all-gather.8
where the time goes:
time: 218 us; the launch traced here: 217 us
  Pallas kernels  80.4 us (37%)
  waiting for transfers between devices  51.4 us (24%)
  blocking collectives  35.3 us (16%)
  starting transfers between devices  27.6 us (13%)
  between operations  13.3 us (6%)
  local copies, waits for them, and re-layouts  7.32 us (3%)
    pallas_call x1, Pallas kernels, cholesky(): pl.pallas_call(cholesky_kernel, name='cholesky', out_shape=(jax.ShapeDtyp...  54.5 us
    all_to_all x2, waiting for transfers between devices, gather(): return lax.all_to_all(spread, axis, 0, 0)  26.2 us
    pallas_call x1, Pallas kernels, schur(): pl.pallas_call(schur_kernel, name='schur', grid=(steps,), out_shape=jax.S...  22.7 us
    all_gather x1, waiting for transfers between devices, one_pass(): rows = lax.all_gather(packed, 'front', axis=0)  22.1 us
    all_to_all x2, starting transfers between devices, gather(): return lax.all_to_all(spread, axis, 0, 0)  21 us
    all_to_all x1, blocking collectives, gather(): return lax.all_to_all(spread, axis, 0, 0)  20.5 us
    all_to_all x1, blocking collectives, one_pass(): given = lax.all_to_all(blocks, 'leaf', 0, 0)  14.7 us
  transfers between devices with their start and end apart: 8, of which 4 were waited for; matrix products, arithmetic and copies ran while one was open for 2% of the time, Pallas kernels for 25%

commit v1 on v0

--- a/solution.py
+++ b/solution.py
@@ -92,8 +92,8 @@
     return jnp.broadcast_to(x[:, j : j + 1], (8, BLK))
 
 
-def subs(x, i):
-    return jnp.broadcast_to(x[i : i + 1, :], (8, BLK))
+def spread(ref, i):
+    return ref[pl.ds(i, 8, stride=0), :]
 
 
 def sum_products(v, r):
@@ -103,16 +103,24 @@
     return t[0]
 
 
-def factor(g_ref, e_ref):
+def high_part(x):
+    return x.astype(BF16).astype(F32)
+
+
+def factor(g_ref, e_ref, c_ref):
     for p in range(16):
         rows = pl.ds(8 * p, 8)
         below = pl.ds(8 * p + 8, 8)
         top = g_ref[rows, :]
-        side = e_ref[rows, :]
-        cols = [lanes(top, 8 * p + j) for j in range(8)]
-        a = [[subs(cols[j], i) if j <= i else None for j in range(8)] for i in range(8)]
-        r = [subs(top, i) for i in range(8)]
-        e = [subs(side, i) for i in range(8)]
+        slot = p % 2 * 64
+        for j in range(8):
+            c_ref[slot + 8 * j : slot + 8 * j + 8, :] = lanes(top, 8 * p + j)
+        a = [
+            [spread(c_ref, slot + 8 * j + i) if j <= i else None for j in range(8)]
+            for i in range(8)
+        ]
+        r = [spread(g_ref, 8 * p + i) for i in range(8)]
+        e = [spread(e_ref, 8 * p + i) for i in range(8)]
         more = p < 15
         if more:
             after = g_ref[below, :]
@@ -145,12 +153,22 @@
         g_ref[rows, :] = u
         e_ref[rows, :] = w
         if p < 14:
-            turned = jnp.transpose(u)
-            for g in range(p + 2, 16):
-                vg = [lanes(turned[8 * g : 8 * g + 8, :], i) for i in range(8)]
-                there = pl.ds(8 * g, 8)
-                g_ref[there, :] = g_ref[there, :] - sum_products(vg, r)
-                e_ref[there, :] = e_ref[there, :] - sum_products(vg, e)
+            turned = jnp.transpose(u)[8 * p + 16 : 8 * p + 24, :]
+            vg = [lanes(turned, i) for i in range(8)]
+            there = pl.ds(8 * p + 16, 8)
+            g_ref[there, :] = g_ref[there, :] - sum_products(vg, r)
+            e_ref[there, :] = e_ref[there, :] - sum_products(vg, e)
+        if p < 13:
+            uh, wh = high_part(u), high_part(w)
+            ul, wl = u - uh, w - wh
+            left = jnp.concatenate([uh, uh, ul, ul], axis=0).astype(BF16)
+            top = jnp.concatenate([uh, wh], axis=1)
+            low = jnp.concatenate([ul, wl], axis=1)
+            right = jnp.concatenate([top, low, top, low], axis=0).astype(BF16)
+            both = dot(left, right, 0, 0)
+            there = slice(8 * p + 24, BLK)
+            g_ref[there, :] = g_ref[there, :] - both[there, :BLK]
+            e_ref[there, :] = e_ref[there, :] - both[there, BLK:]
 
 
 def halves(x):
@@ -158,20 +176,21 @@
     return high, (x - high.astype(F32)).astype(BF16)
 
 
-def dot3(a, b, ca, cb):
-    return dot(a[0], b[0], ca, cb) + (dot(a[0], b[1], ca, cb) + dot(a[1], b[0], ca, cb))
-
-
 def cholesky_kernel(
-    a_ref, m_hbm, l_ref, s_ref, d_ref, g_ref, e_ref, nh_ref, nl_ref, m_ref, sem
+    *refs
 ):
+    piece_refs, refs = refs[:N_LEAF], refs[N_LEAF:]
+    (m_hbm, l_ref, s_ref, d_ref, g_ref, e_ref, nl_ref, nr_ref, m_ref, c_ref, sem) = refs
+    leaf, front = place()
     half = BLK // 2
-    for r in range(KS):
-        for c in range(r, KS):
-            cols = slice(c * BLK, (c + 1) * BLK)
-            lower = a_ref[r, KS] if c == r else a_ref[r, c]
-            s_ref[r * BLK : r * BLK + half, cols] = a_ref[c, r].astype(F32)
-            s_ref[r * BLK + half : (r + 1) * BLK, cols] = lower.astype(F32)
+    for k in range(N_LEAF):
+        giver = (leaf + N_LEAF - k) % N_LEAF * BLK
+        for j in range(KS + 1):
+            top = j * BLK <= giver
+            row = jnp.where(top, j * BLK, giver + half) if j < KS else giver + half
+            col = jnp.where(top, giver, j * BLK) if j < KS else giver
+            rows = pl.ds(pl.multiple_of(row, half), half)
+            s_ref[rows, pl.ds(pl.multiple_of(col, BLK), BLK)] = piece_refs[k][j].astype(F32)
     row_id = lax.broadcasted_iota(jnp.int32, (BLK, BLK), 0)
     col_id = lax.broadcasted_iota(jnp.int32, (BLK, BLK), 1)
     ident = (row_id == col_id).astype(F32)
@@ -181,12 +200,19 @@
         here = pl.ds(pl.multiple_of(k * BLK, BLK), BLK)
         g_ref[...] = s_ref[here, here]
         e_ref[...] = ident
-        factor(g_ref, e_ref)
+        factor(g_ref, e_ref, c_ref)
         d_ref[here, :] = g_ref[...]
         s_ref[here, here] = ident
-        row = dot3(halves(e_ref[...]), halves(s_ref[here, :]), 1, 0)
+        eh, el = halves(e_ref[...])
+        sh, sl = halves(s_ref[here, :])
+        left = jnp.concatenate([eh, el, eh], axis=1)
+        row = dot(left, jnp.concatenate([sh, sh, sl], axis=0), 1, 0)
         s_ref[here, :] = row
-        nh_ref[...], nl_ref[...] = halves(row)
+        high, low = halves(row)
+        for n in range(3):
+            part = slice(n * BLK, (n + 1) * BLK)
+            nl_ref[part, :] = low if n == 1 else high
+            nr_ref[part, :] = low if n == 2 else high
         keep = lax.broadcasted_iota(jnp.int32, (BLK, ORDER), 1) < (k + 1) * BLK
         m_ref[here, :] = jnp.where(keep, row, 0.0).astype(BF16)
 
@@ -194,12 +220,10 @@
         def _(i):
             there = pl.ds(pl.multiple_of(i * BLK, BLK), BLK)
             s_ref[there, here] = jnp.zeros((BLK, BLK), F32)
-            part = nh_ref[:, there], nl_ref[:, there]
-            s_ref[there, :] = s_ref[there, :] - dot3(part, (nh_ref[...], nl_ref[...]), 0, 0)
+            s_ref[there, :] = s_ref[there, :] - dot(nl_ref[:, there], nr_ref[...], 0, 0)
 
     out = pltpu.make_async_copy(m_ref, m_hbm, sem)
     out.start()
-    leaf, front = place()
     front = jnp.minimum(front, KS - 1)
     mine = pl.ds(pl.multiple_of(leaf * BLK, BLK), BLK)
     other = pl.ds(pl.multiple_of(front * BLK, BLK), BLK)
@@ -209,7 +233,7 @@
     out.wait()
 
 
-def cholesky(a):
+def cholesky(pieces):
     return pl.pallas_call(
         cholesky_kernel,
         name="cholesky",
@@ -217,23 +241,24 @@
             jax.ShapeDtypeStruct((ORDER, ORDER), BF16),
             jax.ShapeDtypeStruct((BLK, BLK), F32),
         ),
-        in_specs=[WHOLE],
+        in_specs=[WHOLE] * N_LEAF,
         out_specs=(pl.BlockSpec(memory_space=pltpu.HBM), WHOLE),
         scratch_shapes=[
             pltpu.VMEM((ORDER, ORDER), F32),
             pltpu.VMEM((ORDER, BLK), F32),
             pltpu.VMEM((BLK, BLK), F32),
             pltpu.VMEM((BLK, BLK), F32),
-            pltpu.VMEM((BLK, ORDER), BF16),
-            pltpu.VMEM((BLK, ORDER), BF16),
+            pltpu.VMEM((3 * BLK, ORDER), BF16),
+            pltpu.VMEM((3 * BLK, ORDER), BF16),
             pltpu.VMEM((ORDER, ORDER), BF16),
+            pltpu.VMEM((BLK, BLK), F32),
             pltpu.SemaphoreType.DMA,
         ],
         compiler_params=pltpu.CompilerParams(vmem_limit_bytes=24 << 20),
         cost_estimate=pl.CostEstimate(
             flops=60_000_000_000, bytes_accessed=6 << 20, transcendentals=1024
         ),
-    )(a)
+    )(*pieces)
 
 
 def schur_kernel(
@@ -243,7 +268,6 @@
     step = pl.program_id(0)
     leaf, front = place()
     owner = jnp.minimum(front, KS - 1)
-    rows_here = STEP_ROWS * BLK
 
     def copies():
         yield pltpu.make_async_copy(m_hbm, m_ref, sem.at[2, 0])
@@ -282,19 +306,22 @@
                 product += dot(rows, panel_ref[c, :, n * BLK : (n + 1) * BLK], 1, 1)
             update_ref[c, 1] = (given_ref[c, 1].astype(F32) - product).astype(BF16)
 
-    for q in range(STEP_ROWS):
-        source = pl.ds(pl.multiple_of((step * (STEP_ROWS // 2) + q // 2) * BLK, BLK), BLK)
-        mine = slice(q * BLK, (q + 1) * BLK)
-        for n in range(4):
-            take = slice(n * 256, (n + 1) * 256)
-            upto = slice(0, (n + 1) * 256)
-            low_ref[mine, take] = dot(rows_ref[q % 2, source, upto], m_ref[take, upto], 1, 1)
+    pair = STEP_ROWS // 2 * BLK
+    source = pl.ds(pl.multiple_of(step * pair, pair), pair)
+    for n in range(4):
+        take = slice(n * 256, (n + 1) * 256)
+        upto = slice(0, (n + 1) * 256)
+        both = jnp.concatenate([rows_ref[0, source, upto], rows_ref[1, source, upto]], axis=0)
+        low_ref[:, take] = dot(both, m_ref[take, upto], 1, 1)
     low = low_ref[...].astype(BF16)
+    order = [q % 2 * pair + q // 2 * BLK for q in range(STEP_ROWS)]
     for n in range(4):
         part = dot(low, w_ref[:, n * 256 : (n + 1) * 256], 1, 0)
         for s in range(2):
-            there = pl.ds(2 * n + s, rows_here, stride=8)
-            out_ref[there, :] = front_ref[there, :] - part[:, s * BLK : (s + 1) * BLK]
+            for q, at in enumerate(order):
+                there = pl.ds(q * 8 * BLK + 2 * n + s, BLK, stride=8)
+                product = part[at : at + BLK, s * BLK : (s + 1) * BLK]
+                out_ref[there, :] = front_ref[there, :] - product
     for c in range(N_LEAF):
         s = map_ref[c, front] // N_FRONT
         for b in range(2):
@@ -308,7 +335,8 @@
     @pl.when(front < KS)
     def _():
         column = pl.ds(pl.multiple_of(owner * BLK, BLK), BLK)
-        out_ref[pl.ds(0, rows_here, stride=8), :] = low_ref[:, column]
+        for q, at in enumerate(order):
+            out_ref[pl.ds(q * 8 * BLK, BLK, stride=8), :] = low_ref[at : at + BLK, column]
 
     @pl.when(step == 0)
     def _():
@@ -362,17 +390,17 @@
     front_id = lax.axis_index("front")
     leaf_id = lax.axis_index("leaf")
     own = child_panels[0]
-    panels = lax.all_gather(own, "leaf", axis=0)
     halves_of = own.reshape(2, BLK // 2, own.shape[1])
     early = front_id < N_LEAF
     same = lax.ppermute(jnp.where(early, halves_of[0], halves_of[1]), MESH_AXES, exchange(0))
     other = lax.ppermute(jnp.where(early, halves_of[1], halves_of[0]), MESH_AXES, exchange(1))
+    blocks = child_blocks[0].reshape(2, N_LEAF, BLK, BLK).transpose(1, 0, 2, 3)
+    given = lax.all_to_all(blocks, "leaf", 0, 0)
+    own, same, other, given = lax.optimization_barrier((own, same, other, given))
+    panels = lax.all_gather(own, "leaf", axis=0)
     upper = gather(jnp.where(early, same, other), "front", N_FRONT)
     upper = upper.reshape(2, N_LEAF, BLK // 2, own.shape[1])
     lower = jnp.where(early, other, same).reshape(BLK // 2, 4, BLK).transpose(1, 0, 2)
-    blocks = child_blocks[0].reshape(2, N_LEAF, BLK, BLK).transpose(1, 0, 2, 3)
-    blocks, upper = lax.optimization_barrier((blocks, upper))
-    given = lax.all_to_all(blocks, "leaf", 0, 0)
     flat, turned, first = pivot_rows(child_map, front, given, upper, panels)
     turned = lax.ppermute(turned, MESH_AXES, exchange(0))
     packed = jnp.concatenate([turned.reshape(ORDER, BLK), lower.reshape(2 * BLK, BLK)], axis=0)
@@ -381,8 +409,10 @@
     rows = lax.all_gather(packed, "front", axis=0)
     extra = lax.dynamic_index_in_dim(pieces[:, 1], leaf_id, 0, keepdims=True)
     whole = jnp.concatenate([pieces[:, 0], extra], axis=0)
-    separator = gather(whole, "leaf", N_LEAF)
-    flat, separator = lax.optimization_barrier((flat, separator))
+    separator = [whole] + [
+        lax.ppermute(whole, "leaf", [(i, (i + k) % N_LEAF) for i in range(N_LEAF)])
+        for k in range(1, N_LEAF)
+    ]
     cols = lax.all_gather(flat, "leaf", axis=0, tiled=True)
     m, low = cholesky(separator)
     rows = rows.reshape(2, KS, ORDER + 2 * BLK, BLK)

time: 218 us -> 171 us (0.78)
  waiting for transfers between devices: 51.4 us -> 29.6 us
  Pallas kernels: 80.4 us -> 66.1 us
  blocking collectives: 35.3 us -> 28.1 us
  starting transfers between devices: 27.6 us -> 24.4 us
    all_gather x1, waiting for transfers between devices: 22.1 us -> 0.01 us  [one_pass(): rows = lax.all_gather(packed, 'front', axis=0)]
    all_to_all x2 -> x1, waiting for transfers between devices: 26.2 us -> 11 us  [gather(): return lax.all_to_all(spread, axis, 0, 0)]
    all_to_all x1 -> x0, blocking collectives: 14.7 us -> none  [one_pass(): given = lax.all_to_all(blocks, 'leaf', 0, 0)]
    ppermute x0 -> x7, waiting for transfers between devices: none -> 13.8 us  [one_pass(): lax.ppermute(whole, 'leaf', [(i, (i + k) % N_LEAF) for i in range(N_LEAF)])]
    all_to_all x2 -> x1, starting transfers between devices: 21 us -> 7.83 us  [gather(): return lax.all_to_all(spread, axis, 0, 0)]
    pallas_call x1, Pallas kernels: 54.5 us -> 44.1 us  [cholesky(): pl.pallas_call(cholesky_kernel, name='cholesky', out_shape=(jax.ShapeDtyp...]
    all_to_all x1, blocking collectives: 20.5 us -> 28.1 us  [gather(): return lax.all_to_all(spread, axis, 0, 0)]
    ppermute x0 -> x7, starting transfers between devices: none -> 5.61 us  [one_pass(): lax.ppermute(whole, 'leaf', [(i, (i + k) % N_LEAF) for i in range(N_LEAF)])]
  transfers between devices with their start and end apart: 8 -> 15, of which waited for: 4 -> 9; matrix products, arithmetic and copies ran while one was open for 2% -> 2% of each run, Pallas kernels for 25% -> 26%
where the time goes in v1:
time: 171 us; the launch traced here: 170 us
  Pallas kernels  66.1 us (39%)
  waiting for transfers between devices  29.6 us (17%)
  blocking collectives  28.1 us (16%)
  starting transfers between devices  24.4 us (14%)
  between operations  13.3 us (8%)
  local copies, waits for them, and re-layouts  6.67 us (4%)
    pallas_call x1, Pallas kernels, cholesky(): pl.pallas_call(cholesky_kernel, name='cholesky', out_shape=(jax.ShapeDtyp...  44.1 us
    all_to_all x1, blocking collectives, gather(): return lax.all_to_all(spread, axis, 0, 0)  28.1 us
    pallas_call x1, Pallas kernels, schur(): pl.pallas_call(schur_kernel, name='schur', grid=(steps,), out_shape=jax.S...  18.9 us
    ppermute x7, waiting for transfers between devices, one_pass(): lax.ppermute(whole, 'leaf', [(i, (i + k) % N_LEAF) for i in range(N_LEAF)])  13.8 us
    all_to_all x1, waiting for transfers between devices, gather(): return lax.all_to_all(spread, axis, 0, 0)  11 us
    all_to_all x1, starting transfers between devices, gather(): return lax.all_to_all(spread, axis, 0, 0)  7.83 us
    ppermute x7, starting transfers between devices, one_pass(): lax.ppermute(whole, 'leaf', [(i, (i + k) % N_LEAF) for i in range(N_LEAF)])  5.61 us
    all_to_all x1, starting transfers between devices, one_pass(): given = lax.all_to_all(blocks, 'leaf', 0, 0)  4.58 us
  transfers between devices with their start and end apart: 15, of which 9 were waited for; matrix products, arithmetic and copies ran while one was open for 2% of the time, Pallas kernels for 26%

profile of v1, /device:TPU:0, one launch (start us, length us, event | category | flops | bytes accessed | tf_op | source)
XLA Modules:
  0.0 169.9 jit_solution(2339828060241279642)
XLA Ops:
  6.5 1.9 %copy.16 = bf16[2,8,128,128]{3,2,0,1:T(8,128)(2,1)} copy(bf16[2,8,128,128]{3,2,1,0:T(8,128)(2,1)} %bitcast.30) | data formatting | bytes 1048576 | tf_op jit(solution)/shard_map/reshape;squeeze | solution.py:397
  8.4 4.6 %all-to-all-start = ((bf16[8,2,128,128]{3,2,1,0:T(8,128)(2,1)}), bf16[8,2,128,128]{3,2,1,0:T(8,128)(2,1)S(1)}, u32[]{:S(2)}, u32[]{:S(2)}) async-start(bf16[8,2,128,128]{3,2,1,0:T(8,128)(2,1)} %bitcast.22), calls=%async_computation | async-start | bytes 1048576 | tf_op jit(solution)/shard_map/all_to_all | solution.py:398
  13.0 0.0 all-gather.8.cloned.1.call-start
  13.1 0.9 select_bitcast_fusion
  13.9 4.0 %collective-permute-start.1 = (bf16[64,512]{1,0:T(8,128)(2,1)S(1)}, bf16[64,512]{1,0:T(8,128)(2,1)S(1)}, u32[]{:S(2)}, u32[]{:S(2)}) collective-permute-start(bf16[64,512]{1,0:T(8,128)(2,1)S(1)} %get-tuple-element.31), channel_id=1, source_target_pairs={{0,8},{1,24},{2,40},{3,56},{4,72},{5,88},{6,104},{7,120},{8,0},{9,... | collective-permute-start | bytes 196616 | tf_op jit(solution)/shard_map/ppermute | solution.py:396
  17.9 0.7 collective-permute-start
  18.6 1.6 collective-permute-done.1
  20.1 0.0 collective-permute-done
  20.1 3.2 %all-to-all-done.given_ref = bf16[8,2,128,128]{3,2,1,0:T(8,128)(2,1)S(1)} async-done(((bf16[8,2,128,128]{3,2,1,0:T(8,128)(2,1)}), bf16[8,2,128,128]{3,2,1,0:T(8,128)(2,1)S(1)}, u32[]{:S(2)}, u32[]{:S(2)}) %all-to-all-start) | async-done | bytes 524320 | tf_op jit(solution)/shard_map/all_to_all | solution.py:398
  23.3 0.0 copy-start.1
  23.3 0.0 all-gather.8.cloned.1.call-update
  23.3 0.0 all-gather.6.cloned.1.call-start
  23.4 0.1 broadcast_in_dim.4
  23.5 28.1 %all_to_all.15 = bf16[16,64,512]{2,1,0:T(8,128)(2,1)} all-to-all(bf16[16,64,512]{2,1,0:T(8,128)(2,1)S(1)} %broadcast_in_dim.4), channel_id=1, replica_groups=mesh['leaf'=8,'front'=16] {'front'}, dimensions={0} | all-to-all | bytes 2097152 | tf_op jit(solution)/shard_map/all_to_all | solution.py:376
  51.7 0.0 all-gather.8.cloned.1.call-done
  51.7 0.0 copy-done.1
  51.7 3.2 %pivot_rows.1 = (bf16[128,1024]{1,0:T(8,128)(2,1)}, bf16[8,128,128]{2,1,0:T(8,128)(2,1)}, bf16[2,64,128]{2,1,0:T(8,128)(2,1)}) custom-call(s32[8,16]{1,0:T(8,128)} %map_ref.3, f32[16384,128]{1,0:T(8,128)} %bitcast.27, bf16[8,2,128,128]{3,2,1,0:T(8,128)(2,1)} %copy-done.1, bf16[2,8,64,512]{3,2,1,0:T(8,128)(2,1)} %bitcast.23, bf16[8,128,512]{2,1,0:T(8,128)(2,1)} %bitcast.25), custom_call_target="tpu_custom_call" | custom-call | tf_op jit(solution)/shard_map/pivot_rows/pallas_call | solution.py:66
  54.8 0.0 all-gather.6.cloned.1.call-update
  54.8 1.6 collective-permute-start.2
  56.5 1.7 broadcast_in_dim.5
  58.1 7.8 %all-to-all-start.2 = ((bf16[16,2,64,128]{3,2,1,0:T(8,128)(2,1)}), bf16[16,2,64,128]{3,2,1,0:T(8,128)(2,1)S(1)}, u32[]{:S(2)}, u32[]{:S(2)}) async-start(bf16[16,2,64,128]{3,2,1,0:T(8,128)(2,1)} %broadcast_in_dim.5), calls=%async_computation.2 | async-start | bytes 1048576 | tf_op jit(solution)/shard_map/all_to_all | solution.py:376
  66.0 0.0 all-gather.10.cloned.1.call-start
  66.1 0.0 collective-permute-done.2
  66.1 0.8 pad_maximum_fusion
  66.9 11.0 %all-to-all-done.2 = bf16[16,2,64,128]{3,2,1,0:T(8,128)(2,1)S(1)} async-done(((bf16[16,2,64,128]{3,2,1,0:T(8,128)(2,1)}), bf16[16,2,64,128]{3,2,1,0:T(8,128)(2,1)S(1)}, u32[]{:S(2)}, u32[]{:S(2)}) %all-to-all-start.2) | async-done | bytes 524320 | tf_op jit(solution)/shard_map/all_to_all | solution.py:376
  77.9 0.0 all-gather.10.cloned.1.call-update
  78.0 0.0 copy-start
  78.0 0.0 copy-start.2
  78.1 0.0 copy-start.3
  78.1 0.0 copy-start.6
  78.1 0.4 collective-permute-start.9
  78.5 1.9 %collective-permute-start.8 = (bf16[9,64,128]{2,1,0:T(8,128)(2,1)S(1)}, bf16[9,64,128]{2,1,0:T(8,128)(2,1)S(1)}, u32[]{:S(2)}, u32[]{:S(2)}) collective-permute-start(bf16[9,64,128]{2,1,0:T(8,128)(2,1)S(1)} %pad_maximum_fusion.1.refs_0_), channel_id=1, source_target_pairs={{0,96},{16,112},{32,0},{48,16},{64,32},{80,48},{96,64},{112,80},{1... | collective-permute-start | bytes 442376 | tf_op jit(solution)/shard_map/ppermute | solution.py:413
  80.4 0.6 collective-permute-start.7
  81.0 2.6 %collective-permute-start.6 = (bf16[9,64,128]{2,1,0:T(8,128)(2,1)S(1)}, bf16[9,64,128]{2,1,0:T(8,128)(2,1)S(1)}, u32[]{:S(2)}, u32[]{:S(2)}) collective-permute-start(bf16[9,64,128]{2,1,0:T(8,128)(2,1)S(1)} %pad_maximum_fusion.1.refs_0_), channel_id=1, source_target_pairs={{0,64},{16,80},{32,96},{48,112},{64,0},{80,16},{96,32},{112,48},{1... | collective-permute-start | bytes 442376 | tf_op jit(solution)/shard_map/ppermute | solution.py:413
  83.7 0.0 collective-permute-start.5
  83.7 0.0 collective-permute-done.9.refs_7_
  83.7 0.0 collective-permute-start.4
  83.7 2.8 %collective-permute-done.8.refs_6_ = bf16[9,64,128]{2,1,0:T(8,128)(2,1)S(1)} collective-permute-done((bf16[9,64,128]{2,1,0:T(8,128)(2,1)S(1)}, bf16[9,64,128]{2,1,0:T(8,128)(2,1)S(1)}, u32[]{:S(2)}, u32[]{:S(2)}) %collective-permute-start.8) | collective-permute-done | bytes 147488 | tf_op jit(solution)/shard_map/ppermute | solution.py:413
  86.5 0.0 collective-permute-start.3
  86.5 1.0 collective-permute-done.7.refs_5_
  87.5 3.5 %collective-permute-done.6.refs_4_ = bf16[9,64,128]{2,1,0:T(8,128)(2,1)S(1)} collective-permute-done((bf16[9,64,128]{2,1,0:T(8,128)(2,1)S(1)}, bf16[9,64,128]{2,1,0:T(8,128)(2,1)S(1)}, u32[]{:S(2)}, u32[]{:S(2)}) %collective-permute-start.6) | collective-permute-done | bytes 147488 | tf_op jit(solution)/shard_map/ppermute | solution.py:413
  91.0 0.3 collective-permute-done.5.refs_3_
  91.4 6.0 %collective-permute-done.4.refs_2_ = bf16[9,64,128]{2,1,0:T(8,128)(2,1)S(1)} collective-permute-done((bf16[9,64,128]{2,1,0:T(8,128)(2,1)S(1)}, bf16[9,64,128]{2,1,0:T(8,128)(2,1)S(1)}, u32[]{:S(2)}, u32[]{:S(2)}) %collective-permute-start.4) | collective-permute-done | bytes 147488 | tf_op jit(solution)/shard_map/ppermute | solution.py:413
  97.4 0.1 collective-permute-done.3.refs_1_
  97.5 44.1 %cholesky.1 = (bf16[1024,1024]{1,0:T(8,128)(2,1)S(1)}, f32[128,128]{1,0:T(8,128)S(1)}) custom-call(bf16[9,64,128]{2,1,0:T(8,128)(2,1)S(1)} %pad_maximum_fusion.1.refs_0_, bf16[9,64,128]{2,1,0:T(8,128)(2,1)S(1)} %collective-permute-done.3.refs_1_, bf16[9,64,128]{2,1,0:T(8,128)(2,1)S(1)} %collective-permute-done.4.refs_2_, ...), custom_call_target="tpu_custom_call" | custom-call | flops 60000002048 | bytes 6291456 | tf_op jit(solution)/shard_map/cholesky/pallas_call | solution.py:237
  141.5 0.0 copy-start.4
  141.5 1.3 copy-done.4
  142.9 0.0 all-gather.6.cloned.1.call-done.cols_hbm
  142.9 0.0 all-gather.10.cloned.1.call-done
  142.9 0.0 copy-done
  142.9 0.0 copy-done.2
  142.9 0.0 copy-done.3
  142.9 0.0 copy-done.6
  142.9 0.0 copy-start.5
  142.9 1.6 copy-done.5
  144.5 18.9 %schur.1 = f32[16384,128]{1,0:T(8,128)} custom-call(s32[8,16]{1,0:T(8,128)S(1)} %copy-done.6, f32[128,128]{1,0:T(8,128)S(1)} %get-tuple-element.23.l_ref, bf16[8,2,128,128]{3,2,1,0:T(8,128)(2,1)S(1)} %copy-done.2, bf16[2,8,64,512]{3,2,1,0:T(8,128)(2,1)S(1)} %bitcast.24, bf16[8,128,512]{2,1,0:T(8,128)(2,1)S(1)} %bitcast.26, bf16[1024,1024]{1,0:T(8,128)(2,1)S(1)} %copy-done.5, ...), custom_call_target="tpu_custom_call" | custom-call | tf_op jit(solution)/shard_map/schur/pallas_call | solution.py:353
  (8 shorter events, 0.1 us)
Async XLA Ops:
  8.4 14.9 %all-to-all-start = ((bf16[8,2,128,128]{3,2,1,0:T(8,128)(2,1)}), bf16[8,2,128,128]{3,2,1,0:T(8,128)(2,1)S(1)}, u32[]{:S(2)}, u32[]{:S(2)}) async-start(bf16[8,2,128,128]{3,2,1,0:T(8,128)(2,1)} %bitcast.22), calls=%async_computation | async-start | bytes 1048576 | tf_op jit(solution)/shard_map/all_to_all | solution.py:398
  13.0 38.7 %all-gather.8.cloned.1.call-start = ((), (), s32[]{:S(2)}) async-start(), calls=%async_computation.4 | async-start | bytes 1179648 | tf_op jit(solution)/shard_map/all_gather | solution.py:400
  13.9 6.2 %collective-permute-start.1 = (bf16[64,512]{1,0:T(8,128)(2,1)S(1)}, bf16[64,512]{1,0:T(8,128)(2,1)S(1)}, u32[]{:S(2)}, u32[]{:S(2)}) collective-permute-start(bf16[64,512]{1,0:T(8,128)(2,1)S(1)} %get-tuple-element.31), channel_id=1, source_target_pairs={{0,8},{1,24},{2,40},{3,56},{4,72},{5,88},{6,104},{7,120},{8,0},{9,... | collective-permute-start | bytes 196616 | tf_op jit(solution)/shard_map/ppermute | solution.py:396
  17.9 2.2 %collective-permute-start = (bf16[64,512]{1,0:T(8,128)(2,1)S(1)}, bf16[64,512]{1,0:T(8,128)(2,1)S(1)}, u32[]{:S(2)}, u32[]{:S(2)}) collective-permute-start(bf16[64,512]{1,0:T(8,128)(2,1)S(1)} %get-tuple-element.32), channel_id=1, source_target_pairs={{0,0},{1,16},{2,32},{3,48},{4,64},{5,80},{6,96},{7,112},{8,8},{9,2... | collective-permute-start | bytes 196616 | tf_op jit(solution)/shard_map/ppermute | solution.py:395
  23.3 28.4 %copy-start.1 = (bf16[8,2,128,128]{3,2,1,0:T(8,128)(2,1)}, bf16[8,2,128,128]{3,2,1,0:T(8,128)(2,1)S(1)}, u32[]{:S(2)}) copy-start(bf16[8,2,128,128]{3,2,1,0:T(8,128)(2,1)S(1)} %all-to-all-done.given_ref) | copy-start | bytes 1572868
  23.3 119.5 %all-gather.6.cloned.1.call-start = ((), (), s32[]{:S(2)}) async-start(), calls=%async_computation.3 | async-start | bytes 2359296 | tf_op jit(solution)/shard_map/all_gather | solution.py:416
  54.8 11.2 %collective-permute-start.2 = (bf16[8,128,128]{2,1,0:T(8,128)(2,1)}, bf16[8,128,128]{2,1,0:T(8,128)(2,1)S(1)}, u32[]{:S(2)}, u32[]{:S(2)}) collective-permute-start(bf16[8,128,128]{2,1,0:T(8,128)(2,1)} %get-tuple-element.20), channel_id=1, source_target_pairs={{0,0},{1,16},{2,32},{3,48},{4,64},{5,80},{6,96},{7,112},{8,8},{9,2... | collective-permute-start | bytes 786440 | tf_op jit(solution)/shard_map/ppermute | solution.py:405
  58.1 19.8 %all-to-all-start.2 = ((bf16[16,2,64,128]{3,2,1,0:T(8,128)(2,1)}), bf16[16,2,64,128]{3,2,1,0:T(8,128)(2,1)S(1)}, u32[]{:S(2)}, u32[]{:S(2)}) async-start(bf16[16,2,64,128]{3,2,1,0:T(8,128)(2,1)} %broadcast_in_dim.5), calls=%async_computation.2 | async-start | bytes 1048576 | tf_op jit(solution)/shard_map/all_to_all | solution.py:376
  66.0 76.9 %all-gather.10.cloned.1.call-start = ((), (), s32[]{:S(2)}) async-start(), calls=%async_computation.5 | async-start | bytes 5570560 | tf_op jit(solution)/shard_map/all_gather | solution.py:409
  78.0 64.8 %copy-start = (bf16[16,64,512]{2,1,0:T(8,128)(2,1)S(1)}, bf16[16,64,512]{2,1,0:T(8,128)(2,1)}, u32[]{:S(2)}) copy-start(bf16[16,64,512]{2,1,0:T(8,128)(2,1)} %all_to_all.15) | copy-start | bytes 3145732
  78.0 64.8 %copy-start.2 = (bf16[8,2,128,128]{3,2,1,0:T(8,128)(2,1)S(1)}, bf16[8,2,128,128]{3,2,1,0:T(8,128)(2,1)}, u32[]{:S(2)}) copy-start(bf16[8,2,128,128]{3,2,1,0:T(8,128)(2,1)} %copy-done.1) | copy-start | bytes 1572868
  78.1 64.8 %copy-start.3 = (bf16[1024,512]{1,0:T(8,128)(2,1)S(1)}, bf16[1024,512]{1,0:T(8,128)(2,1)}, u32[]{:S(2)}) copy-start(bf16[1024,512]{1,0:T(8,128)(2,1)} %all-gather.8.cloned.1.call-done) | copy-start | bytes 3145732
  78.1 64.8 %copy-start.6 = (s32[8,16]{1,0:T(8,128)S(1)}, s32[8,16]{1,0:T(8,128)}, u32[]{:S(2)}) copy-start(s32[8,16]{1,0:T(8,128)} %map_ref.3) | copy-start | bytes 1540
  78.1 5.6 %collective-permute-start.9 = (bf16[9,64,128]{2,1,0:T(8,128)(2,1)S(1)}, bf16[9,64,128]{2,1,0:T(8,128)(2,1)S(1)}, u32[]{:S(2)}, u32[]{:S(2)}) collective-permute-start(bf16[9,64,128]{2,1,0:T(8,128)(2,1)S(1)} %pad_maximum_fusion.1.refs_0_), channel_id=1, source_target_pairs={{0,112},{16,0},{32,16},{48,32},{64,48},{80,64},{96,80},{112,96},{1... | collective-permute-start | bytes 442376 | tf_op jit(solution)/shard_map/ppermute | solution.py:413
  78.5 8.0 %collective-permute-start.8 = (bf16[9,64,128]{2,1,0:T(8,128)(2,1)S(1)}, bf16[9,64,128]{2,1,0:T(8,128)(2,1)S(1)}, u32[]{:S(2)}, u32[]{:S(2)}) collective-permute-start(bf16[9,64,128]{2,1,0:T(8,128)(2,1)S(1)} %pad_maximum_fusion.1.refs_0_), channel_id=1, source_target_pairs={{0,96},{16,112},{32,0},{48,16},{64,32},{80,48},{96,64},{112,80},{1... | collective-permute-start | bytes 442376 | tf_op jit(solution)/shard_map/ppermute | solution.py:413
  80.4 7.1 %collective-permute-start.7 = (bf16[9,64,128]{2,1,0:T(8,128)(2,1)S(1)}, bf16[9,64,128]{2,1,0:T(8,128)(2,1)S(1)}, u32[]{:S(2)}, u32[]{:S(2)}) collective-permute-start(bf16[9,64,128]{2,1,0:T(8,128)(2,1)S(1)} %pad_maximum_fusion.1.refs_0_), channel_id=1, source_target_pairs={{0,80},{16,96},{32,112},{48,0},{64,16},{80,32},{96,48},{112,64},{1... | collective-permute-start | bytes 442376 | tf_op jit(solution)/shard_map/ppermute | solution.py:413
  81.0 10.0 %collective-permute-start.6 = (bf16[9,64,128]{2,1,0:T(8,128)(2,1)S(1)}, bf16[9,64,128]{2,1,0:T(8,128)(2,1)S(1)}, u32[]{:S(2)}, u32[]{:S(2)}) collective-permute-start(bf16[9,64,128]{2,1,0:T(8,128)(2,1)S(1)} %pad_maximum_fusion.1.refs_0_), channel_id=1, source_target_pairs={{0,64},{16,80},{32,96},{48,112},{64,0},{80,16},{96,32},{112,48},{1... | collective-permute-start | bytes 442376 | tf_op jit(solution)/shard_map/ppermute | solution.py:413
  83.7 7.7 %collective-permute-start.5 = (bf16[9,64,128]{2,1,0:T(8,128)(2,1)S(1)}, bf16[9,64,128]{2,1,0:T(8,128)(2,1)S(1)}, u32[]{:S(2)}, u32[]{:S(2)}) collective-permute-start(bf16[9,64,128]{2,1,0:T(8,128)(2,1)S(1)} %pad_maximum_fusion.1.refs_0_), channel_id=1, source_target_pairs={{0,48},{16,64},{32,80},{48,96},{64,112},{80,0},{96,16},{112,32},{1... | collective-permute-start | bytes 442376 | tf_op jit(solution)/shard_map/ppermute | solution.py:413
  83.7 13.7 %collective-permute-start.4 = (bf16[9,64,128]{2,1,0:T(8,128)(2,1)S(1)}, bf16[9,64,128]{2,1,0:T(8,128)(2,1)S(1)}, u32[]{:S(2)}, u32[]{:S(2)}) collective-permute-start(bf16[9,64,128]{2,1,0:T(8,128)(2,1)S(1)} %pad_maximum_fusion.1.refs_0_), channel_id=1, source_target_pairs={{0,32},{16,48},{32,64},{48,80},{64,96},{80,112},{96,0},{112,16},{1... | collective-permute-start | bytes 442376 | tf_op jit(solution)/shard_map/ppermute | solution.py:413
  86.5 11.0 %collective-permute-start.3 = (bf16[9,64,128]{2,1,0:T(8,128)(2,1)S(1)}, bf16[9,64,128]{2,1,0:T(8,128)(2,1)S(1)}, u32[]{:S(2)}, u32[]{:S(2)}) collective-permute-start(bf16[9,64,128]{2,1,0:T(8,128)(2,1)S(1)} %pad_maximum_fusion.1.refs_0_), channel_id=1, source_target_pairs={{0,16},{16,32},{32,48},{48,64},{64,80},{80,96},{96,112},{112,0},{1... | collective-permute-start | bytes 442376 | tf_op jit(solution)/shard_map/ppermute | solution.py:413
  141.5 1.3 copy-start.4
  142.9 1.6 copy-start.5
Sparse Core Ops, SparseCore 0:
  23.5 27.3 all-gather.7
  55.0 24.3 all-gather.5
  81.5 59.1 all-gather.9

commit v2 on v1

--- a/solution.py
+++ b/solution.py
@@ -185,12 +185,13 @@
     half = BLK // 2
     for k in range(N_LEAF):
         giver = (leaf + N_LEAF - k) % N_LEAF * BLK
-        for j in range(KS + 1):
-            top = j * BLK <= giver
-            row = jnp.where(top, j * BLK, giver + half) if j < KS else giver + half
-            col = jnp.where(top, giver, j * BLK) if j < KS else giver
+        for n in range(KS + 1):
+            at = (n % 2 * 4 + (front + 4 - n // 2) % 4) * BLK
+            top = at <= giver
+            row = jnp.where(top, at, giver + half) if n < KS else giver + half
+            col = jnp.where(top, giver, at) if n < KS else giver
             rows = pl.ds(pl.multiple_of(row, half), half)
-            s_ref[rows, pl.ds(pl.multiple_of(col, BLK), BLK)] = piece_refs[k][j].astype(F32)
+            s_ref[rows, pl.ds(pl.multiple_of(col, BLK), BLK)] = piece_refs[k][n].astype(F32)
     row_id = lax.broadcasted_iota(jnp.int32, (BLK, BLK), 0)
     col_id = lax.broadcasted_iota(jnp.int32, (BLK, BLK), 1)
     ident = (row_id == col_id).astype(F32)
@@ -254,7 +255,7 @@
             pltpu.VMEM((BLK, BLK), F32),
             pltpu.SemaphoreType.DMA,
         ],
-        compiler_params=pltpu.CompilerParams(vmem_limit_bytes=24 << 20),
+        compiler_params=pltpu.CompilerParams(vmem_limit_bytes=52 << 20),
         cost_estimate=pl.CostEstimate(
             flops=60_000_000_000, bytes_accessed=6 << 20, transcendentals=1024
         ),
@@ -367,7 +368,7 @@
             pltpu.VMEM((N_LEAF, 2, BLK, BLK), BF16),
             pltpu.SemaphoreType.DMA((5, KS)),
         ],
-        compiler_params=pltpu.CompilerParams(vmem_limit_bytes=48 << 20),
+        compiler_params=pltpu.CompilerParams(vmem_limit_bytes=52 << 20),
     )(child_map, low, given, upper, panels, m, cols, rows, front)
 
 
@@ -383,6 +384,27 @@
         for b in range(2)
         for c in range(N_LEAF)
     ]
+
+
+def front_pieces(first, leaf_id, front_id):
+    z, x = front_id // 4, front_id % 4
+    got = [
+        lax.ppermute(first, "front", [(4 * i + j, (i + k) % 4 * 4 + j) for i in (0, 1) for j in range(4)])
+        for k in (1, 2, 3)
+    ]
+    near = jnp.where(z == 0, first, jnp.where(z == 1, got[0], jnp.where(z == 2, got[1], got[2])))
+    far = jnp.where(z == 0, got[2], jnp.where(z == 1, first, jnp.where(z == 2, got[0], got[1])))
+    extra = jnp.where(leaf_id < 4, near[1], far[1])
+    mine = jnp.stack([near[0], far[0], extra])
+    every = [mine] + [
+        lax.ppermute(mine, "front", [(4 * i + j, 4 * i + (j + k) % 4) for i in range(4) for j in range(4)])
+        for k in (1, 2, 3)
+    ]
+    at = (x + 8 - leaf_id) % 4
+    extra = every[0][2]
+    for k in (1, 2, 3):
+        extra = jnp.where(at == k, every[k][2], extra)
+    return jnp.concatenate([one[:2] for one in every] + [extra[None]], axis=0)
 
 
 def one_pass(front_entries, child_panels, child_blocks, child_map):
@@ -402,18 +424,16 @@
     upper = upper.reshape(2, N_LEAF, BLK // 2, own.shape[1])
     lower = jnp.where(early, other, same).reshape(BLK // 2, 4, BLK).transpose(1, 0, 2)
     flat, turned, first = pivot_rows(child_map, front, given, upper, panels)
-    turned = lax.ppermute(turned, MESH_AXES, exchange(0))
-    packed = jnp.concatenate([turned.reshape(ORDER, BLK), lower.reshape(2 * BLK, BLK)], axis=0)
-    pieces = gather(first, "front", N_FRONT)[:KS]
-    packed, pieces = lax.optimization_barrier((packed, pieces))
-    rows = lax.all_gather(packed, "front", axis=0)
-    extra = lax.dynamic_index_in_dim(pieces[:, 1], leaf_id, 0, keepdims=True)
-    whole = jnp.concatenate([pieces[:, 0], extra], axis=0)
+    cols = lax.all_gather(flat, "leaf", axis=0, tiled=True)
+    whole = front_pieces(first, leaf_id, front_id)
     separator = [whole] + [
         lax.ppermute(whole, "leaf", [(i, (i + k) % N_LEAF) for i in range(N_LEAF)])
         for k in range(1, N_LEAF)
     ]
-    cols = lax.all_gather(flat, "leaf", axis=0, tiled=True)
+    turned, whole = lax.optimization_barrier((turned, whole))
+    turned = lax.ppermute(turned, MESH_AXES, exchange(0))
+    packed = jnp.concatenate([turned.reshape(ORDER, BLK), lower.reshape(2 * BLK, BLK)], axis=0)
+    rows = lax.all_gather(packed, "front", axis=0)
     m, low = cholesky(separator)
     rows = rows.reshape(2, KS, ORDER + 2 * BLK, BLK)
     out = schur(child_map, low, given, upper, panels, m, cols, rows, front)

time: 171 us -> 179 us (1.047)
  starting transfers between devices: 24.4 us -> 39.3 us
  waiting for transfers between devices: 29.6 us -> 24.7 us
  local copies, waits for them, and re-layouts: 6.67 us -> 2.07 us
    ppermute x0 -> x6, starting transfers between devices: none -> 12.5 us  [the longest x3 8.06 us: front_pieces(): lax.ppermute(first, 'front', [(4 * i + j, (i + k) % 4 * 4 + j) for i in (...]
    all_to_all x1 -> x0, waiting for transfers between devices: 11 us -> none  [gather(): return lax.all_to_all(spread, axis, 0, 0)]
    ppermute x7, starting transfers between devices: 5.61 us -> 15.9 us  [one_pass(): lax.ppermute(whole, 'leaf', [(i, (i + k) % N_LEAF) for i in range(N_LEAF)])]
    all_to_all x1 -> x0, starting transfers between devices: 7.83 us -> none  [gather(): return lax.all_to_all(spread, axis, 0, 0)]
    ppermute x0 -> x6, waiting for transfers between devices: none -> 6.26 us  [the longest x3 4.43 us: front_pieces(): lax.ppermute(mine, 'front', [(4 * i + j, 4 * i + (j + k) % 4) for i in ra...]
    unnamed x14 -> x12, local copies, waits for them, and re-layouts: 2.92 us -> 0.06 us
  transfers between devices with their start and end apart: 15 -> 20, of which waited for: 9 -> 8; matrix products, arithmetic and copies ran while one was open for 2% -> 1% of each run, Pallas kernels for 26% -> 25%
where the time goes in v2:
time: 179 us; the launch traced here: 178 us
  Pallas kernels  67.8 us (38%)
  starting transfers between devices  39.3 us (22%)
  blocking collectives  28.1 us (16%)
  waiting for transfers between devices  24.7 us (14%)
  between operations  13.4 us (7%)
  other arithmetic  2.45 us (1%)
  local copies, waits for them, and re-layouts  2.07 us (1%)
    pallas_call x1, Pallas kernels, cholesky(): pl.pallas_call(cholesky_kernel, name='cholesky', out_shape=(jax.ShapeDtyp...  45.1 us
    all_to_all x1, blocking collectives, gather(): return lax.all_to_all(spread, axis, 0, 0)  28.1 us
    pallas_call x1, Pallas kernels, schur(): pl.pallas_call(schur_kernel, name='schur', grid=(steps,), out_shape=jax.S...  19.6 us
    ppermute x7, starting transfers between devices, one_pass(): lax.ppermute(whole, 'leaf', [(i, (i + k) % N_LEAF) for i in range(N_LEAF)])  15.9 us
    ppermute x7, waiting for transfers between devices, one_pass(): lax.ppermute(whole, 'leaf', [(i, (i + k) % N_LEAF) for i in range(N_LEAF)])  13.6 us
    ppermute x3, starting transfers between devices, front_pieces(): lax.ppermute(first, 'front', [(4 * i + j, (i + k) % 4 * 4 + j) for i in (...  8.06 us
    all_to_all x1, starting transfers between devices, one_pass(): given = lax.all_to_all(blocks, 'leaf', 0, 0)  4.58 us
    ppermute x3, starting transfers between devices, front_pieces(): lax.ppermute(mine, 'front', [(4 * i + j, 4 * i + (j + k) % 4) for i in ra...  4.47 us
  transfers between devices with their start and end apart: 20, of which 8 were waited for; matrix products, arithmetic and copies ran while one was open for 1% of the time, Pallas kernels for 25%

profile of v2, /device:TPU:0, one launch (start us, length us, event | category | flops | bytes accessed | tf_op | source)
XLA Modules:
  0.0 177.9 jit_solution(8701135541737430132)
XLA Ops:
  6.5 1.9 %copy.11 = bf16[2,8,128,128]{3,2,0,1:T(8,128)(2,1)} copy(bf16[2,8,128,128]{3,2,1,0:T(8,128)(2,1)} %bitcast.26) | data formatting | bytes 1048576 | tf_op jit(solution)/shard_map/reshape;squeeze | solution.py:419
  8.4 4.6 %all-to-all-start = ((bf16[8,2,128,128]{3,2,1,0:T(8,128)(2,1)}), bf16[8,2,128,128]{3,2,1,0:T(8,128)(2,1)S(1)}, u32[]{:S(2)}, u32[]{:S(2)}) async-start(bf16[8,2,128,128]{3,2,1,0:T(8,128)(2,1)} %bitcast.18), calls=%async_computation | async-start | bytes 1048576 | tf_op jit(solution)/shard_map/all_to_all | solution.py:420
  13.0 0.0 all-gather.8.cloned.1.call-start
  13.1 0.9 select_bitcast_fusion
  13.9 4.0 %collective-permute-start.1 = (bf16[64,512]{1,0:T(8,128)(2,1)S(1)}, bf16[64,512]{1,0:T(8,128)(2,1)S(1)}, u32[]{:S(2)}, u32[]{:S(2)}) collective-permute-start(bf16[64,512]{1,0:T(8,128)(2,1)S(1)} %get-tuple-element.29), channel_id=1, source_target_pairs={{0,8},{1,24},{2,40},{3,56},{4,72},{5,88},{6,104},{7,120},{8,0},{9,... | collective-permute-start | bytes 196616 | tf_op jit(solution)/shard_map/ppermute | solution.py:418
  17.9 0.7 collective-permute-start
  18.6 1.6 collective-permute-done.1
  20.1 0.0 collective-permute-done
  20.1 3.2 %all-to-all-done.given_ref = bf16[8,2,128,128]{3,2,1,0:T(8,128)(2,1)S(1)} async-done(((bf16[8,2,128,128]{3,2,1,0:T(8,128)(2,1)}), bf16[8,2,128,128]{3,2,1,0:T(8,128)(2,1)S(1)}, u32[]{:S(2)}, u32[]{:S(2)}) %all-to-all-start) | async-done | bytes 524320 | tf_op jit(solution)/shard_map/all_to_all | solution.py:420
  23.3 0.0 copy-start.1
  23.3 0.0 all-gather.8.cloned.1.call-update
  23.3 0.0 all-gather.6.cloned.1.call-start
  23.4 0.1 broadcast_in_dim.2
  23.5 28.1 %all_to_all.10 = bf16[16,64,512]{2,1,0:T(8,128)(2,1)} all-to-all(bf16[16,64,512]{2,1,0:T(8,128)(2,1)S(1)} %broadcast_in_dim.2), channel_id=1, replica_groups=mesh['leaf'=8,'front'=16] {'front'}, dimensions={0} | all-to-all | bytes 2097152 | tf_op jit(solution)/shard_map/all_to_all | solution.py:377
  51.7 0.0 all-gather.8.cloned.1.call-done
  51.7 0.0 copy-done.1
  51.7 3.1 %pivot_rows.1 = (bf16[128,1024]{1,0:T(8,128)(2,1)}, bf16[8,128,128]{2,1,0:T(8,128)(2,1)}, bf16[2,64,128]{2,1,0:T(8,128)(2,1)}) custom-call(s32[8,16]{1,0:T(8,128)} %map_ref.3, f32[16384,128]{1,0:T(8,128)} %bitcast.21, bf16[8,2,128,128]{3,2,1,0:T(8,128)(2,1)} %copy-done.1, bf16[2,8,64,512]{3,2,1,0:T(8,128)(2,1)} %bitcast.19, bf16[8,128,512]{2,1,0:T(8,128)(2,1)} %bitcast.24), custom_call_target="tpu_custom_call" | custom-call | tf_op jit(solution)/shard_map/pivot_rows/pallas_call | solution.py:66
  54.8 0.0 all-gather.6.cloned.1.call-update
  54.8 0.0 all-gather.10.cloned.1.call-start
  54.9 4.0 %collective-permute-start.4 = (bf16[2,64,128]{2,1,0:T(8,128)(2,1)}, bf16[2,64,128]{2,1,0:T(8,128)(2,1)S(1)}, u32[]{:S(2)}, u32[]{:S(2)}) collective-permute-start(bf16[2,64,128]{2,1,0:T(8,128)(2,1)} %get-tuple-element.19), channel_id=1, source_target_pairs={{0,12},{1,13},{2,14},{3,15},{4,0},{5,1},{6,2},{7,3},{16,28},{17,29... | collective-permute-start | bytes 98312 | tf_op jit(solution)/shard_map/ppermute | solution.py:392
  58.9 1.3 collective-permute-start.3
  60.2 2.8 %collective-permute-start.2 = (bf16[2,64,128]{2,1,0:T(8,128)(2,1)}, bf16[2,64,128]{2,1,0:T(8,128)(2,1)S(1)}, u32[]{:S(2)}, u32[]{:S(2)}) collective-permute-start(bf16[2,64,128]{2,1,0:T(8,128)(2,1)} %get-tuple-element.19), channel_id=1, source_target_pairs={{0,4},{1,5},{2,6},{3,7},{4,8},{5,9},{6,10},{7,11},{16,20},{17,21},... | collective-permute-start | bytes 98312 | tf_op jit(solution)/shard_map/ppermute | solution.py:392
  63.0 0.0 collective-permute-done.4
  63.0 0.0 collective-permute-done.3
  63.0 1.8 %collective-permute-done.2 = bf16[2,64,128]{2,1,0:T(8,128)(2,1)S(1)} collective-permute-done((bf16[2,64,128]{2,1,0:T(8,128)(2,1)}, bf16[2,64,128]{2,1,0:T(8,128)(2,1)S(1)}, u32[]{:S(2)}, u32[]{:S(2)}) %collective-permute-start.2) | collective-permute-done | bytes 32800 | tf_op jit(solution)/shard_map/ppermute | solution.py:392
  64.9 0.8 select_select_fusion
  65.7 2.8 %collective-permute-start.7 = (bf16[3,64,128]{2,1,0:T(8,128)(2,1)S(1)}, bf16[3,64,128]{2,1,0:T(8,128)(2,1)S(1)}, u32[]{:S(2)}, u32[]{:S(2)}) collective-permute-start(bf16[3,64,128]{2,1,0:T(8,128)(2,1)S(1)} %pad_maximum_fusion.1), channel_id=1, source_target_pairs={{0,3},{1,0},{2,1},{3,2},{4,7},{5,4},{6,5},{7,6},{8,11},{9,8},{10,9... | collective-permute-start | bytes 147464 | tf_op jit(solution)/shard_map/ppermute | solution.py:400
  68.4 0.8 collective-permute-start.6
  69.3 0.9 collective-permute-start.5
  70.1 4.4 %collective-permute-done.5 = bf16[3,64,128]{2,1,0:T(8,128)(2,1)S(1)} collective-permute-done((bf16[3,64,128]{2,1,0:T(8,128)(2,1)S(1)}, bf16[3,64,128]{2,1,0:T(8,128)(2,1)S(1)}, u32[]{:S(2)}, u32[]{:S(2)}) %collective-permute-start.5) | collective-permute-done | bytes 49184 | tf_op jit(solution)/shard_map/ppermute | solution.py:400
  74.6 0.0 collective-permute-done.6
  74.6 0.0 collective-permute-done.7
  74.7 1.6 collective-permute-start.15
  76.3 0.0 collective-permute-done.15
  76.3 0.7 pad_maximum_fusion
  77.0 0.0 all-gather.10.cloned.1.call-update
  77.1 0.0 copy-start
  77.1 0.0 copy-start.2
  77.1 0.0 copy-start.3
  77.1 9.4 %collective-permute-start.14 = (bf16[9,64,128]{2,1,0:T(8,128)(2,1)S(1)}, bf16[9,64,128]{2,1,0:T(8,128)(2,1)S(1)}, u32[]{:S(2)}, u32[]{:S(2)}) collective-permute-start(bf16[9,64,128]{2,1,0:T(8,128)(2,1)S(1)} %fusion.2.refs_0_), channel_id=1, source_target_pairs={{0,112},{16,0},{32,16},{48,32},{64,48},{80,64},{96,80},{112,96},{1... | collective-permute-start | bytes 442376 | tf_op jit(solution)/shard_map/ppermute | solution.py:430
  86.5 3.2 %collective-permute-start.13 = (bf16[9,64,128]{2,1,0:T(8,128)(2,1)S(1)}, bf16[9,64,128]{2,1,0:T(8,128)(2,1)S(1)}, u32[]{:S(2)}, u32[]{:S(2)}) collective-permute-start(bf16[9,64,128]{2,1,0:T(8,128)(2,1)S(1)} %fusion.2.refs_0_), channel_id=1, source_target_pairs={{0,96},{16,112},{32,0},{48,16},{64,32},{80,48},{96,64},{112,80},{1... | collective-permute-start | bytes 442376 | tf_op jit(solution)/shard_map/ppermute | solution.py:430
  89.7 0.0 collective-permute-start.12
  89.7 3.3 %collective-permute-start.11 = (bf16[9,64,128]{2,1,0:T(8,128)(2,1)S(1)}, bf16[9,64,128]{2,1,0:T(8,128)(2,1)S(1)}, u32[]{:S(2)}, u32[]{:S(2)}) collective-permute-start(bf16[9,64,128]{2,1,0:T(8,128)(2,1)S(1)} %fusion.2.refs_0_), channel_id=1, source_target_pairs={{0,64},{16,80},{32,96},{48,112},{64,0},{80,16},{96,32},{112,48},{1... | collective-permute-start | bytes 442376 | tf_op jit(solution)/shard_map/ppermute | solution.py:430
  93.0 0.0 collective-permute-start.10
  93.0 0.0 collective-permute-done.14.refs_7_
  93.0 0.0 collective-permute-start.9
  93.0 7.1 %collective-permute-done.13.refs_6_ = bf16[9,64,128]{2,1,0:T(8,128)(2,1)S(1)} collective-permute-done((bf16[9,64,128]{2,1,0:T(8,128)(2,1)S(1)}, bf16[9,64,128]{2,1,0:T(8,128)(2,1)S(1)}, u32[]{:S(2)}, u32[]{:S(2)}) %collective-permute-start.13) | collective-permute-done | bytes 147488 | tf_op jit(solution)/shard_map/ppermute | solution.py:430
  100.1 0.0 collective-permute-start.8
  100.1 0.0 collective-permute-done.12.refs_5_
  100.1 0.0 collective-permute-done.11.refs_4_
  100.1 0.5 collective-permute-done.10.refs_3_
  100.6 5.2 %collective-permute-done.9.refs_2_ = bf16[9,64,128]{2,1,0:T(8,128)(2,1)S(1)} collective-permute-done((bf16[9,64,128]{2,1,0:T(8,128)(2,1)S(1)}, bf16[9,64,128]{2,1,0:T(8,128)(2,1)S(1)}, u32[]{:S(2)}, u32[]{:S(2)}) %collective-permute-start.9) | collective-permute-done | bytes 147488 | tf_op jit(solution)/shard_map/ppermute | solution.py:430
  105.8 0.8 collective-permute-done.8.refs_1_
  106.6 45.1 %cholesky.1 = (bf16[1024,1024]{1,0:T(8,128)(2,1)}, f32[128,128]{1,0:T(8,128)S(1)}) custom-call(bf16[9,64,128]{2,1,0:T(8,128)(2,1)S(1)} %fusion.2.refs_0_, bf16[9,64,128]{2,1,0:T(8,128)(2,1)S(1)} %collective-permute-done.8.refs_1_, bf16[9,64,128]{2,1,0:T(8,128)(2,1)S(1)} %collective-permute-done.9.refs_2_, ...), custom_call_target="tpu_custom_call" | custom-call | flops 60000002048 | bytes 6291456 | tf_op jit(solution)/shard_map/cholesky/pallas_call | solution.py:238
  151.7 0.0 all-gather.6.cloned.1.call-done.cols_hbm
  151.7 0.0 all-gather.10.cloned.1.call-done
  151.8 0.0 copy-done
  151.8 0.0 copy-done.2
  151.8 0.0 copy-done.3
  151.8 19.6 %schur.1 = f32[16384,128]{1,0:T(8,128)} custom-call(s32[8,16]{1,0:T(8,128)S(1)} %copy-done.3, f32[128,128]{1,0:T(8,128)S(1)} %get-tuple-element.20.l_ref, bf16[8,2,128,128]{3,2,1,0:T(8,128)(2,1)S(1)} %copy-done.2, bf16[2,8,64,512]{3,2,1,0:T(8,128)(2,1)S(1)} %bitcast.20, bf16[8,128,512]{2,1,0:T(8,128)(2,1)} %bitcast.25, ...), custom_call_target="tpu_custom_call" | custom-call | tf_op jit(solution)/shard_map/schur/pallas_call | solution.py:354
  (10 shorter events, 0.1 us)
Async XLA Ops:
  8.4 14.9 %all-to-all-start = ((bf16[8,2,128,128]{3,2,1,0:T(8,128)(2,1)}), bf16[8,2,128,128]{3,2,1,0:T(8,128)(2,1)S(1)}, u32[]{:S(2)}, u32[]{:S(2)}) async-start(bf16[8,2,128,128]{3,2,1,0:T(8,128)(2,1)} %bitcast.18), calls=%async_computation | async-start | bytes 1048576 | tf_op jit(solution)/shard_map/all_to_all | solution.py:420
  13.0 38.7 %all-gather.8.cloned.1.call-start = ((), (), s32[]{:S(2)}) async-start(), calls=%async_computation.3 | async-start | bytes 1179648 | tf_op jit(solution)/shard_map/all_gather | solution.py:422
  13.9 6.2 %collective-permute-start.1 = (bf16[64,512]{1,0:T(8,128)(2,1)S(1)}, bf16[64,512]{1,0:T(8,128)(2,1)S(1)}, u32[]{:S(2)}, u32[]{:S(2)}) collective-permute-start(bf16[64,512]{1,0:T(8,128)(2,1)S(1)} %get-tuple-element.29), channel_id=1, source_target_pairs={{0,8},{1,24},{2,40},{3,56},{4,72},{5,88},{6,104},{7,120},{8,0},{9,... | collective-permute-start | bytes 196616 | tf_op jit(solution)/shard_map/ppermute | solution.py:418
  17.9 2.2 %collective-permute-start = (bf16[64,512]{1,0:T(8,128)(2,1)S(1)}, bf16[64,512]{1,0:T(8,128)(2,1)S(1)}, u32[]{:S(2)}, u32[]{:S(2)}) collective-permute-start(bf16[64,512]{1,0:T(8,128)(2,1)S(1)} %get-tuple-element.30), channel_id=1, source_target_pairs={{0,0},{1,16},{2,32},{3,48},{4,64},{5,80},{6,96},{7,112},{8,8},{9,2... | collective-permute-start | bytes 196616 | tf_op jit(solution)/shard_map/ppermute | solution.py:417
  23.3 28.4 %copy-start.1 = (bf16[8,2,128,128]{3,2,1,0:T(8,128)(2,1)}, bf16[8,2,128,128]{3,2,1,0:T(8,128)(2,1)S(1)}, u32[]{:S(2)}) copy-start(bf16[8,2,128,128]{3,2,1,0:T(8,128)(2,1)S(1)} %all-to-all-done.given_ref) | copy-start | bytes 1572868
  23.3 128.4 %all-gather.6.cloned.1.call-start = ((), (), s32[]{:S(2)}) async-start(), calls=%async_computation.2 | async-start | bytes 2359296 | tf_op jit(solution)/shard_map/all_gather | solution.py:427
  54.8 96.9 %all-gather.10.cloned.1.call-start = ((), (), s32[]{:S(2)}) async-start(), calls=%async_computation.4 | async-start | bytes 5570560 | tf_op jit(solution)/shard_map/all_gather | solution.py:436
  54.9 8.1 %collective-permute-start.4 = (bf16[2,64,128]{2,1,0:T(8,128)(2,1)}, bf16[2,64,128]{2,1,0:T(8,128)(2,1)S(1)}, u32[]{:S(2)}, u32[]{:S(2)}) collective-permute-start(bf16[2,64,128]{2,1,0:T(8,128)(2,1)} %get-tuple-element.19), channel_id=1, source_target_pairs={{0,12},{1,13},{2,14},{3,15},{4,0},{5,1},{6,2},{7,3},{16,28},{17,29... | collective-permute-start | bytes 98312 | tf_op jit(solution)/shard_map/ppermute | solution.py:392
  58.9 4.1 %collective-permute-start.3 = (bf16[2,64,128]{2,1,0:T(8,128)(2,1)}, bf16[2,64,128]{2,1,0:T(8,128)(2,1)S(1)}, u32[]{:S(2)}, u32[]{:S(2)}) collective-permute-start(bf16[2,64,128]{2,1,0:T(8,128)(2,1)} %get-tuple-element.19), channel_id=1, source_target_pairs={{0,8},{1,9},{2,10},{3,11},{4,12},{5,13},{6,14},{7,15},{16,24},{17,... | collective-permute-start | bytes 98312 | tf_op jit(solution)/shard_map/ppermute | solution.py:392
  60.2 4.7 %collective-permute-start.2 = (bf16[2,64,128]{2,1,0:T(8,128)(2,1)}, bf16[2,64,128]{2,1,0:T(8,128)(2,1)S(1)}, u32[]{:S(2)}, u32[]{:S(2)}) collective-permute-start(bf16[2,64,128]{2,1,0:T(8,128)(2,1)} %get-tuple-element.19), channel_id=1, source_target_pairs={{0,4},{1,5},{2,6},{3,7},{4,8},{5,9},{6,10},{7,11},{16,20},{17,21},... | collective-permute-start | bytes 98312 | tf_op jit(solution)/shard_map/ppermute | solution.py:392
  65.7 8.9 %collective-permute-start.7 = (bf16[3,64,128]{2,1,0:T(8,128)(2,1)S(1)}, bf16[3,64,128]{2,1,0:T(8,128)(2,1)S(1)}, u32[]{:S(2)}, u32[]{:S(2)}) collective-permute-start(bf16[3,64,128]{2,1,0:T(8,128)(2,1)S(1)} %pad_maximum_fusion.1), channel_id=1, source_target_pairs={{0,3},{1,0},{2,1},{3,2},{4,7},{5,4},{6,5},{7,6},{8,11},{9,8},{10,9... | collective-permute-start | bytes 147464 | tf_op jit(solution)/shard_map/ppermute | solution.py:400
  68.4 6.2 %collective-permute-start.6 = (bf16[3,64,128]{2,1,0:T(8,128)(2,1)S(1)}, bf16[3,64,128]{2,1,0:T(8,128)(2,1)S(1)}, u32[]{:S(2)}, u32[]{:S(2)}) collective-permute-start(bf16[3,64,128]{2,1,0:T(8,128)(2,1)S(1)} %pad_maximum_fusion.1), channel_id=1, source_target_pairs={{0,2},{1,3},{2,0},{3,1},{4,6},{5,7},{6,4},{7,5},{8,10},{9,11},{10,... | collective-permute-start | bytes 147464 | tf_op jit(solution)/shard_map/ppermute | solution.py:400
  69.3 5.3 %collective-permute-start.5 = (bf16[3,64,128]{2,1,0:T(8,128)(2,1)S(1)}, bf16[3,64,128]{2,1,0:T(8,128)(2,1)S(1)}, u32[]{:S(2)}, u32[]{:S(2)}) collective-permute-start(bf16[3,64,128]{2,1,0:T(8,128)(2,1)S(1)} %pad_maximum_fusion.1), channel_id=1, source_target_pairs={{0,1},{1,2},{2,3},{3,0},{4,5},{5,6},{6,7},{7,4},{8,9},{9,10},{10,1... | collective-permute-start | bytes 147464 | tf_op jit(solution)/shard_map/ppermute | solution.py:400
  74.7 1.7 collective-permute-start.15
  77.1 74.7 %copy-start = (bf16[16,64,512]{2,1,0:T(8,128)(2,1)S(1)}, bf16[16,64,512]{2,1,0:T(8,128)(2,1)}, u32[]{:S(2)}) copy-start(bf16[16,64,512]{2,1,0:T(8,128)(2,1)} %all_to_all.10) | copy-start | bytes 3145732
  77.1 74.7 %copy-start.2 = (bf16[8,2,128,128]{3,2,1,0:T(8,128)(2,1)S(1)}, bf16[8,2,128,128]{3,2,1,0:T(8,128)(2,1)}, u32[]{:S(2)}) copy-start(bf16[8,2,128,128]{3,2,1,0:T(8,128)(2,1)} %copy-done.1) | copy-start | bytes 1572868
  77.1 74.7 %copy-start.3 = (s32[8,16]{1,0:T(8,128)S(1)}, s32[8,16]{1,0:T(8,128)}, u32[]{:S(2)}) copy-start(s32[8,16]{1,0:T(8,128)} %map_ref.3) | copy-start | bytes 1540
  77.1 15.9 %collective-permute-start.14 = (bf16[9,64,128]{2,1,0:T(8,128)(2,1)S(1)}, bf16[9,64,128]{2,1,0:T(8,128)(2,1)S(1)}, u32[]{:S(2)}, u32[]{:S(2)}) collective-permute-start(bf16[9,64,128]{2,1,0:T(8,128)(2,1)S(1)} %fusion.2.refs_0_), channel_id=1, source_target_pairs={{0,112},{16,0},{32,16},{48,32},{64,48},{80,64},{96,80},{112,96},{1... | collective-permute-start | bytes 442376 | tf_op jit(solution)/shard_map/ppermute | solution.py:430
  86.5 13.6 %collective-permute-start.13 = (bf16[9,64,128]{2,1,0:T(8,128)(2,1)S(1)}, bf16[9,64,128]{2,1,0:T(8,128)(2,1)S(1)}, u32[]{:S(2)}, u32[]{:S(2)}) collective-permute-start(bf16[9,64,128]{2,1,0:T(8,128)(2,1)S(1)} %fusion.2.refs_0_), channel_id=1, source_target_pairs={{0,96},{16,112},{32,0},{48,16},{64,32},{80,48},{96,64},{112,80},{1... | collective-permute-start | bytes 442376 | tf_op jit(solution)/shard_map/ppermute | solution.py:430
  89.7 10.4 %collective-permute-start.12 = (bf16[9,64,128]{2,1,0:T(8,128)(2,1)S(1)}, bf16[9,64,128]{2,1,0:T(8,128)(2,1)S(1)}, u32[]{:S(2)}, u32[]{:S(2)}) collective-permute-start(bf16[9,64,128]{2,1,0:T(8,128)(2,1)S(1)} %fusion.2.refs_0_), channel_id=1, source_target_pairs={{0,80},{16,96},{32,112},{48,0},{64,16},{80,32},{96,48},{112,64},{1... | collective-permute-start | bytes 442376 | tf_op jit(solution)/shard_map/ppermute | solution.py:430
  89.7 10.4 %collective-permute-start.11 = (bf16[9,64,128]{2,1,0:T(8,128)(2,1)S(1)}, bf16[9,64,128]{2,1,0:T(8,128)(2,1)S(1)}, u32[]{:S(2)}, u32[]{:S(2)}) collective-permute-start(bf16[9,64,128]{2,1,0:T(8,128)(2,1)S(1)} %fusion.2.refs_0_), channel_id=1, source_target_pairs={{0,64},{16,80},{32,96},{48,112},{64,0},{80,16},{96,32},{112,48},{1... | collective-permute-start | bytes 442376 | tf_op jit(solution)/shard_map/ppermute | solution.py:430
  93.0 7.6 %collective-permute-start.10 = (bf16[9,64,128]{2,1,0:T(8,128)(2,1)S(1)}, bf16[9,64,128]{2,1,0:T(8,128)(2,1)S(1)}, u32[]{:S(2)}, u32[]{:S(2)}) collective-permute-start(bf16[9,64,128]{2,1,0:T(8,128)(2,1)S(1)} %fusion.2.refs_0_), channel_id=1, source_target_pairs={{0,48},{16,64},{32,80},{48,96},{64,112},{80,0},{96,16},{112,32},{1... | collective-permute-start | bytes 442376 | tf_op jit(solution)/shard_map/ppermute | solution.py:430
  93.0 12.8 %collective-permute-start.9 = (bf16[9,64,128]{2,1,0:T(8,128)(2,1)S(1)}, bf16[9,64,128]{2,1,0:T(8,128)(2,1)S(1)}, u32[]{:S(2)}, u32[]{:S(2)}) collective-permute-start(bf16[9,64,128]{2,1,0:T(8,128)(2,1)S(1)} %fusion.2.refs_0_), channel_id=1, source_target_pairs={{0,32},{16,48},{32,64},{48,80},{64,96},{80,112},{96,0},{112,16},{1... | collective-permute-start | bytes 442376 | tf_op jit(solution)/shard_map/ppermute | solution.py:430
  100.1 6.5 %collective-permute-start.8 = (bf16[9,64,128]{2,1,0:T(8,128)(2,1)S(1)}, bf16[9,64,128]{2,1,0:T(8,128)(2,1)S(1)}, u32[]{:S(2)}, u32[]{:S(2)}) collective-permute-start(bf16[9,64,128]{2,1,0:T(8,128)(2,1)S(1)} %fusion.2.refs_0_), channel_id=1, source_target_pairs={{0,16},{16,32},{32,48},{48,64},{64,80},{80,96},{96,112},{112,0},{1... | collective-permute-start | bytes 442376 | tf_op jit(solution)/shard_map/ppermute | solution.py:430
Sparse Core Ops, SparseCore 0:
  23.5 27.3 all-gather.7
  55.0 24.4 all-gather.5
  81.6 61.6 all-gather.9

commit v3 on v2

--- a/solution.py
+++ b/solution.py
@@ -126,7 +126,12 @@
             after = g_ref[below, :]
             v = [lanes(after, 8 * p + j) for j in range(8)]
         for j in range(8):
-            inv = lax.rsqrt(a[j][j])
+            if j % 2 == 0:
+                corner = a[j + 1][j + 1] * a[j][j] - a[j + 1][j] * a[j + 1][j]
+                inv = lax.rsqrt(a[j][j])
+                second = lax.rsqrt(corner) * (a[j][j] * inv)
+            else:
+                inv = second
             r[j] = r[j] * inv
             e[j] = e[j] * inv
             if more:
@@ -136,7 +141,8 @@
                 col[i] = a[i][j] * inv
             for i in range(j + 1, 8):
                 for k in range(j + 1, i + 1):
-                    a[i][k] = a[i][k] - col[i] * col[k]
+                    if j % 2 or i > j + 1:
+                        a[i][k] = a[i][k] - col[i] * col[k]
             for i in range(j + 1, 8):
                 r[i] = r[i] - col[i] * r[j]
                 e[i] = e[i] - col[i] * e[j]
@@ -425,13 +431,13 @@
     lower = jnp.where(early, other, same).reshape(BLK // 2, 4, BLK).transpose(1, 0, 2)
     flat, turned, first = pivot_rows(child_map, front, given, upper, panels)
     cols = lax.all_gather(flat, "leaf", axis=0, tiled=True)
+    turned = lax.ppermute(turned, MESH_AXES, exchange(0))
     whole = front_pieces(first, leaf_id, front_id)
+    turned, whole = lax.optimization_barrier((turned, whole))
     separator = [whole] + [
         lax.ppermute(whole, "leaf", [(i, (i + k) % N_LEAF) for i in range(N_LEAF)])
         for k in range(1, N_LEAF)
     ]
-    turned, whole = lax.optimization_barrier((turned, whole))
-    turned = lax.ppermute(turned, MESH_AXES, exchange(0))
     packed = jnp.concatenate([turned.reshape(ORDER, BLK), lower.reshape(2 * BLK, BLK)], axis=0)
     rows = lax.all_gather(packed, "front", axis=0)
     m, low = cholesky(separator)

time: 179 us -> 174 us (0.972)
  starting transfers between devices: 39.3 us -> 33.2 us
  waiting for transfers between devices: 24.7 us -> 26.9 us
    ppermute x7, starting transfers between devices: 15.9 us -> 9.62 us  [one_pass(): lax.ppermute(whole, 'leaf', [(i, (i + k) % N_LEAF) for i in range(N_LEAF)])]
    all_gather x1, waiting for transfers between devices: 0.02 us -> 2.66 us  [one_pass(): rows = lax.all_gather(packed, 'front', axis=0)]
    ppermute x3, waiting for transfers between devices: 4.43 us -> 6.86 us  [front_pieces(): lax.ppermute(mine, 'front', [(4 * i + j, 4 * i + (j + k) % 4) for i in ra...]
  transfers between devices with their start and end apart: 20 -> 20, of which waited for: 8 -> 9; matrix products, arithmetic and copies ran while one was open for 1% -> 2% of each run, Pallas kernels for 25% -> 25%
where the time goes in v3:
time: 174 us; the launch traced here: 173 us
  Pallas kernels  66.7 us (38%)
  starting transfers between devices  33.2 us (19%)
  blocking collectives  28.1 us (16%)
  waiting for transfers between devices  26.9 us (15%)
  between operations  13.4 us (8%)
  other arithmetic  2.45 us (1%)
  local copies, waits for them, and re-layouts  2.07 us (1%)
    pallas_call x1, Pallas kernels, cholesky(): pl.pallas_call(cholesky_kernel, name='cholesky', out_shape=(jax.ShapeDtyp...  44 us
    all_to_all x1, blocking collectives, gather(): return lax.all_to_all(spread, axis, 0, 0)  28.1 us
    pallas_call x1, Pallas kernels, schur(): pl.pallas_call(schur_kernel, name='schur', grid=(steps,), out_shape=jax.S...  19.6 us
    ppermute x7, waiting for transfers between devices, one_pass(): lax.ppermute(whole, 'leaf', [(i, (i + k) % N_LEAF) for i in range(N_LEAF)])  12.3 us
    ppermute x7, starting transfers between devices, one_pass(): lax.ppermute(whole, 'leaf', [(i, (i + k) % N_LEAF) for i in range(N_LEAF)])  9.62 us
    ppermute x3, starting transfers between devices, front_pieces(): lax.ppermute(first, 'front', [(4 * i + j, (i + k) % 4 * 4 + j) for i in (...  8.06 us
    ppermute x3, waiting for transfers between devices, front_pieces(): lax.ppermute(mine, 'front', [(4 * i + j, 4 * i + (j + k) % 4) for i in ra...  6.86 us
    ppermute x3, starting transfers between devices, front_pieces(): lax.ppermute(mine, 'front', [(4 * i + j, 4 * i + (j + k) % 4) for i in ra...  4.64 us
  transfers between devices with their start and end apart: 20, of which 9 were waited for; matrix products, arithmetic and copies ran while one was open for 2% of the time, Pallas kernels for 25%

profile of v3, /device:TPU:0, one launch (start us, length us, event | category | flops | bytes accessed | tf_op | source)
XLA Modules:
  0.0 172.8 jit_solution(3859314184956931354)
XLA Ops:
  6.5 1.9 %copy.11 = bf16[2,8,128,128]{3,2,0,1:T(8,128)(2,1)} copy(bf16[2,8,128,128]{3,2,1,0:T(8,128)(2,1)} %bitcast.26) | data formatting | bytes 1048576 | tf_op jit(solution)/shard_map/reshape;squeeze | solution.py:425
  8.4 4.6 %all-to-all-start = ((bf16[8,2,128,128]{3,2,1,0:T(8,128)(2,1)}), bf16[8,2,128,128]{3,2,1,0:T(8,128)(2,1)S(1)}, u32[]{:S(2)}, u32[]{:S(2)}) async-start(bf16[8,2,128,128]{3,2,1,0:T(8,128)(2,1)} %bitcast.18), calls=%async_computation | async-start | bytes 1048576 | tf_op jit(solution)/shard_map/all_to_all | solution.py:426
  13.0 0.0 all-gather.8.cloned.1.call-start
  13.1 0.9 select_bitcast_fusion
  13.9 4.0 %collective-permute-start.1 = (bf16[64,512]{1,0:T(8,128)(2,1)S(1)}, bf16[64,512]{1,0:T(8,128)(2,1)S(1)}, u32[]{:S(2)}, u32[]{:S(2)}) collective-permute-start(bf16[64,512]{1,0:T(8,128)(2,1)S(1)} %get-tuple-element.31), channel_id=1, source_target_pairs={{0,8},{1,24},{2,40},{3,56},{4,72},{5,88},{6,104},{7,120},{8,0},{9,... | collective-permute-start | bytes 196616 | tf_op jit(solution)/shard_map/ppermute | solution.py:424
  17.9 0.7 collective-permute-start
  18.6 1.6 collective-permute-done.1
  20.1 0.0 collective-permute-done
  20.1 3.2 %all-to-all-done.given_ref = bf16[8,2,128,128]{3,2,1,0:T(8,128)(2,1)S(1)} async-done(((bf16[8,2,128,128]{3,2,1,0:T(8,128)(2,1)}), bf16[8,2,128,128]{3,2,1,0:T(8,128)(2,1)S(1)}, u32[]{:S(2)}, u32[]{:S(2)}) %all-to-all-start) | async-done | bytes 524320 | tf_op jit(solution)/shard_map/all_to_all | solution.py:426
  23.3 0.0 copy-start.1
  23.3 0.0 all-gather.8.cloned.1.call-update
  23.3 0.0 all-gather.6.cloned.1.call-start
  23.4 0.1 broadcast_in_dim.2
  23.5 28.1 %all_to_all.10 = bf16[16,64,512]{2,1,0:T(8,128)(2,1)} all-to-all(bf16[16,64,512]{2,1,0:T(8,128)(2,1)S(1)} %broadcast_in_dim.2), channel_id=1, replica_groups=mesh['leaf'=8,'front'=16] {'front'}, dimensions={0} | all-to-all | bytes 2097152 | tf_op jit(solution)/shard_map/all_to_all | solution.py:383
  51.7 0.0 all-gather.8.cloned.1.call-done
  51.7 0.0 copy-done.1
  51.7 3.1 %pivot_rows.1 = (bf16[128,1024]{1,0:T(8,128)(2,1)}, bf16[8,128,128]{2,1,0:T(8,128)(2,1)}, bf16[2,64,128]{2,1,0:T(8,128)(2,1)}) custom-call(s32[8,16]{1,0:T(8,128)} %map_ref.3, f32[16384,128]{1,0:T(8,128)} %bitcast.21, bf16[8,2,128,128]{3,2,1,0:T(8,128)(2,1)} %copy-done.1, bf16[2,8,64,512]{3,2,1,0:T(8,128)(2,1)} %bitcast.19, bf16[8,128,512]{2,1,0:T(8,128)(2,1)} %bitcast.24), custom_call_target="tpu_custom_call" | custom-call | tf_op jit(solution)/shard_map/pivot_rows/pallas_call | solution.py:66
  54.8 0.0 all-gather.6.cloned.1.call-update
  54.8 0.0 all-gather.10.cloned.1.call-start
  54.9 4.0 %collective-permute-start.5 = (bf16[2,64,128]{2,1,0:T(8,128)(2,1)}, bf16[2,64,128]{2,1,0:T(8,128)(2,1)S(1)}, u32[]{:S(2)}, u32[]{:S(2)}) collective-permute-start(bf16[2,64,128]{2,1,0:T(8,128)(2,1)} %get-tuple-element.21), channel_id=1, source_target_pairs={{0,12},{1,13},{2,14},{3,15},{4,0},{5,1},{6,2},{7,3},{16,28},{17,29... | collective-permute-start | bytes 98312 | tf_op jit(solution)/shard_map/ppermute | solution.py:398
  58.9 1.3 collective-permute-start.4
  60.2 2.8 %collective-permute-start.3 = (bf16[2,64,128]{2,1,0:T(8,128)(2,1)}, bf16[2,64,128]{2,1,0:T(8,128)(2,1)S(1)}, u32[]{:S(2)}, u32[]{:S(2)}) collective-permute-start(bf16[2,64,128]{2,1,0:T(8,128)(2,1)} %get-tuple-element.21), channel_id=1, source_target_pairs={{0,4},{1,5},{2,6},{3,7},{4,8},{5,9},{6,10},{7,11},{16,20},{17,21},... | collective-permute-start | bytes 98312 | tf_op jit(solution)/shard_map/ppermute | solution.py:398
  63.1 1.6 collective-permute-start.2
  64.7 0.0 collective-permute-done.5
  64.7 0.0 collective-permute-done.4
  64.7 0.2 collective-permute-done.3
  64.9 0.8 select_select_fusion
  65.7 2.9 %collective-permute-start.8 = (bf16[3,64,128]{2,1,0:T(8,128)(2,1)S(1)}, bf16[3,64,128]{2,1,0:T(8,128)(2,1)S(1)}, u32[]{:S(2)}, u32[]{:S(2)}) collective-permute-start(bf16[3,64,128]{2,1,0:T(8,128)(2,1)S(1)} %pad_maximum_fusion.1), channel_id=1, source_target_pairs={{0,3},{1,0},{2,1},{3,2},{4,7},{5,4},{6,5},{7,6},{8,11},{9,8},{10,9... | collective-permute-start | bytes 147464 | tf_op jit(solution)/shard_map/ppermute | solution.py:406
  68.6 0.8 collective-permute-start.7
  69.4 0.9 collective-permute-start.6
  70.3 6.8 %collective-permute-done.6 = bf16[3,64,128]{2,1,0:T(8,128)(2,1)S(1)} collective-permute-done((bf16[3,64,128]{2,1,0:T(8,128)(2,1)S(1)}, bf16[3,64,128]{2,1,0:T(8,128)(2,1)S(1)}, u32[]{:S(2)}, u32[]{:S(2)}) %collective-permute-start.6) | collective-permute-done | bytes 49184 | tf_op jit(solution)/shard_map/ppermute | solution.py:406
  77.2 0.0 collective-permute-done.7
  77.2 0.0 collective-permute-done.8
  77.2 0.0 collective-permute-done.2
  77.3 0.7 pad_maximum_fusion
  78.0 0.0 all-gather.10.cloned.1.call-update
  78.0 0.0 copy-start
  78.0 0.0 copy-start.2
  78.0 0.0 copy-start.3
  78.0 2.8 %collective-permute-start.15 = (bf16[9,64,128]{2,1,0:T(8,128)(2,1)S(1)}, bf16[9,64,128]{2,1,0:T(8,128)(2,1)S(1)}, u32[]{:S(2)}, u32[]{:S(2)}) collective-permute-start(bf16[9,64,128]{2,1,0:T(8,128)(2,1)S(1)} %fusion.2.refs_0_), channel_id=1, source_target_pairs={{0,112},{16,0},{32,16},{48,32},{64,48},{80,64},{96,80},{112,96},{1... | collective-permute-start | bytes 442376 | tf_op jit(solution)/shard_map/ppermute | solution.py:438
  80.8 0.0 collective-permute-start.14
  80.8 3.4 %collective-permute-start.13 = (bf16[9,64,128]{2,1,0:T(8,128)(2,1)S(1)}, bf16[9,64,128]{2,1,0:T(8,128)(2,1)S(1)}, u32[]{:S(2)}, u32[]{:S(2)}) collective-permute-start(bf16[9,64,128]{2,1,0:T(8,128)(2,1)S(1)} %fusion.2.refs_0_), channel_id=1, source_target_pairs={{0,80},{16,96},{32,112},{48,0},{64,16},{80,32},{96,48},{112,64},{1... | collective-permute-start | bytes 442376 | tf_op jit(solution)/shard_map/ppermute | solution.py:438
  84.2 0.1 collective-permute-start.12
  84.3 0.8 collective-permute-start.11
  85.1 0.0 collective-permute-done.15.refs_7_
  85.1 2.6 %collective-permute-start.10 = (bf16[9,64,128]{2,1,0:T(8,128)(2,1)S(1)}, bf16[9,64,128]{2,1,0:T(8,128)(2,1)S(1)}, u32[]{:S(2)}, u32[]{:S(2)}) collective-permute-start(bf16[9,64,128]{2,1,0:T(8,128)(2,1)S(1)} %fusion.2.refs_0_), channel_id=1, source_target_pairs={{0,32},{16,48},{32,64},{48,80},{64,96},{80,112},{96,0},{112,16},{1... | collective-permute-start | bytes 442376 | tf_op jit(solution)/shard_map/ppermute | solution.py:438
  87.7 5.5 %collective-permute-done.14.refs_6_ = bf16[9,64,128]{2,1,0:T(8,128)(2,1)S(1)} collective-permute-done((bf16[9,64,128]{2,1,0:T(8,128)(2,1)S(1)}, bf16[9,64,128]{2,1,0:T(8,128)(2,1)S(1)}, u32[]{:S(2)}, u32[]{:S(2)}) %collective-permute-start.14) | collective-permute-done | bytes 147488 | tf_op jit(solution)/shard_map/ppermute | solution.py:438
  93.2 0.0 collective-permute-start.9
  93.2 0.0 collective-permute-done.13.refs_5_
  93.2 0.0 collective-permute-done.12.refs_4_
  93.2 1.8 %collective-permute-done.11.refs_3_ = bf16[9,64,128]{2,1,0:T(8,128)(2,1)S(1)} collective-permute-done((bf16[9,64,128]{2,1,0:T(8,128)(2,1)S(1)}, bf16[9,64,128]{2,1,0:T(8,128)(2,1)S(1)}, u32[]{:S(2)}, u32[]{:S(2)}) %collective-permute-start.11) | collective-permute-done | bytes 147488 | tf_op jit(solution)/shard_map/ppermute | solution.py:438
  95.0 4.5 %collective-permute-done.10.refs_2_ = bf16[9,64,128]{2,1,0:T(8,128)(2,1)S(1)} collective-permute-done((bf16[9,64,128]{2,1,0:T(8,128)(2,1)S(1)}, bf16[9,64,128]{2,1,0:T(8,128)(2,1)S(1)}, u32[]{:S(2)}, u32[]{:S(2)}) %collective-permute-start.10) | collective-permute-done | bytes 147488 | tf_op jit(solution)/shard_map/ppermute | solution.py:438
  99.5 0.5 collective-permute-done.9.refs_1_
  100.0 44.0 %cholesky.1 = (bf16[1024,1024]{1,0:T(8,128)(2,1)}, f32[128,128]{1,0:T(8,128)S(1)}) custom-call(bf16[9,64,128]{2,1,0:T(8,128)(2,1)S(1)} %fusion.2.refs_0_, bf16[9,64,128]{2,1,0:T(8,128)(2,1)S(1)} %collective-permute-done.9.refs_1_, bf16[9,64,128]{2,1,0:T(8,128)(2,1)S(1)} %collective-permute-done.10.refs_2_, ...), custom_call_target="tpu_custom_call" | custom-call | flops 60000002048 | bytes 6291456 | tf_op jit(solution)/shard_map/cholesky/pallas_call | solution.py:244
  144.0 0.0 all-gather.6.cloned.1.call-done.cols_hbm
  144.1 2.7 %all-gather.10.cloned.1.call-done = bf16[20480,128]{1,0:T(8,128)(2,1)} async-done(((bf16[1280,128]{1,0:T(8,128)(2,1)}), bf16[20480,128]{1,0:T(8,128)(2,1)}) %all-gather.10.cloned.1.call-update) | async-done | bytes 5242896 | tf_op jit(solution)/shard_map/all_gather | solution.py:442
  146.7 0.0 copy-done
  146.7 0.0 copy-done.2
  146.7 0.0 copy-done.3
  146.7 19.6 %schur.1 = f32[16384,128]{1,0:T(8,128)} custom-call(s32[8,16]{1,0:T(8,128)S(1)} %copy-done.3, f32[128,128]{1,0:T(8,128)S(1)} %get-tuple-element.23.l_ref, bf16[8,2,128,128]{3,2,1,0:T(8,128)(2,1)S(1)} %copy-done.2, bf16[2,8,64,512]{3,2,1,0:T(8,128)(2,1)S(1)} %bitcast.20, bf16[8,128,512]{2,1,0:T(8,128)(2,1)} %bitcast.25, ...), custom_call_target="tpu_custom_call" | custom-call | tf_op jit(solution)/shard_map/schur/pallas_call | solution.py:360
  (10 shorter events, 0.1 us)
Async XLA Ops:
  8.4 14.9 %all-to-all-start = ((bf16[8,2,128,128]{3,2,1,0:T(8,128)(2,1)}), bf16[8,2,128,128]{3,2,1,0:T(8,128)(2,1)S(1)}, u32[]{:S(2)}, u32[]{:S(2)}) async-start(bf16[8,2,128,128]{3,2,1,0:T(8,128)(2,1)} %bitcast.18), calls=%async_computation | async-start | bytes 1048576 | tf_op jit(solution)/shard_map/all_to_all | solution.py:426
  13.0 38.7 %all-gather.8.cloned.1.call-start = ((), (), s32[]{:S(2)}) async-start(), calls=%async_computation.3 | async-start | bytes 1179648 | tf_op jit(solution)/shard_map/all_gather | solution.py:428
  13.9 6.2 %collective-permute-start.1 = (bf16[64,512]{1,0:T(8,128)(2,1)S(1)}, bf16[64,512]{1,0:T(8,128)(2,1)S(1)}, u32[]{:S(2)}, u32[]{:S(2)}) collective-permute-start(bf16[64,512]{1,0:T(8,128)(2,1)S(1)} %get-tuple-element.31), channel_id=1, source_target_pairs={{0,8},{1,24},{2,40},{3,56},{4,72},{5,88},{6,104},{7,120},{8,0},{9,... | collective-permute-start | bytes 196616 | tf_op jit(solution)/shard_map/ppermute | solution.py:424
  17.9 2.2 %collective-permute-start = (bf16[64,512]{1,0:T(8,128)(2,1)S(1)}, bf16[64,512]{1,0:T(8,128)(2,1)S(1)}, u32[]{:S(2)}, u32[]{:S(2)}) collective-permute-start(bf16[64,512]{1,0:T(8,128)(2,1)S(1)} %get-tuple-element.32), channel_id=1, source_target_pairs={{0,0},{1,16},{2,32},{3,48},{4,64},{5,80},{6,96},{7,112},{8,8},{9,2... | collective-permute-start | bytes 196616 | tf_op jit(solution)/shard_map/ppermute | solution.py:423
  23.3 28.4 %copy-start.1 = (bf16[8,2,128,128]{3,2,1,0:T(8,128)(2,1)}, bf16[8,2,128,128]{3,2,1,0:T(8,128)(2,1)S(1)}, u32[]{:S(2)}) copy-start(bf16[8,2,128,128]{3,2,1,0:T(8,128)(2,1)S(1)} %all-to-all-done.given_ref) | copy-start | bytes 1572868
  23.3 120.7 %all-gather.6.cloned.1.call-start = ((), (), s32[]{:S(2)}) async-start(), calls=%async_computation.2 | async-start | bytes 2359296 | tf_op jit(solution)/shard_map/all_gather | solution.py:433
  54.8 91.9 %all-gather.10.cloned.1.call-start = ((), (), s32[]{:S(2)}) async-start(), calls=%async_computation.4 | async-start | bytes 5570560 | tf_op jit(solution)/shard_map/all_gather | solution.py:442
  54.9 9.8 %collective-permute-start.5 = (bf16[2,64,128]{2,1,0:T(8,128)(2,1)}, bf16[2,64,128]{2,1,0:T(8,128)(2,1)S(1)}, u32[]{:S(2)}, u32[]{:S(2)}) collective-permute-start(bf16[2,64,128]{2,1,0:T(8,128)(2,1)} %get-tuple-element.21), channel_id=1, source_target_pairs={{0,12},{1,13},{2,14},{3,15},{4,0},{5,1},{6,2},{7,3},{16,28},{17,29... | collective-permute-start | bytes 98312 | tf_op jit(solution)/shard_map/ppermute | solution.py:398
  58.9 5.8 %collective-permute-start.4 = (bf16[2,64,128]{2,1,0:T(8,128)(2,1)}, bf16[2,64,128]{2,1,0:T(8,128)(2,1)S(1)}, u32[]{:S(2)}, u32[]{:S(2)}) collective-permute-start(bf16[2,64,128]{2,1,0:T(8,128)(2,1)} %get-tuple-element.21), channel_id=1, source_target_pairs={{0,8},{1,9},{2,10},{3,11},{4,12},{5,13},{6,14},{7,15},{16,24},{17,... | collective-permute-start | bytes 98312 | tf_op jit(solution)/shard_map/ppermute | solution.py:398
  60.2 4.7 %collective-permute-start.3 = (bf16[2,64,128]{2,1,0:T(8,128)(2,1)}, bf16[2,64,128]{2,1,0:T(8,128)(2,1)S(1)}, u32[]{:S(2)}, u32[]{:S(2)}) collective-permute-start(bf16[2,64,128]{2,1,0:T(8,128)(2,1)} %get-tuple-element.21), channel_id=1, source_target_pairs={{0,4},{1,5},{2,6},{3,7},{4,8},{5,9},{6,10},{7,11},{16,20},{17,21},... | collective-permute-start | bytes 98312 | tf_op jit(solution)/shard_map/ppermute | solution.py:398
  63.1 14.2 %collective-permute-start.2 = (bf16[8,128,128]{2,1,0:T(8,128)(2,1)}, bf16[8,128,128]{2,1,0:T(8,128)(2,1)S(1)}, u32[]{:S(2)}, u32[]{:S(2)}) collective-permute-start(bf16[8,128,128]{2,1,0:T(8,128)(2,1)} %get-tuple-element.20), channel_id=1, source_target_pairs={{0,0},{1,16},{2,32},{3,48},{4,64},{5,80},{6,96},{7,112},{8,8},{9,2... | collective-permute-start | bytes 786440 | tf_op jit(solution)/shard_map/ppermute | solution.py:434
  65.7 11.5 %collective-permute-start.8 = (bf16[3,64,128]{2,1,0:T(8,128)(2,1)S(1)}, bf16[3,64,128]{2,1,0:T(8,128)(2,1)S(1)}, u32[]{:S(2)}, u32[]{:S(2)}) collective-permute-start(bf16[3,64,128]{2,1,0:T(8,128)(2,1)S(1)} %pad_maximum_fusion.1), channel_id=1, source_target_pairs={{0,3},{1,0},{2,1},{3,2},{4,7},{5,4},{6,5},{7,6},{8,11},{9,8},{10,9... | collective-permute-start | bytes 147464 | tf_op jit(solution)/shard_map/ppermute | solution.py:406
  68.6 8.6 %collective-permute-start.7 = (bf16[3,64,128]{2,1,0:T(8,128)(2,1)S(1)}, bf16[3,64,128]{2,1,0:T(8,128)(2,1)S(1)}, u32[]{:S(2)}, u32[]{:S(2)}) collective-permute-start(bf16[3,64,128]{2,1,0:T(8,128)(2,1)S(1)} %pad_maximum_fusion.1), channel_id=1, source_target_pairs={{0,2},{1,3},{2,0},{3,1},{4,6},{5,7},{6,4},{7,5},{8,10},{9,11},{10,... | collective-permute-start | bytes 147464 | tf_op jit(solution)/shard_map/ppermute | solution.py:406
  69.4 7.7 %collective-permute-start.6 = (bf16[3,64,128]{2,1,0:T(8,128)(2,1)S(1)}, bf16[3,64,128]{2,1,0:T(8,128)(2,1)S(1)}, u32[]{:S(2)}, u32[]{:S(2)}) collective-permute-start(bf16[3,64,128]{2,1,0:T(8,128)(2,1)S(1)} %pad_maximum_fusion.1), channel_id=1, source_target_pairs={{0,1},{1,2},{2,3},{3,0},{4,5},{5,6},{6,7},{7,4},{8,9},{9,10},{10,1... | collective-permute-start | bytes 147464 | tf_op jit(solution)/shard_map/ppermute | solution.py:406
  78.0 68.7 %copy-start = (bf16[16,64,512]{2,1,0:T(8,128)(2,1)S(1)}, bf16[16,64,512]{2,1,0:T(8,128)(2,1)}, u32[]{:S(2)}) copy-start(bf16[16,64,512]{2,1,0:T(8,128)(2,1)} %all_to_all.10) | copy-start | bytes 3145732
  78.0 68.7 %copy-start.2 = (bf16[8,2,128,128]{3,2,1,0:T(8,128)(2,1)S(1)}, bf16[8,2,128,128]{3,2,1,0:T(8,128)(2,1)}, u32[]{:S(2)}) copy-start(bf16[8,2,128,128]{3,2,1,0:T(8,128)(2,1)} %copy-done.1) | copy-start | bytes 1572868
  78.0 68.7 %copy-start.3 = (s32[8,16]{1,0:T(8,128)S(1)}, s32[8,16]{1,0:T(8,128)}, u32[]{:S(2)}) copy-start(s32[8,16]{1,0:T(8,128)} %map_ref.3) | copy-start | bytes 1540
  78.0 7.1 %collective-permute-start.15 = (bf16[9,64,128]{2,1,0:T(8,128)(2,1)S(1)}, bf16[9,64,128]{2,1,0:T(8,128)(2,1)S(1)}, u32[]{:S(2)}, u32[]{:S(2)}) collective-permute-start(bf16[9,64,128]{2,1,0:T(8,128)(2,1)S(1)} %fusion.2.refs_0_), channel_id=1, source_target_pairs={{0,112},{16,0},{32,16},{48,32},{64,48},{80,64},{96,80},{112,96},{1... | collective-permute-start | bytes 442376 | tf_op jit(solution)/shard_map/ppermute | solution.py:438
  80.8 12.4 %collective-permute-start.14 = (bf16[9,64,128]{2,1,0:T(8,128)(2,1)S(1)}, bf16[9,64,128]{2,1,0:T(8,128)(2,1)S(1)}, u32[]{:S(2)}, u32[]{:S(2)}) collective-permute-start(bf16[9,64,128]{2,1,0:T(8,128)(2,1)S(1)} %fusion.2.refs_0_), channel_id=1, source_target_pairs={{0,96},{16,112},{32,0},{48,16},{64,32},{80,48},{96,64},{112,80},{1... | collective-permute-start | bytes 442376 | tf_op jit(solution)/shard_map/ppermute | solution.py:438
  80.8 12.4 %collective-permute-start.13 = (bf16[9,64,128]{2,1,0:T(8,128)(2,1)S(1)}, bf16[9,64,128]{2,1,0:T(8,128)(2,1)S(1)}, u32[]{:S(2)}, u32[]{:S(2)}) collective-permute-start(bf16[9,64,128]{2,1,0:T(8,128)(2,1)S(1)} %fusion.2.refs_0_), channel_id=1, source_target_pairs={{0,80},{16,96},{32,112},{48,0},{64,16},{80,32},{96,48},{112,64},{1... | collective-permute-start | bytes 442376 | tf_op jit(solution)/shard_map/ppermute | solution.py:438
  84.2 9.0 %collective-permute-start.12 = (bf16[9,64,128]{2,1,0:T(8,128)(2,1)S(1)}, bf16[9,64,128]{2,1,0:T(8,128)(2,1)S(1)}, u32[]{:S(2)}, u32[]{:S(2)}) collective-permute-start(bf16[9,64,128]{2,1,0:T(8,128)(2,1)S(1)} %fusion.2.refs_0_), channel_id=1, source_target_pairs={{0,64},{16,80},{32,96},{48,112},{64,0},{80,16},{96,32},{112,48},{1... | collective-permute-start | bytes 442376 | tf_op jit(solution)/shard_map/ppermute | solution.py:438
  84.3 10.6 %collective-permute-start.11 = (bf16[9,64,128]{2,1,0:T(8,128)(2,1)S(1)}, bf16[9,64,128]{2,1,0:T(8,128)(2,1)S(1)}, u32[]{:S(2)}, u32[]{:S(2)}) collective-permute-start(bf16[9,64,128]{2,1,0:T(8,128)(2,1)S(1)} %fusion.2.refs_0_), channel_id=1, source_target_pairs={{0,48},{16,64},{32,80},{48,96},{64,112},{80,0},{96,16},{112,32},{1... | collective-permute-start | bytes 442376 | tf_op jit(solution)/shard_map/ppermute | solution.py:438
  85.1 14.3 %collective-permute-start.10 = (bf16[9,64,128]{2,1,0:T(8,128)(2,1)S(1)}, bf16[9,64,128]{2,1,0:T(8,128)(2,1)S(1)}, u32[]{:S(2)}, u32[]{:S(2)}) collective-permute-start(bf16[9,64,128]{2,1,0:T(8,128)(2,1)S(1)} %fusion.2.refs_0_), channel_id=1, source_target_pairs={{0,32},{16,48},{32,64},{48,80},{64,96},{80,112},{96,0},{112,16},{1... | collective-permute-start | bytes 442376 | tf_op jit(solution)/shard_map/ppermute | solution.py:438
  93.2 6.8 %collective-permute-start.9 = (bf16[9,64,128]{2,1,0:T(8,128)(2,1)S(1)}, bf16[9,64,128]{2,1,0:T(8,128)(2,1)S(1)}, u32[]{:S(2)}, u32[]{:S(2)}) collective-permute-start(bf16[9,64,128]{2,1,0:T(8,128)(2,1)S(1)} %fusion.2.refs_0_), channel_id=1, source_target_pairs={{0,16},{16,32},{32,48},{48,64},{64,80},{80,96},{96,112},{112,0},{1... | collective-permute-start | bytes 442376 | tf_op jit(solution)/shard_map/ppermute | solution.py:438
Sparse Core Ops, SparseCore 0:
  23.5 27.3 all-gather.7
  55.0 29.1 all-gather.5
  86.3 60.4 all-gather.9

commit v4 on v3

--- a/solution.py
+++ b/solution.py
@@ -15,6 +15,7 @@
 N_FRONT = 16
 STEP_ROWS = 4
 MESH_AXES = ("leaf", "front")
+CORES = [(i, i ^ 1) for i in range(N_LEAF)]
 WHOLE = pl.BlockSpec(memory_space=pltpu.VMEM)
 TABLE = pl.BlockSpec(memory_space=pltpu.SMEM)
 
@@ -190,7 +191,8 @@
     leaf, front = place()
     half = BLK // 2
     for k in range(N_LEAF):
-        giver = (leaf + N_LEAF - k) % N_LEAF * BLK
+        near = leaf if k < 4 else leaf + 1 - 2 * (leaf % 2)
+        giver = (near + N_LEAF - 2 * (k % 4)) % N_LEAF * BLK
         for n in range(KS + 1):
             at = (n % 2 * 4 + (front + 4 - n // 2) % 4) * BLK
             top = at <= giver
@@ -268,9 +270,42 @@
     )(*pieces)
 
 
+def columns_kernel(m_ref, cols_ref, given_ref, upper_ref, panel_ref, w_ref, early_ref):
+    for n in range(4):
+        take = slice(n * 256, (n + 1) * 256)
+        upto = slice(0, (n + 1) * 256)
+        w_ref[take, :] = dot(m_ref[take, upto], cols_ref[upto, :], 1, 0).astype(BF16)
+    for c in range(N_LEAF):
+        early_ref[c] = update_of(given_ref[c, 0], rows_of(upper_ref, c), panel_ref[c])
+
+
+def columns(m, cols, given, upper, panels):
+    return pl.pallas_call(
+        columns_kernel,
+        name="columns",
+        grid=(1,),
+        out_shape=(
+            jax.ShapeDtypeStruct((ORDER, ORDER), BF16),
+            jax.ShapeDtypeStruct((N_LEAF, BLK, BLK), BF16),
+        ),
+        in_specs=[
+            WHOLE,
+            WHOLE,
+            pl.BlockSpec((N_LEAF, 1, BLK, BLK), lambda i: (0, 0, 0, 0)),
+            WHOLE,
+            WHOLE,
+        ],
+        out_specs=(WHOLE, WHOLE),
+        compiler_params=pltpu.CompilerParams(vmem_limit_bytes=52 << 20),
+        cost_estimate=pl.CostEstimate(
+            flops=4_000_000_000, bytes_accessed=8 << 20, transcendentals=0
+        ),
+    )(m, cols, given, upper, panels)
+
+
 def schur_kernel(
-    map_ref, l_ref, given_ref, upper_ref, panel_ref, m_hbm, cols_hbm, rows_hbm, front_ref,
-    out_ref, m_ref, cols_ref, rows_ref, lower_ref, w_ref, low_ref, update_ref, sem
+    map_ref, l_ref, given_ref, early_ref, panel_ref, w_ref, m_hbm, rows_hbm, front_ref,
+    out_ref, m_ref, rows_ref, lower_ref, low_ref, late_ref, sem
 ):
     step = pl.program_id(0)
     leaf, front = place()
@@ -278,7 +313,6 @@
 
     def copies():
         yield pltpu.make_async_copy(m_hbm, m_ref, sem.at[2, 0])
-        yield pltpu.make_async_copy(cols_hbm, cols_ref, sem.at[2, 1])
         for b in range(2):
             for a in range(KS):
                 columns = pl.ds(a * BLK, BLK)
@@ -294,16 +328,7 @@
     def _():
         for copy in copies():
             copy.start()
-        for c in range(N_LEAF):
-            update_ref[c, 0] = update_of(given_ref[c, 0], rows_of(upper_ref, c), panel_ref[c])
-        waits = list(copies())
-        waits[0].wait()
-        waits[1].wait()
-        for n in range(4):
-            take = slice(n * 256, (n + 1) * 256)
-            upto = slice(0, (n + 1) * 256)
-            w_ref[take, :] = dot(m_ref[take, upto], cols_ref[upto, :], 1, 0).astype(BF16)
-        for copy in waits[2:]:
+        for copy in copies():
             copy.wait()
         for c in range(N_LEAF):
             product = jnp.zeros((BLK, BLK), F32)
@@ -311,7 +336,7 @@
                 part = slice(n * BLK // 2, (n + 1) * BLK // 2)
                 rows = jnp.concatenate([lower_ref[0, c, part], lower_ref[1, c, part]], axis=0)
                 product += dot(rows, panel_ref[c, :, n * BLK : (n + 1) * BLK], 1, 1)
-            update_ref[c, 1] = (given_ref[c, 1].astype(F32) - product).astype(BF16)
+            late_ref[c] = (given_ref[c, 0].astype(F32) - product).astype(BF16)
 
     pair = STEP_ROWS // 2 * BLK
     source = pl.ds(pl.multiple_of(step * pair, pair), pair)
@@ -337,7 +362,8 @@
             @pl.when((q >= 0) & (q < STEP_ROWS))
             def _():
                 there = pl.ds(q * (8 * BLK) + s, BLK, stride=8)
-                out_ref[there, :] = out_ref[there, :] + update_ref[c, b].astype(F32)
+                added = (late_ref if b else early_ref)[c].astype(F32)
+                out_ref[there, :] = out_ref[there, :] + added
 
     @pl.when(front < KS)
     def _():
@@ -354,7 +380,7 @@
             out_ref[pl.ds(0, BLK, stride=8), :] = l_ref[...]
 
 
-def schur(child_map, low, given, upper, panels, m, cols, rows, front):
+def schur(child_map, low, given, early, panels, w, m, rows, front):
     steps = 16 // STEP_ROWS
     block = pl.BlockSpec((STEP_ROWS * BLK * 8, BLK), lambda i: (i, 0))
     return pl.pallas_call(
@@ -362,20 +388,28 @@
         name="schur",
         grid=(steps,),
         out_shape=jax.ShapeDtypeStruct((16 * BLK * 8, BLK), F32),
-        in_specs=[TABLE] + [WHOLE] * 4 + [pl.BlockSpec(memory_space=pltpu.HBM)] * 3 + [block],
+        in_specs=[
+            TABLE,
+            WHOLE,
+            pl.BlockSpec((N_LEAF, 1, BLK, BLK), lambda i: (0, 1, 0, 0)),
+            WHOLE,
+            WHOLE,
+            WHOLE,
+            pl.BlockSpec(memory_space=pltpu.HBM),
+            pl.BlockSpec(memory_space=pltpu.HBM),
+            block,
+        ],
         out_specs=block,
         scratch_shapes=[
             pltpu.VMEM((ORDER, ORDER), BF16),
-            pltpu.VMEM((ORDER, ORDER), BF16),
             pltpu.VMEM((2, ORDER, ORDER), BF16),
             pltpu.VMEM((2, KS, 2 * BLK, BLK), BF16),
-            pltpu.VMEM((ORDER, ORDER), BF16),
             pltpu.VMEM((STEP_ROWS * BLK, ORDER), F32),
-            pltpu.VMEM((N_LEAF, 2, BLK, BLK), BF16),
+            pltpu.VMEM((N_LEAF, BLK, BLK), BF16),
             pltpu.SemaphoreType.DMA((5, KS)),
         ],
         compiler_params=pltpu.CompilerParams(vmem_limit_bytes=52 << 20),
-    )(child_map, low, given, upper, panels, m, cols, rows, front)
+    )(child_map, low, given, early, panels, w, m, rows, front)
 
 
 def gather(x, axis, count):
@@ -434,15 +468,19 @@
     turned = lax.ppermute(turned, MESH_AXES, exchange(0))
     whole = front_pieces(first, leaf_id, front_id)
     turned, whole = lax.optimization_barrier((turned, whole))
-    separator = [whole] + [
-        lax.ppermute(whole, "leaf", [(i, (i + k) % N_LEAF) for i in range(N_LEAF)])
-        for k in range(1, N_LEAF)
+    across = [lax.ppermute(whole, "leaf", CORES)]
+    along = [whole] + [
+        lax.ppermute(whole, "leaf", [(i, (i + 2 * k) % N_LEAF) for i in range(N_LEAF)])
+        for k in (1, 2, 3)
     ]
+    across += [lax.ppermute(one, "leaf", CORES) for one in along[1:]]
+    separator = along + across
     packed = jnp.concatenate([turned.reshape(ORDER, BLK), lower.reshape(2 * BLK, BLK)], axis=0)
     rows = lax.all_gather(packed, "front", axis=0)
     m, low = cholesky(separator)
     rows = rows.reshape(2, KS, ORDER + 2 * BLK, BLK)
-    out = schur(child_map, low, given, upper, panels, m, cols, rows, front)
+    w, early_updates = columns(m, cols, given, upper, panels)
+    out = schur(child_map, low, given, early_updates, panels, w, m, rows, front)
     return out.reshape(16, 1, BLK, 8, 1, BLK)
 
 

time: 174 us -> 174 us (level)
  Pallas kernels: 66.7 us -> 71.9 us
  waiting for transfers between devices: 26.9 us -> 23 us
    ppermute x7, waiting for transfers between devices: 12.3 us -> 6.37 us  [the longest x3 5.01 us: one_pass(): lax.ppermute(whole, 'leaf', [(i, (i + 2 * k) % N_LEAF) for i in range(N_L...]
    pallas_call x0 -> x1, Pallas kernels: none -> 5.52 us  [columns(): pl.pallas_call(columns_kernel, name='columns', grid=(1,), out_shape=(jax....]
    all_gather x1, waiting for transfers between devices: 2.66 us -> 4.79 us  [one_pass(): rows = lax.all_gather(packed, 'front', axis=0)]
  transfers between devices with their start and end apart: 20 -> 20, of which waited for: 9 -> 8; matrix products, arithmetic and copies ran while one was open for 2% -> 2% of each run, Pallas kernels for 25% -> 29%
where the time goes in v4:
time: 174 us; the launch traced here: 173 us
  Pallas kernels  71.9 us (41%)
  starting transfers between devices  31.7 us (18%)
  blocking collectives  28.1 us (16%)
  waiting for transfers between devices  23 us (13%)
  between operations  13.4 us (8%)
  other arithmetic  2.48 us (1%)
  local copies, waits for them, and re-layouts  2.07 us (1%)
    pallas_call x1, Pallas kernels, cholesky(): pl.pallas_call(cholesky_kernel, name='cholesky', out_shape=(jax.ShapeDtyp...  44.2 us
    all_to_all x1, blocking collectives, gather(): return lax.all_to_all(spread, axis, 0, 0)  28.1 us
    pallas_call x1, Pallas kernels, schur(): pl.pallas_call(schur_kernel, name='schur', grid=(steps,), out_shape=jax.S...  19.1 us
    ppermute x3, starting transfers between devices, front_pieces(): lax.ppermute(first, 'front', [(4 * i + j, (i + k) % 4 * 4 + j) for i in (...  8.06 us
    ppermute x3, starting transfers between devices, one_pass(): lax.ppermute(whole, 'leaf', [(i, (i + 2 * k) % N_LEAF) for i in range(N_L...  7.52 us
    ppermute x3, waiting for transfers between devices, front_pieces(): lax.ppermute(mine, 'front', [(4 * i + j, 4 * i + (j + k) % 4) for i in ra...  6.86 us
    pallas_call x1, Pallas kernels, columns(): pl.pallas_call(columns_kernel, name='columns', grid=(1,), out_shape=(jax....  5.52 us
    ppermute x3, waiting for transfers between devices, one_pass(): lax.ppermute(whole, 'leaf', [(i, (i + 2 * k) % N_LEAF) for i in range(N_L...  5.01 us
  transfers between devices with their start and end apart: 20, of which 8 were waited for; matrix products, arithmetic and copies ran while one was open for 2% of the time, Pallas kernels for 29%

profile of v4, /device:TPU:0, one launch (start us, length us, event | category | flops | bytes accessed | tf_op | source)
XLA Modules:
  0.0 172.7 jit_solution(15121798182442305492)
XLA Ops:
  6.5 1.9 %copy.11 = bf16[2,8,128,128]{3,2,0,1:T(8,128)(2,1)} copy(bf16[2,8,128,128]{3,2,1,0:T(8,128)(2,1)} %bitcast.27) | data formatting | bytes 1048576 | tf_op jit(solution)/shard_map/reshape;squeeze | solution.py:459
  8.4 4.6 %all-to-all-start = ((bf16[8,2,128,128]{3,2,1,0:T(8,128)(2,1)}), bf16[8,2,128,128]{3,2,1,0:T(8,128)(2,1)S(1)}, u32[]{:S(2)}, u32[]{:S(2)}) async-start(bf16[8,2,128,128]{3,2,1,0:T(8,128)(2,1)} %bitcast.18), calls=%async_computation | async-start | bytes 1048576 | tf_op jit(solution)/shard_map/all_to_all | solution.py:460
  13.0 0.0 all-gather.8.cloned.1.call-start
  13.1 0.9 select_bitcast_fusion
  13.9 4.0 %collective-permute-start.1 = (bf16[64,512]{1,0:T(8,128)(2,1)S(1)}, bf16[64,512]{1,0:T(8,128)(2,1)S(1)}, u32[]{:S(2)}, u32[]{:S(2)}) collective-permute-start(bf16[64,512]{1,0:T(8,128)(2,1)S(1)} %get-tuple-element.35), channel_id=1, source_target_pairs={{0,8},{1,24},{2,40},{3,56},{4,72},{5,88},{6,104},{7,120},{8,0},{9,... | collective-permute-start | bytes 196616 | tf_op jit(solution)/shard_map/ppermute | solution.py:458
  17.9 0.7 collective-permute-start
  18.6 1.6 collective-permute-done.1
  20.1 0.0 collective-permute-done
  20.1 3.2 %all-to-all-done.given_ref = bf16[8,2,128,128]{3,2,1,0:T(8,128)(2,1)S(1)} async-done(((bf16[8,2,128,128]{3,2,1,0:T(8,128)(2,1)}), bf16[8,2,128,128]{3,2,1,0:T(8,128)(2,1)S(1)}, u32[]{:S(2)}, u32[]{:S(2)}) %all-to-all-start) | async-done | bytes 524320 | tf_op jit(solution)/shard_map/all_to_all | solution.py:460
  23.3 0.0 copy-start
  23.3 0.0 all-gather.8.cloned.1.call-update
  23.3 0.0 all-gather.6.cloned.1.call-start
  23.4 0.1 broadcast_in_dim.2
  23.5 28.1 %all_to_all.10 = bf16[16,64,512]{2,1,0:T(8,128)(2,1)} all-to-all(bf16[16,64,512]{2,1,0:T(8,128)(2,1)S(1)} %broadcast_in_dim.2), channel_id=1, replica_groups=mesh['leaf'=8,'front'=16] {'front'}, dimensions={0} | all-to-all | bytes 2097152 | tf_op jit(solution)/shard_map/all_to_all | solution.py:417
  51.7 0.0 all-gather.8.cloned.1.call-done
  51.7 0.0 copy-done
  51.7 3.1 %pivot_rows.1 = (bf16[128,1024]{1,0:T(8,128)(2,1)}, bf16[8,128,128]{2,1,0:T(8,128)(2,1)}, bf16[2,64,128]{2,1,0:T(8,128)(2,1)}) custom-call(s32[8,16]{1,0:T(8,128)} %map_ref.3, f32[16384,128]{1,0:T(8,128)} %bitcast.24, bf16[8,2,128,128]{3,2,1,0:T(8,128)(2,1)} %copy-done, bf16[2,8,64,512]{3,2,1,0:T(8,128)(2,1)} %bitcast.22, bf16[8,128,512]{2,1,0:T(8,128)(2,1)} %bitcast.19), custom_call_target="tpu_custom_call" | custom-call | tf_op jit(solution)/shard_map/pivot_rows/pallas_call | solution.py:67
  54.8 0.0 all-gather.6.cloned.1.call-update
  54.8 0.0 all-gather.10.cloned.1.call-start
  54.9 4.0 %collective-permute-start.5 = (bf16[2,64,128]{2,1,0:T(8,128)(2,1)}, bf16[2,64,128]{2,1,0:T(8,128)(2,1)S(1)}, u32[]{:S(2)}, u32[]{:S(2)}) collective-permute-start(bf16[2,64,128]{2,1,0:T(8,128)(2,1)} %get-tuple-element.23), channel_id=1, source_target_pairs={{0,12},{1,13},{2,14},{3,15},{4,0},{5,1},{6,2},{7,3},{16,28},{17,29... | collective-permute-start | bytes 98312 | tf_op jit(solution)/shard_map/ppermute | solution.py:432
  58.9 1.3 collective-permute-start.4
  60.2 2.8 %collective-permute-start.3 = (bf16[2,64,128]{2,1,0:T(8,128)(2,1)}, bf16[2,64,128]{2,1,0:T(8,128)(2,1)S(1)}, u32[]{:S(2)}, u32[]{:S(2)}) collective-permute-start(bf16[2,64,128]{2,1,0:T(8,128)(2,1)} %get-tuple-element.23), channel_id=1, source_target_pairs={{0,4},{1,5},{2,6},{3,7},{4,8},{5,9},{6,10},{7,11},{16,20},{17,21},... | collective-permute-start | bytes 98312 | tf_op jit(solution)/shard_map/ppermute | solution.py:432
  63.0 1.6 collective-permute-start.2
  64.7 0.0 collective-permute-done.5
  64.7 0.0 collective-permute-done.4
  64.7 0.2 collective-permute-done.3
  64.8 0.8 select_select_fusion
  65.7 2.9 %collective-permute-start.8 = (bf16[3,64,128]{2,1,0:T(8,128)(2,1)S(1)}, bf16[3,64,128]{2,1,0:T(8,128)(2,1)S(1)}, u32[]{:S(2)}, u32[]{:S(2)}) collective-permute-start(bf16[3,64,128]{2,1,0:T(8,128)(2,1)S(1)} %pad_maximum_fusion.1), channel_id=1, source_target_pairs={{0,3},{1,0},{2,1},{3,2},{4,7},{5,4},{6,5},{7,6},{8,11},{9,8},{10,9... | collective-permute-start | bytes 147464 | tf_op jit(solution)/shard_map/ppermute | solution.py:440
  68.6 0.8 collective-permute-start.7
  69.4 0.9 collective-permute-start.6
  70.3 6.8 %collective-permute-done.6 = bf16[3,64,128]{2,1,0:T(8,128)(2,1)S(1)} collective-permute-done((bf16[3,64,128]{2,1,0:T(8,128)(2,1)S(1)}, bf16[3,64,128]{2,1,0:T(8,128)(2,1)S(1)}, u32[]{:S(2)}, u32[]{:S(2)}) %collective-permute-start.6) | collective-permute-done | bytes 49184 | tf_op jit(solution)/shard_map/ppermute | solution.py:440
  77.2 0.0 collective-permute-done.7
  77.2 0.0 collective-permute-done.8
  77.2 0.0 collective-permute-done.2
  77.2 0.8 pad_maximum_fusion
  78.0 0.0 all-gather.10.cloned.1.call-update
  78.0 0.0 copy-start.1
  78.0 0.0 copy-start.3
  78.1 0.8 collective-permute-start.11
  78.8 5.4 %collective-permute-start.10 = (bf16[9,64,128]{2,1,0:T(8,128)(2,1)S(1)}, bf16[9,64,128]{2,1,0:T(8,128)(2,1)S(1)}, u32[]{:S(2)}, u32[]{:S(2)}) collective-permute-start(bf16[9,64,128]{2,1,0:T(8,128)(2,1)S(1)} %fusion.2.refs_0_), channel_id=1, source_target_pairs={{0,64},{16,80},{32,96},{48,112},{64,0},{80,16},{96,32},{112,48},{1... | collective-permute-start | bytes 442376 | tf_op jit(solution)/shard_map/ppermute | solution.py:473
  84.3 1.3 collective-permute-start.9
  85.6 0.0 collective-permute-start.12
  85.6 0.0 collective-permute-done.11.refs_3_
  85.6 0.5 collective-permute-start.15
  86.1 2.9 %collective-permute-done.10.refs_2_ = bf16[9,64,128]{2,1,0:T(8,128)(2,1)S(1)} collective-permute-done((bf16[9,64,128]{2,1,0:T(8,128)(2,1)S(1)}, bf16[9,64,128]{2,1,0:T(8,128)(2,1)S(1)}, u32[]{:S(2)}, u32[]{:S(2)}) %collective-permute-start.10) | collective-permute-done | bytes 147488 | tf_op jit(solution)/shard_map/ppermute | solution.py:473
  89.0 0.0 collective-permute-start.14
  89.0 2.1 %collective-permute-done.9.refs_1_ = bf16[9,64,128]{2,1,0:T(8,128)(2,1)S(1)} collective-permute-done((bf16[9,64,128]{2,1,0:T(8,128)(2,1)S(1)}, bf16[9,64,128]{2,1,0:T(8,128)(2,1)S(1)}, u32[]{:S(2)}, u32[]{:S(2)}) %collective-permute-start.9) | collective-permute-done | bytes 147488 | tf_op jit(solution)/shard_map/ppermute | solution.py:473
  91.1 0.0 collective-permute-start.13
  91.1 0.0 collective-permute-done.12.refs_4_
  91.1 0.0 collective-permute-done.15.refs_7_
  91.1 0.0 collective-permute-done.14.refs_6_
  91.1 1.3 collective-permute-done.13.refs_5_
  92.5 44.2 %cholesky.1 = (bf16[1024,1024]{1,0:T(8,128)(2,1)}, f32[128,128]{1,0:T(8,128)S(1)}) custom-call(bf16[9,64,128]{2,1,0:T(8,128)(2,1)S(1)} %fusion.2.refs_0_, bf16[9,64,128]{2,1,0:T(8,128)(2,1)S(1)} %collective-permute-done.9.refs_1_, bf16[9,64,128]{2,1,0:T(8,128)(2,1)S(1)} %collective-permute-done.10.refs_2_, ...), custom_call_target="tpu_custom_call" | custom-call | flops 60000002048 | bytes 6291456 | tf_op jit(solution)/shard_map/cholesky/pallas_call | solution.py:246
  136.7 0.0 all-gather.6.cloned.1.call-done.cols_ref
  136.7 0.0 copy-done.1
  136.7 0.0 copy-done.3
  136.7 0.0 copy-start.2
  136.7 0.0 copy-start.4
  136.7 5.5 %columns.1 = (bf16[1024,1024]{1,0:T(8,128)(2,1)}, bf16[8,128,128]{2,1,0:T(8,128)(2,1)S(1)}) custom-call(bf16[1024,1024]{1,0:T(8,128)(2,1)} %get-tuple-element.26.m_ref.m_hbm, bf16[1024,1024]{1,0:T(8,128)(2,1)} %all-gather.6.cloned.1.call-done.cols_ref, bf16[8,2,128,128]{3,2,1,0:T(8,128)(2,1)S(1)} %copy-done.1, bf16[2,8,64,512]{3,2,1,0:T(8,128)(2,1)S(1)} %bitcast.23, ...), custom_call_target="tpu_custom_call" | custom-call | flops 4000000000 | bytes 8388608 | tf_op jit(solution)/shard_map/columns/pallas_call | solution.py:283
  142.3 4.8 %all-gather.10.cloned.1.call-done = bf16[20480,128]{1,0:T(8,128)(2,1)} async-done(((bf16[1280,128]{1,0:T(8,128)(2,1)}), bf16[20480,128]{1,0:T(8,128)(2,1)}) %all-gather.10.cloned.1.call-update) | async-done | bytes 5242896 | tf_op jit(solution)/shard_map/all_gather | solution.py:479
  147.0 0.0 copy-done.2
  147.0 0.0 copy-done.4
  147.0 19.1 %schur.1 = f32[16384,128]{1,0:T(8,128)} custom-call(s32[8,16]{1,0:T(8,128)S(1)} %copy-done.4, f32[128,128]{1,0:T(8,128)S(1)} %get-tuple-element.25.l_ref, bf16[8,2,128,128]{3,2,1,0:T(8,128)(2,1)S(1)} %copy-done.1, bf16[8,128,128]{2,1,0:T(8,128)(2,1)S(1)} %get-tuple-element.28.early_ref, bf16[8,128,512]{2,1,0:T(8,128)(2,1)S(1)} %bitcast.21, ...), custom_call_target="tpu_custom_call" | custom-call | tf_op jit(solution)/shard_map/schur/pallas_call | solution.py:386
  (10 shorter events, 0.1 us)
Async XLA Ops:
  8.4 14.9 %all-to-all-start = ((bf16[8,2,128,128]{3,2,1,0:T(8,128)(2,1)}), bf16[8,2,128,128]{3,2,1,0:T(8,128)(2,1)S(1)}, u32[]{:S(2)}, u32[]{:S(2)}) async-start(bf16[8,2,128,128]{3,2,1,0:T(8,128)(2,1)} %bitcast.18), calls=%async_computation | async-start | bytes 1048576 | tf_op jit(solution)/shard_map/all_to_all | solution.py:460
  13.0 38.7 %all-gather.8.cloned.1.call-start = ((), (), s32[]{:S(2)}) async-start(), calls=%async_computation.3 | async-start | bytes 1179648 | tf_op jit(solution)/shard_map/all_gather | solution.py:462
  13.9 6.2 %collective-permute-start.1 = (bf16[64,512]{1,0:T(8,128)(2,1)S(1)}, bf16[64,512]{1,0:T(8,128)(2,1)S(1)}, u32[]{:S(2)}, u32[]{:S(2)}) collective-permute-start(bf16[64,512]{1,0:T(8,128)(2,1)S(1)} %get-tuple-element.35), channel_id=1, source_target_pairs={{0,8},{1,24},{2,40},{3,56},{4,72},{5,88},{6,104},{7,120},{8,0},{9,... | collective-permute-start | bytes 196616 | tf_op jit(solution)/shard_map/ppermute | solution.py:458
  17.9 2.2 %collective-permute-start = (bf16[64,512]{1,0:T(8,128)(2,1)S(1)}, bf16[64,512]{1,0:T(8,128)(2,1)S(1)}, u32[]{:S(2)}, u32[]{:S(2)}) collective-permute-start(bf16[64,512]{1,0:T(8,128)(2,1)S(1)} %get-tuple-element.36), channel_id=1, source_target_pairs={{0,0},{1,16},{2,32},{3,48},{4,64},{5,80},{6,96},{7,112},{8,8},{9,2... | collective-permute-start | bytes 196616 | tf_op jit(solution)/shard_map/ppermute | solution.py:457
  23.3 28.4 %copy-start = (bf16[8,2,128,128]{3,2,1,0:T(8,128)(2,1)}, bf16[8,2,128,128]{3,2,1,0:T(8,128)(2,1)S(1)}, u32[]{:S(2)}) copy-start(bf16[8,2,128,128]{3,2,1,0:T(8,128)(2,1)S(1)} %all-to-all-done.given_ref) | copy-start | bytes 1572868
  23.3 113.3 %all-gather.6.cloned.1.call-start = ((), (), s32[]{:S(2)}) async-start(), calls=%async_computation.2 | async-start | bytes 2359296 | tf_op jit(solution)/shard_map/all_gather | solution.py:467
  54.8 92.2 %all-gather.10.cloned.1.call-start = ((), (), s32[]{:S(2)}) async-start(), calls=%async_computation.4 | async-start | bytes 5570560 | tf_op jit(solution)/shard_map/all_gather | solution.py:479
  54.9 9.8 %collective-permute-start.5 = (bf16[2,64,128]{2,1,0:T(8,128)(2,1)}, bf16[2,64,128]{2,1,0:T(8,128)(2,1)S(1)}, u32[]{:S(2)}, u32[]{:S(2)}) collective-permute-start(bf16[2,64,128]{2,1,0:T(8,128)(2,1)} %get-tuple-element.23), channel_id=1, source_target_pairs={{0,12},{1,13},{2,14},{3,15},{4,0},{5,1},{6,2},{7,3},{16,28},{17,29... | collective-permute-start | bytes 98312 | tf_op jit(solution)/shard_map/ppermute | solution.py:432
  58.9 5.8 %collective-permute-start.4 = (bf16[2,64,128]{2,1,0:T(8,128)(2,1)}, bf16[2,64,128]{2,1,0:T(8,128)(2,1)S(1)}, u32[]{:S(2)}, u32[]{:S(2)}) collective-permute-start(bf16[2,64,128]{2,1,0:T(8,128)(2,1)} %get-tuple-element.23), channel_id=1, source_target_pairs={{0,8},{1,9},{2,10},{3,11},{4,12},{5,13},{6,14},{7,15},{16,24},{17,... | collective-permute-start | bytes 98312 | tf_op jit(solution)/shard_map/ppermute | solution.py:432
  60.2 4.7 %collective-permute-start.3 = (bf16[2,64,128]{2,1,0:T(8,128)(2,1)}, bf16[2,64,128]{2,1,0:T(8,128)(2,1)S(1)}, u32[]{:S(2)}, u32[]{:S(2)}) collective-permute-start(bf16[2,64,128]{2,1,0:T(8,128)(2,1)} %get-tuple-element.23), channel_id=1, source_target_pairs={{0,4},{1,5},{2,6},{3,7},{4,8},{5,9},{6,10},{7,11},{16,20},{17,21},... | collective-permute-start | bytes 98312 | tf_op jit(solution)/shard_map/ppermute | solution.py:432
  63.0 14.2 %collective-permute-start.2 = (bf16[8,128,128]{2,1,0:T(8,128)(2,1)}, bf16[8,128,128]{2,1,0:T(8,128)(2,1)S(1)}, u32[]{:S(2)}, u32[]{:S(2)}) collective-permute-start(bf16[8,128,128]{2,1,0:T(8,128)(2,1)} %get-tuple-element.22), channel_id=1, source_target_pairs={{0,0},{1,16},{2,32},{3,48},{4,64},{5,80},{6,96},{7,112},{8,8},{9,2... | collective-permute-start | bytes 786440 | tf_op jit(solution)/shard_map/ppermute | solution.py:468
  65.7 11.5 %collective-permute-start.8 = (bf16[3,64,128]{2,1,0:T(8,128)(2,1)S(1)}, bf16[3,64,128]{2,1,0:T(8,128)(2,1)S(1)}, u32[]{:S(2)}, u32[]{:S(2)}) collective-permute-start(bf16[3,64,128]{2,1,0:T(8,128)(2,1)S(1)} %pad_maximum_fusion.1), channel_id=1, source_target_pairs={{0,3},{1,0},{2,1},{3,2},{4,7},{5,4},{6,5},{7,6},{8,11},{9,8},{10,9... | collective-permute-start | bytes 147464 | tf_op jit(solution)/shard_map/ppermute | solution.py:440
  68.6 8.6 %collective-permute-start.7 = (bf16[3,64,128]{2,1,0:T(8,128)(2,1)S(1)}, bf16[3,64,128]{2,1,0:T(8,128)(2,1)S(1)}, u32[]{:S(2)}, u32[]{:S(2)}) collective-permute-start(bf16[3,64,128]{2,1,0:T(8,128)(2,1)S(1)} %pad_maximum_fusion.1), channel_id=1, source_target_pairs={{0,2},{1,3},{2,0},{3,1},{4,6},{5,7},{6,4},{7,5},{8,10},{9,11},{10,... | collective-permute-start | bytes 147464 | tf_op jit(solution)/shard_map/ppermute | solution.py:440
  69.4 7.7 %collective-permute-start.6 = (bf16[3,64,128]{2,1,0:T(8,128)(2,1)S(1)}, bf16[3,64,128]{2,1,0:T(8,128)(2,1)S(1)}, u32[]{:S(2)}, u32[]{:S(2)}) collective-permute-start(bf16[3,64,128]{2,1,0:T(8,128)(2,1)S(1)} %pad_maximum_fusion.1), channel_id=1, source_target_pairs={{0,1},{1,2},{2,3},{3,0},{4,5},{5,6},{6,7},{7,4},{8,9},{9,10},{10,1... | collective-permute-start | bytes 147464 | tf_op jit(solution)/shard_map/ppermute | solution.py:440
  78.0 58.7 %copy-start.1 = (bf16[8,2,128,128]{3,2,1,0:T(8,128)(2,1)S(1)}, bf16[8,2,128,128]{3,2,1,0:T(8,128)(2,1)}, u32[]{:S(2)}) copy-start(bf16[8,2,128,128]{3,2,1,0:T(8,128)(2,1)} %copy-done) | copy-start | bytes 1572868
  78.0 58.7 %copy-start.3 = (bf16[16,64,512]{2,1,0:T(8,128)(2,1)S(1)}, bf16[16,64,512]{2,1,0:T(8,128)(2,1)}, u32[]{:S(2)}) copy-start(bf16[16,64,512]{2,1,0:T(8,128)(2,1)} %all_to_all.10) | copy-start | bytes 3145732
  78.1 7.5 %collective-permute-start.11 = (bf16[9,64,128]{2,1,0:T(8,128)(2,1)S(1)}, bf16[9,64,128]{2,1,0:T(8,128)(2,1)S(1)}, u32[]{:S(2)}, u32[]{:S(2)}) collective-permute-start(bf16[9,64,128]{2,1,0:T(8,128)(2,1)S(1)} %fusion.2.refs_0_), channel_id=1, source_target_pairs={{0,96},{16,112},{32,0},{48,16},{64,32},{80,48},{96,64},{112,80},{1... | collective-permute-start | bytes 442376 | tf_op jit(solution)/shard_map/ppermute | solution.py:473
  78.8 10.2 %collective-permute-start.10 = (bf16[9,64,128]{2,1,0:T(8,128)(2,1)S(1)}, bf16[9,64,128]{2,1,0:T(8,128)(2,1)S(1)}, u32[]{:S(2)}, u32[]{:S(2)}) collective-permute-start(bf16[9,64,128]{2,1,0:T(8,128)(2,1)S(1)} %fusion.2.refs_0_), channel_id=1, source_target_pairs={{0,64},{16,80},{32,96},{48,112},{64,0},{80,16},{96,32},{112,48},{1... | collective-permute-start | bytes 442376 | tf_op jit(solution)/shard_map/ppermute | solution.py:473
  84.3 6.9 %collective-permute-start.9 = (bf16[9,64,128]{2,1,0:T(8,128)(2,1)S(1)}, bf16[9,64,128]{2,1,0:T(8,128)(2,1)S(1)}, u32[]{:S(2)}, u32[]{:S(2)}) collective-permute-start(bf16[9,64,128]{2,1,0:T(8,128)(2,1)S(1)} %fusion.2.refs_0_), channel_id=1, source_target_pairs={{0,32},{16,48},{32,64},{48,80},{64,96},{80,112},{96,0},{112,16},{1... | collective-permute-start | bytes 442376 | tf_op jit(solution)/shard_map/ppermute | solution.py:473
  85.6 5.5 %collective-permute-start.12 = (bf16[9,64,128]{2,1,0:T(8,128)(2,1)S(1)}, bf16[9,64,128]{2,1,0:T(8,128)(2,1)S(1)}, u32[]{:S(2)}, u32[]{:S(2)}) collective-permute-start(bf16[9,64,128]{2,1,0:T(8,128)(2,1)S(1)} %fusion.2.refs_0_), channel_id=1, source_target_pairs={{0,16},{16,0},{32,48},{48,32},{64,80},{80,64},{96,112},{112,96},{1... | collective-permute-start | bytes 442376 | tf_op jit(solution)/shard_map/ppermute | solution.py:471
  85.6 5.5 %collective-permute-start.15 = (bf16[9,64,128]{2,1,0:T(8,128)(2,1)S(1)}, bf16[9,64,128]{2,1,0:T(8,128)(2,1)S(1)}, u32[]{:S(2)}, u32[]{:S(2)}) collective-permute-start(bf16[9,64,128]{2,1,0:T(8,128)(2,1)S(1)} %collective-permute-done.11.refs_3_), channel_id=1, source_target_pairs={{0,16},{16,0},{32,48},{48,32},{64,80},{80,64},{96,112},{112,96},{1... | collective-permute-start | bytes 442376 | tf_op jit(solution)/shard_map/ppermute | solution.py:476
  89.0 2.1 %collective-permute-start.14 = (bf16[9,64,128]{2,1,0:T(8,128)(2,1)S(1)}, bf16[9,64,128]{2,1,0:T(8,128)(2,1)S(1)}, u32[]{:S(2)}, u32[]{:S(2)}) collective-permute-start(bf16[9,64,128]{2,1,0:T(8,128)(2,1)S(1)} %collective-permute-done.10.refs_2_), channel_id=1, source_target_pairs={{0,16},{16,0},{32,48},{48,32},{64,80},{80,64},{96,112},{112,96},{1... | collective-permute-start | bytes 442376 | tf_op jit(solution)/shard_map/ppermute | solution.py:476
  91.1 1.4 collective-permute-start.13
  136.7 10.3 %copy-start.2 = (bf16[1024,512]{1,0:T(8,128)(2,1)S(1)}, bf16[1024,512]{1,0:T(8,128)(2,1)}, u32[]{:S(2)}) copy-start(bf16[1024,512]{1,0:T(8,128)(2,1)} %all-gather.8.cloned.1.call-done) | copy-start | bytes 3145732
  136.7 10.3 %copy-start.4 = (s32[8,16]{1,0:T(8,128)S(1)}, s32[8,16]{1,0:T(8,128)}, u32[]{:S(2)}) copy-start(s32[8,16]{1,0:T(8,128)} %map_ref.3) | copy-start | bytes 1540
Sparse Core Ops, SparseCore 0:
  23.5 27.3 all-gather.7
  54.9 28.8 all-gather.5
  86.0 61.0 all-gather.9

commit v5 on v4

--- a/solution.py
+++ b/solution.py
@@ -305,30 +305,48 @@
 
 def schur_kernel(
     map_ref, l_ref, given_ref, early_ref, panel_ref, w_ref, m_hbm, rows_hbm, front_ref,
-    out_ref, m_ref, rows_ref, lower_ref, low_ref, late_ref, sem
+    out_ref, m_ref, rows_ref, lower_ref, low_ref, late_ref, sem, late_sem, m_sem
 ):
     step = pl.program_id(0)
     leaf, front = place()
     owner = jnp.minimum(front, KS - 1)
 
-    def copies():
-        yield pltpu.make_async_copy(m_hbm, m_ref, sem.at[2, 0])
+    pair = STEP_ROWS // 2 * BLK
+
+    def row_copies(turn):
         for b in range(2):
             for a in range(KS):
-                columns = pl.ds(a * BLK, BLK)
-                source = rows_hbm.at[b, a]
+                here = pl.ds(pl.multiple_of(turn * pair, pair), pair)
                 yield pltpu.make_async_copy(
-                    source.at[pl.ds(0, ORDER)], rows_ref.at[b, :, columns], sem.at[b, a]
+                    rows_hbm.at[b, a, here],
+                    rows_ref.at[b, here, pl.ds(a * BLK, BLK)],
+                    sem.at[turn, b * KS + a],
                 )
+
+    def late_copies():
+        for b in range(2):
+            for a in range(KS):
                 yield pltpu.make_async_copy(
-                    source.at[pl.ds(ORDER, 2 * BLK)], lower_ref.at[b, a], sem.at[3 + b, a]
+                    rows_hbm.at[b, a, pl.ds(ORDER, 2 * BLK)], lower_ref.at[b, a], late_sem.at[b, a]
                 )
+
+    inverse = pltpu.make_async_copy(m_hbm, m_ref, m_sem)
 
     @pl.when(step == 0)
     def _():
-        for copy in copies():
+        for copy in [inverse, *row_copies(0), *late_copies()]:
             copy.start()
-        for copy in copies():
+        for turn in range(1, 16 // STEP_ROWS):
+            for copy in row_copies(turn):
+                copy.start()
+        inverse.wait()
+
+    for copy in row_copies(step):
+        copy.wait()
+
+    @pl.when(step == 0)
+    def _():
+        for copy in late_copies():
             copy.wait()
         for c in range(N_LEAF):
             product = jnp.zeros((BLK, BLK), F32)
@@ -338,7 +356,6 @@
                 product += dot(rows, panel_ref[c, :, n * BLK : (n + 1) * BLK], 1, 1)
             late_ref[c] = (given_ref[c, 0].astype(F32) - product).astype(BF16)
 
-    pair = STEP_ROWS // 2 * BLK
     source = pl.ds(pl.multiple_of(step * pair, pair), pair)
     for n in range(4):
         take = slice(n * 256, (n + 1) * 256)
@@ -406,7 +423,9 @@
             pltpu.VMEM((2, KS, 2 * BLK, BLK), BF16),
             pltpu.VMEM((STEP_ROWS * BLK, ORDER), F32),
             pltpu.VMEM((N_LEAF, BLK, BLK), BF16),
-            pltpu.SemaphoreType.DMA((5, KS)),
+            pltpu.SemaphoreType.DMA((16 // STEP_ROWS, 2 * KS)),
+            pltpu.SemaphoreType.DMA((2, KS)),
+            pltpu.SemaphoreType.DMA,
         ],
         compiler_params=pltpu.CompilerParams(vmem_limit_bytes=52 << 20),
     )(child_map, low, given, early, panels, w, m, rows, front)

time: 174 us -> 174 us (level)
  no operation moved by 1% of the time
where the time goes in v5:
time: 174 us; the launch traced here: 173 us
  Pallas kernels  72.6 us (42%)
  starting transfers between devices  31.7 us (18%)
  blocking collectives  28.1 us (16%)
  waiting for transfers between devices  23 us (13%)
  between operations  13.4 us (8%)
  other arithmetic  2.48 us (1%)
  local copies, waits for them, and re-layouts  2.07 us (1%)
    pallas_call x1, Pallas kernels, cholesky(): pl.pallas_call(cholesky_kernel, name='cholesky', out_shape=(jax.ShapeDtyp...  44.2 us
    all_to_all x1, blocking collectives, gather(): return lax.all_to_all(spread, axis, 0, 0)  28.1 us
    pallas_call x1, Pallas kernels, schur(): pl.pallas_call(schur_kernel, name='schur', grid=(steps,), out_shape=jax.S...  19.8 us
    ppermute x3, starting transfers between devices, front_pieces(): lax.ppermute(first, 'front', [(4 * i + j, (i + k) % 4 * 4 + j) for i in (...  8.06 us
    ppermute x3, starting transfers between devices, one_pass(): lax.ppermute(whole, 'leaf', [(i, (i + 2 * k) % N_LEAF) for i in range(N_L...  7.52 us
    ppermute x3, waiting for transfers between devices, front_pieces(): lax.ppermute(mine, 'front', [(4 * i + j, 4 * i + (j + k) % 4) for i in ra...  6.86 us
    pallas_call x1, Pallas kernels, columns(): pl.pallas_call(columns_kernel, name='columns', grid=(1,), out_shape=(jax....  5.52 us
    ppermute x3, waiting for transfers between devices, one_pass(): lax.ppermute(whole, 'leaf', [(i, (i + 2 * k) % N_LEAF) for i in range(N_L...  5.01 us
  transfers between devices with their start and end apart: 20, of which 8 were waited for; matrix products, arithmetic and copies ran while one was open for 2% of the time, Pallas kernels for 29%

profile of v5, /device:TPU:0, one launch (start us, length us, event | category | flops | bytes accessed | tf_op | source)
XLA Modules:
  0.0 173.3 jit_solution(7684485349497571802)
XLA Ops:
  6.5 1.9 %copy.11 = bf16[2,8,128,128]{3,2,0,1:T(8,128)(2,1)} copy(bf16[2,8,128,128]{3,2,1,0:T(8,128)(2,1)} %bitcast.27) | data formatting | bytes 1048576 | tf_op jit(solution)/shard_map/reshape;squeeze | solution.py:478
  8.4 4.6 %all-to-all-start = ((bf16[8,2,128,128]{3,2,1,0:T(8,128)(2,1)}), bf16[8,2,128,128]{3,2,1,0:T(8,128)(2,1)S(1)}, u32[]{:S(2)}, u32[]{:S(2)}) async-start(bf16[8,2,128,128]{3,2,1,0:T(8,128)(2,1)} %bitcast.18), calls=%async_computation | async-start | bytes 1048576 | tf_op jit(solution)/shard_map/all_to_all | solution.py:479
  13.0 0.0 all-gather.8.cloned.1.call-start
  13.1 0.9 select_bitcast_fusion
  13.9 4.0 %collective-permute-start.1 = (bf16[64,512]{1,0:T(8,128)(2,1)S(1)}, bf16[64,512]{1,0:T(8,128)(2,1)S(1)}, u32[]{:S(2)}, u32[]{:S(2)}) collective-permute-start(bf16[64,512]{1,0:T(8,128)(2,1)S(1)} %get-tuple-element.35), channel_id=1, source_target_pairs={{0,8},{1,24},{2,40},{3,56},{4,72},{5,88},{6,104},{7,120},{8,0},{9,... | collective-permute-start | bytes 196616 | tf_op jit(solution)/shard_map/ppermute | solution.py:477
  17.9 0.7 collective-permute-start
  18.6 1.6 collective-permute-done.1
  20.1 0.0 collective-permute-done
  20.1 3.2 %all-to-all-done.given_ref = bf16[8,2,128,128]{3,2,1,0:T(8,128)(2,1)S(1)} async-done(((bf16[8,2,128,128]{3,2,1,0:T(8,128)(2,1)}), bf16[8,2,128,128]{3,2,1,0:T(8,128)(2,1)S(1)}, u32[]{:S(2)}, u32[]{:S(2)}) %all-to-all-start) | async-done | bytes 524320 | tf_op jit(solution)/shard_map/all_to_all | solution.py:479
  23.3 0.0 copy-start
  23.3 0.0 all-gather.8.cloned.1.call-update
  23.3 0.0 all-gather.6.cloned.1.call-start
  23.4 0.1 broadcast_in_dim.2
  23.5 28.1 %all_to_all.10 = bf16[16,64,512]{2,1,0:T(8,128)(2,1)} all-to-all(bf16[16,64,512]{2,1,0:T(8,128)(2,1)S(1)} %broadcast_in_dim.2), channel_id=1, replica_groups=mesh['leaf'=8,'front'=16] {'front'}, dimensions={0} | all-to-all | bytes 2097152 | tf_op jit(solution)/shard_map/all_to_all | solution.py:436
  51.7 0.0 all-gather.8.cloned.1.call-done
  51.7 0.0 copy-done
  51.7 3.1 %pivot_rows.1 = (bf16[128,1024]{1,0:T(8,128)(2,1)}, bf16[8,128,128]{2,1,0:T(8,128)(2,1)}, bf16[2,64,128]{2,1,0:T(8,128)(2,1)}) custom-call(s32[8,16]{1,0:T(8,128)} %map_ref.3, f32[16384,128]{1,0:T(8,128)} %bitcast.24, bf16[8,2,128,128]{3,2,1,0:T(8,128)(2,1)} %copy-done, bf16[2,8,64,512]{3,2,1,0:T(8,128)(2,1)} %bitcast.22, bf16[8,128,512]{2,1,0:T(8,128)(2,1)} %bitcast.19), custom_call_target="tpu_custom_call" | custom-call | tf_op jit(solution)/shard_map/pivot_rows/pallas_call | solution.py:67
  54.8 0.0 all-gather.6.cloned.1.call-update
  54.8 0.0 all-gather.10.cloned.1.call-start
  54.9 4.0 %collective-permute-start.5 = (bf16[2,64,128]{2,1,0:T(8,128)(2,1)}, bf16[2,64,128]{2,1,0:T(8,128)(2,1)S(1)}, u32[]{:S(2)}, u32[]{:S(2)}) collective-permute-start(bf16[2,64,128]{2,1,0:T(8,128)(2,1)} %get-tuple-element.23), channel_id=1, source_target_pairs={{0,12},{1,13},{2,14},{3,15},{4,0},{5,1},{6,2},{7,3},{16,28},{17,29... | collective-permute-start | bytes 98312 | tf_op jit(solution)/shard_map/ppermute | solution.py:451
  58.9 1.3 collective-permute-start.4
  60.2 2.8 %collective-permute-start.3 = (bf16[2,64,128]{2,1,0:T(8,128)(2,1)}, bf16[2,64,128]{2,1,0:T(8,128)(2,1)S(1)}, u32[]{:S(2)}, u32[]{:S(2)}) collective-permute-start(bf16[2,64,128]{2,1,0:T(8,128)(2,1)} %get-tuple-element.23), channel_id=1, source_target_pairs={{0,4},{1,5},{2,6},{3,7},{4,8},{5,9},{6,10},{7,11},{16,20},{17,21},... | collective-permute-start | bytes 98312 | tf_op jit(solution)/shard_map/ppermute | solution.py:451
  63.0 1.6 collective-permute-start.2
  64.7 0.0 collective-permute-done.5
  64.7 0.0 collective-permute-done.4
  64.7 0.2 collective-permute-done.3
  64.8 0.8 select_select_fusion
  65.7 2.9 %collective-permute-start.8 = (bf16[3,64,128]{2,1,0:T(8,128)(2,1)S(1)}, bf16[3,64,128]{2,1,0:T(8,128)(2,1)S(1)}, u32[]{:S(2)}, u32[]{:S(2)}) collective-permute-start(bf16[3,64,128]{2,1,0:T(8,128)(2,1)S(1)} %pad_maximum_fusion.1), channel_id=1, source_target_pairs={{0,3},{1,0},{2,1},{3,2},{4,7},{5,4},{6,5},{7,6},{8,11},{9,8},{10,9... | collective-permute-start | bytes 147464 | tf_op jit(solution)/shard_map/ppermute | solution.py:459
  68.6 0.8 collective-permute-start.7
  69.4 0.9 collective-permute-start.6
  70.3 6.8 %collective-permute-done.6 = bf16[3,64,128]{2,1,0:T(8,128)(2,1)S(1)} collective-permute-done((bf16[3,64,128]{2,1,0:T(8,128)(2,1)S(1)}, bf16[3,64,128]{2,1,0:T(8,128)(2,1)S(1)}, u32[]{:S(2)}, u32[]{:S(2)}) %collective-permute-start.6) | collective-permute-done | bytes 49184 | tf_op jit(solution)/shard_map/ppermute | solution.py:459
  77.2 0.0 collective-permute-done.7
  77.2 0.0 collective-permute-done.8
  77.2 0.0 collective-permute-done.2
  77.2 0.8 pad_maximum_fusion
  78.0 0.0 all-gather.10.cloned.1.call-update
  78.0 0.0 copy-start.1
  78.0 0.0 copy-start.3
  78.1 0.8 collective-permute-start.11
  78.8 5.4 %collective-permute-start.10 = (bf16[9,64,128]{2,1,0:T(8,128)(2,1)S(1)}, bf16[9,64,128]{2,1,0:T(8,128)(2,1)S(1)}, u32[]{:S(2)}, u32[]{:S(2)}) collective-permute-start(bf16[9,64,128]{2,1,0:T(8,128)(2,1)S(1)} %fusion.2.refs_0_), channel_id=1, source_target_pairs={{0,64},{16,80},{32,96},{48,112},{64,0},{80,16},{96,32},{112,48},{1... | collective-permute-start | bytes 442376 | tf_op jit(solution)/shard_map/ppermute | solution.py:492
  84.3 1.3 collective-permute-start.9
  85.6 0.0 collective-permute-start.12
  85.6 0.0 collective-permute-done.11.refs_3_
  85.6 0.5 collective-permute-start.15
  86.1 2.9 %collective-permute-done.10.refs_2_ = bf16[9,64,128]{2,1,0:T(8,128)(2,1)S(1)} collective-permute-done((bf16[9,64,128]{2,1,0:T(8,128)(2,1)S(1)}, bf16[9,64,128]{2,1,0:T(8,128)(2,1)S(1)}, u32[]{:S(2)}, u32[]{:S(2)}) %collective-permute-start.10) | collective-permute-done | bytes 147488 | tf_op jit(solution)/shard_map/ppermute | solution.py:492
  89.0 0.0 collective-permute-start.14
  89.0 2.1 %collective-permute-done.9.refs_1_ = bf16[9,64,128]{2,1,0:T(8,128)(2,1)S(1)} collective-permute-done((bf16[9,64,128]{2,1,0:T(8,128)(2,1)S(1)}, bf16[9,64,128]{2,1,0:T(8,128)(2,1)S(1)}, u32[]{:S(2)}, u32[]{:S(2)}) %collective-permute-start.9) | collective-permute-done | bytes 147488 | tf_op jit(solution)/shard_map/ppermute | solution.py:492
  91.1 0.0 collective-permute-start.13
  91.1 0.0 collective-permute-done.12.refs_4_
  91.1 0.0 collective-permute-done.15.refs_7_
  91.1 0.0 collective-permute-done.14.refs_6_
  91.1 1.3 collective-permute-done.13.refs_5_
  92.5 44.2 %cholesky.1 = (bf16[1024,1024]{1,0:T(8,128)(2,1)}, f32[128,128]{1,0:T(8,128)S(1)}) custom-call(bf16[9,64,128]{2,1,0:T(8,128)(2,1)S(1)} %fusion.2.refs_0_, bf16[9,64,128]{2,1,0:T(8,128)(2,1)S(1)} %collective-permute-done.9.refs_1_, bf16[9,64,128]{2,1,0:T(8,128)(2,1)S(1)} %collective-permute-done.10.refs_2_, ...), custom_call_target="tpu_custom_call" | custom-call | flops 60000002048 | bytes 6291456 | tf_op jit(solution)/shard_map/cholesky/pallas_call | solution.py:246
  136.7 0.0 all-gather.6.cloned.1.call-done.cols_ref
  136.7 0.0 copy-done.1
  136.7 0.0 copy-done.3
  136.7 0.0 copy-start.2
  136.7 0.0 copy-start.4
  136.7 5.5 %columns.1 = (bf16[1024,1024]{1,0:T(8,128)(2,1)}, bf16[8,128,128]{2,1,0:T(8,128)(2,1)S(1)}) custom-call(bf16[1024,1024]{1,0:T(8,128)(2,1)} %get-tuple-element.26.m_ref.m_hbm, bf16[1024,1024]{1,0:T(8,128)(2,1)} %all-gather.6.cloned.1.call-done.cols_ref, bf16[8,2,128,128]{3,2,1,0:T(8,128)(2,1)S(1)} %copy-done.1, bf16[2,8,64,512]{3,2,1,0:T(8,128)(2,1)S(1)} %bitcast.23, ...), custom_call_target="tpu_custom_call" | custom-call | flops 4000000000 | bytes 8388608 | tf_op jit(solution)/shard_map/columns/pallas_call | solution.py:283
  142.3 4.8 %all-gather.10.cloned.1.call-done = bf16[20480,128]{1,0:T(8,128)(2,1)} async-done(((bf16[1280,128]{1,0:T(8,128)(2,1)}), bf16[20480,128]{1,0:T(8,128)(2,1)}) %all-gather.10.cloned.1.call-update) | async-done | bytes 5242896 | tf_op jit(solution)/shard_map/all_gather | solution.py:498
  147.0 0.0 copy-done.2
  147.0 0.0 copy-done.4
  147.0 19.8 %schur.1 = f32[16384,128]{1,0:T(8,128)} custom-call(s32[8,16]{1,0:T(8,128)S(1)} %copy-done.4, f32[128,128]{1,0:T(8,128)S(1)} %get-tuple-element.25.l_ref, bf16[8,2,128,128]{3,2,1,0:T(8,128)(2,1)S(1)} %copy-done.1, bf16[8,128,128]{2,1,0:T(8,128)(2,1)S(1)} %get-tuple-element.28.early_ref, bf16[8,128,512]{2,1,0:T(8,128)(2,1)S(1)} %bitcast.21, ...), custom_call_target="tpu_custom_call" | custom-call | tf_op jit(solution)/shard_map/schur/pallas_call | solution.py:403
  (10 shorter events, 0.1 us)
Async XLA Ops:
  8.4 14.9 %all-to-all-start = ((bf16[8,2,128,128]{3,2,1,0:T(8,128)(2,1)}), bf16[8,2,128,128]{3,2,1,0:T(8,128)(2,1)S(1)}, u32[]{:S(2)}, u32[]{:S(2)}) async-start(bf16[8,2,128,128]{3,2,1,0:T(8,128)(2,1)} %bitcast.18), calls=%async_computation | async-start | bytes 1048576 | tf_op jit(solution)/shard_map/all_to_all | solution.py:479
  13.0 38.7 %all-gather.8.cloned.1.call-start = ((), (), s32[]{:S(2)}) async-start(), calls=%async_computation.3 | async-start | bytes 1179648 | tf_op jit(solution)/shard_map/all_gather | solution.py:481
  13.9 6.2 %collective-permute-start.1 = (bf16[64,512]{1,0:T(8,128)(2,1)S(1)}, bf16[64,512]{1,0:T(8,128)(2,1)S(1)}, u32[]{:S(2)}, u32[]{:S(2)}) collective-permute-start(bf16[64,512]{1,0:T(8,128)(2,1)S(1)} %get-tuple-element.35), channel_id=1, source_target_pairs={{0,8},{1,24},{2,40},{3,56},{4,72},{5,88},{6,104},{7,120},{8,0},{9,... | collective-permute-start | bytes 196616 | tf_op jit(solution)/shard_map/ppermute | solution.py:477
  17.9 2.2 %collective-permute-start = (bf16[64,512]{1,0:T(8,128)(2,1)S(1)}, bf16[64,512]{1,0:T(8,128)(2,1)S(1)}, u32[]{:S(2)}, u32[]{:S(2)}) collective-permute-start(bf16[64,512]{1,0:T(8,128)(2,1)S(1)} %get-tuple-element.36), channel_id=1, source_target_pairs={{0,0},{1,16},{2,32},{3,48},{4,64},{5,80},{6,96},{7,112},{8,8},{9,2... | collective-permute-start | bytes 196616 | tf_op jit(solution)/shard_map/ppermute | solution.py:476
  23.3 28.4 %copy-start = (bf16[8,2,128,128]{3,2,1,0:T(8,128)(2,1)}, bf16[8,2,128,128]{3,2,1,0:T(8,128)(2,1)S(1)}, u32[]{:S(2)}) copy-start(bf16[8,2,128,128]{3,2,1,0:T(8,128)(2,1)S(1)} %all-to-all-done.given_ref) | copy-start | bytes 1572868
  23.3 113.3 %all-gather.6.cloned.1.call-start = ((), (), s32[]{:S(2)}) async-start(), calls=%async_computation.2 | async-start | bytes 2359296 | tf_op jit(solution)/shard_map/all_gather | solution.py:486
  54.8 92.2 %all-gather.10.cloned.1.call-start = ((), (), s32[]{:S(2)}) async-start(), calls=%async_computation.4 | async-start | bytes 5570560 | tf_op jit(solution)/shard_map/all_gather | solution.py:498
  54.9 9.8 %collective-permute-start.5 = (bf16[2,64,128]{2,1,0:T(8,128)(2,1)}, bf16[2,64,128]{2,1,0:T(8,128)(2,1)S(1)}, u32[]{:S(2)}, u32[]{:S(2)}) collective-permute-start(bf16[2,64,128]{2,1,0:T(8,128)(2,1)} %get-tuple-element.23), channel_id=1, source_target_pairs={{0,12},{1,13},{2,14},{3,15},{4,0},{5,1},{6,2},{7,3},{16,28},{17,29... | collective-permute-start | bytes 98312 | tf_op jit(solution)/shard_map/ppermute | solution.py:451
  58.9 5.8 %collective-permute-start.4 = (bf16[2,64,128]{2,1,0:T(8,128)(2,1)}, bf16[2,64,128]{2,1,0:T(8,128)(2,1)S(1)}, u32[]{:S(2)}, u32[]{:S(2)}) collective-permute-start(bf16[2,64,128]{2,1,0:T(8,128)(2,1)} %get-tuple-element.23), channel_id=1, source_target_pairs={{0,8},{1,9},{2,10},{3,11},{4,12},{5,13},{6,14},{7,15},{16,24},{17,... | collective-permute-start | bytes 98312 | tf_op jit(solution)/shard_map/ppermute | solution.py:451
  60.2 4.7 %collective-permute-start.3 = (bf16[2,64,128]{2,1,0:T(8,128)(2,1)}, bf16[2,64,128]{2,1,0:T(8,128)(2,1)S(1)}, u32[]{:S(2)}, u32[]{:S(2)}) collective-permute-start(bf16[2,64,128]{2,1,0:T(8,128)(2,1)} %get-tuple-element.23), channel_id=1, source_target_pairs={{0,4},{1,5},{2,6},{3,7},{4,8},{5,9},{6,10},{7,11},{16,20},{17,21},... | collective-permute-start | bytes 98312 | tf_op jit(solution)/shard_map/ppermute | solution.py:451
  63.0 14.2 %collective-permute-start.2 = (bf16[8,128,128]{2,1,0:T(8,128)(2,1)}, bf16[8,128,128]{2,1,0:T(8,128)(2,1)S(1)}, u32[]{:S(2)}, u32[]{:S(2)}) collective-permute-start(bf16[8,128,128]{2,1,0:T(8,128)(2,1)} %get-tuple-element.22), channel_id=1, source_target_pairs={{0,0},{1,16},{2,32},{3,48},{4,64},{5,80},{6,96},{7,112},{8,8},{9,2... | collective-permute-start | bytes 786440 | tf_op jit(solution)/shard_map/ppermute | solution.py:487
  65.7 11.5 %collective-permute-start.8 = (bf16[3,64,128]{2,1,0:T(8,128)(2,1)S(1)}, bf16[3,64,128]{2,1,0:T(8,128)(2,1)S(1)}, u32[]{:S(2)}, u32[]{:S(2)}) collective-permute-start(bf16[3,64,128]{2,1,0:T(8,128)(2,1)S(1)} %pad_maximum_fusion.1), channel_id=1, source_target_pairs={{0,3},{1,0},{2,1},{3,2},{4,7},{5,4},{6,5},{7,6},{8,11},{9,8},{10,9... | collective-permute-start | bytes 147464 | tf_op jit(solution)/shard_map/ppermute | solution.py:459
  68.6 8.6 %collective-permute-start.7 = (bf16[3,64,128]{2,1,0:T(8,128)(2,1)S(1)}, bf16[3,64,128]{2,1,0:T(8,128)(2,1)S(1)}, u32[]{:S(2)}, u32[]{:S(2)}) collective-permute-start(bf16[3,64,128]{2,1,0:T(8,128)(2,1)S(1)} %pad_maximum_fusion.1), channel_id=1, source_target_pairs={{0,2},{1,3},{2,0},{3,1},{4,6},{5,7},{6,4},{7,5},{8,10},{9,11},{10,... | collective-permute-start | bytes 147464 | tf_op jit(solution)/shard_map/ppermute | solution.py:459
  69.4 7.7 %collective-permute-start.6 = (bf16[3,64,128]{2,1,0:T(8,128)(2,1)S(1)}, bf16[3,64,128]{2,1,0:T(8,128)(2,1)S(1)}, u32[]{:S(2)}, u32[]{:S(2)}) collective-permute-start(bf16[3,64,128]{2,1,0:T(8,128)(2,1)S(1)} %pad_maximum_fusion.1), channel_id=1, source_target_pairs={{0,1},{1,2},{2,3},{3,0},{4,5},{5,6},{6,7},{7,4},{8,9},{9,10},{10,1... | collective-permute-start | bytes 147464 | tf_op jit(solution)/shard_map/ppermute | solution.py:459
  78.0 58.7 %copy-start.1 = (bf16[8,2,128,128]{3,2,1,0:T(8,128)(2,1)S(1)}, bf16[8,2,128,128]{3,2,1,0:T(8,128)(2,1)}, u32[]{:S(2)}) copy-start(bf16[8,2,128,128]{3,2,1,0:T(8,128)(2,1)} %copy-done) | copy-start | bytes 1572868
  78.0 58.7 %copy-start.3 = (bf16[16,64,512]{2,1,0:T(8,128)(2,1)S(1)}, bf16[16,64,512]{2,1,0:T(8,128)(2,1)}, u32[]{:S(2)}) copy-start(bf16[16,64,512]{2,1,0:T(8,128)(2,1)} %all_to_all.10) | copy-start | bytes 3145732
  78.1 7.5 %collective-permute-start.11 = (bf16[9,64,128]{2,1,0:T(8,128)(2,1)S(1)}, bf16[9,64,128]{2,1,0:T(8,128)(2,1)S(1)}, u32[]{:S(2)}, u32[]{:S(2)}) collective-permute-start(bf16[9,64,128]{2,1,0:T(8,128)(2,1)S(1)} %fusion.2.refs_0_), channel_id=1, source_target_pairs={{0,96},{16,112},{32,0},{48,16},{64,32},{80,48},{96,64},{112,80},{1... | collective-permute-start | bytes 442376 | tf_op jit(solution)/shard_map/ppermute | solution.py:492
  78.8 10.2 %collective-permute-start.10 = (bf16[9,64,128]{2,1,0:T(8,128)(2,1)S(1)}, bf16[9,64,128]{2,1,0:T(8,128)(2,1)S(1)}, u32[]{:S(2)}, u32[]{:S(2)}) collective-permute-start(bf16[9,64,128]{2,1,0:T(8,128)(2,1)S(1)} %fusion.2.refs_0_), channel_id=1, source_target_pairs={{0,64},{16,80},{32,96},{48,112},{64,0},{80,16},{96,32},{112,48},{1... | collective-permute-start | bytes 442376 | tf_op jit(solution)/shard_map/ppermute | solution.py:492
  84.3 6.9 %collective-permute-start.9 = (bf16[9,64,128]{2,1,0:T(8,128)(2,1)S(1)}, bf16[9,64,128]{2,1,0:T(8,128)(2,1)S(1)}, u32[]{:S(2)}, u32[]{:S(2)}) collective-permute-start(bf16[9,64,128]{2,1,0:T(8,128)(2,1)S(1)} %fusion.2.refs_0_), channel_id=1, source_target_pairs={{0,32},{16,48},{32,64},{48,80},{64,96},{80,112},{96,0},{112,16},{1... | collective-permute-start | bytes 442376 | tf_op jit(solution)/shard_map/ppermute | solution.py:492
  85.6 5.5 %collective-permute-start.12 = (bf16[9,64,128]{2,1,0:T(8,128)(2,1)S(1)}, bf16[9,64,128]{2,1,0:T(8,128)(2,1)S(1)}, u32[]{:S(2)}, u32[]{:S(2)}) collective-permute-start(bf16[9,64,128]{2,1,0:T(8,128)(2,1)S(1)} %fusion.2.refs_0_), channel_id=1, source_target_pairs={{0,16},{16,0},{32,48},{48,32},{64,80},{80,64},{96,112},{112,96},{1... | collective-permute-start | bytes 442376 | tf_op jit(solution)/shard_map/ppermute | solution.py:490
  85.6 5.5 %collective-permute-start.15 = (bf16[9,64,128]{2,1,0:T(8,128)(2,1)S(1)}, bf16[9,64,128]{2,1,0:T(8,128)(2,1)S(1)}, u32[]{:S(2)}, u32[]{:S(2)}) collective-permute-start(bf16[9,64,128]{2,1,0:T(8,128)(2,1)S(1)} %collective-permute-done.11.refs_3_), channel_id=1, source_target_pairs={{0,16},{16,0},{32,48},{48,32},{64,80},{80,64},{96,112},{112,96},{1... | collective-permute-start | bytes 442376 | tf_op jit(solution)/shard_map/ppermute | solution.py:495
  89.0 2.1 %collective-permute-start.14 = (bf16[9,64,128]{2,1,0:T(8,128)(2,1)S(1)}, bf16[9,64,128]{2,1,0:T(8,128)(2,1)S(1)}, u32[]{:S(2)}, u32[]{:S(2)}) collective-permute-start(bf16[9,64,128]{2,1,0:T(8,128)(2,1)S(1)} %collective-permute-done.10.refs_2_), channel_id=1, source_target_pairs={{0,16},{16,0},{32,48},{48,32},{64,80},{80,64},{96,112},{112,96},{1... | collective-permute-start | bytes 442376 | tf_op jit(solution)/shard_map/ppermute | solution.py:495
  91.1 1.4 collective-permute-start.13
  136.7 10.3 %copy-start.2 = (bf16[1024,512]{1,0:T(8,128)(2,1)S(1)}, bf16[1024,512]{1,0:T(8,128)(2,1)}, u32[]{:S(2)}) copy-start(bf16[1024,512]{1,0:T(8,128)(2,1)} %all-gather.8.cloned.1.call-done) | copy-start | bytes 3145732
  136.7 10.3 %copy-start.4 = (s32[8,16]{1,0:T(8,128)S(1)}, s32[8,16]{1,0:T(8,128)}, u32[]{:S(2)}) copy-start(s32[8,16]{1,0:T(8,128)} %map_ref.3) | copy-start | bytes 1540
Sparse Core Ops, SparseCore 0:
  23.5 27.3 all-gather.7
  54.9 28.8 all-gather.5
  86.0 61.0 all-gather.9
